TPU v7x, 128 devices: a whole 4x4x4 slice. The times are simulated.
128 devices in a mesh: line: 8 (over y, core), tile: 16 (over x, z).
Axes of the slice: x: 4, y: 4, z: 4, core: 2. Of those that a mesh axis runs over, the one named last changes fastest.
Arguments:
- traces: bfloat16 [16, 4096, 128], P('tile', 'line'), may hold values from -6 to 6
- codes: int32 [16, 64], P('tile'), may hold values from 0 to 255
- routes: int32 [8, 256], P('line', 'tile'), may hold values from 0 to 15, as said below
- beam_matrix: bfloat16 [8, 16, 2, 4096, 1024], P('line', 'tile'), may hold values from -0.046875 to 0.046875
- dip_filter: float32 [5, 5], replicated, may hold values from -1 to 1
Outputs:
- migrated: float32 [2, 64, 128, 128], P(None, 'line', 'tile')
Inputs may be any that keep to these rules, and one draw needn't show every extreme that they name: `routes`: entry [l, f * 16 + b] is the depth tile that block b of frequency f on line l goes to. Among the 16 entries of one device no tile appears more than 4 times, and in every line some device names one tile exactly 4 times. Among the entries of one line no tile appears more than 32 times, and in every line one tile appears exactly 32 times.
All inputs are finite; a program needn't handle non-finite values.
Results may differ from a plain program's by a relative error of at most 0.004.
Values may be sent and summed in bfloat16 or wider, within the bound.
No kernel may reach another device: no remote copies, remote signals or barrier semaphores. Data moves between devices by JAX's collectives and lax.ppermute only.
A program may use at most 64 MiB of HBM per device.

v0:
```python
import jax
import jax.numpy as jnp
from jax import lax
from jax.sharding import PartitionSpec as P

S = 64
P_SIZE = 256
WIN = 128
BR = 128
TZ = 8
TX = 128
MAXB = 32
SEND_MOST = 4


def passed_along(value, axis, steps):
    count = lax.axis_size(axis)
    first, last = (max(0, -steps), min(count, count - steps))
    return lax.ppermute(value, axis, [(source, source + steps) for source in range(first, last)])


def cut_along(array, dim, devices):
    lengths = array.shape
    pieces = array.reshape(*lengths[:dim], devices, lengths[dim] // devices, *lengths[dim + 1 :])
    return jnp.moveaxis(pieces, dim, 0)


def sent_and_summed(array, axis, dim):
    devices = lax.axis_size(axis)
    pieces = lax.all_to_all(cut_along(array, dim, devices), axis, 0, 0, tiled=True)
    return jnp.sum(pieces, axis=0)


def with_halo(cells, sides, width):
    for axis, dim in sides:
        count = lax.axis_size(axis)
        ends = count - 1
        head = lax.slice_in_dim(cells, 0, width, axis=dim)
        tail = lax.slice_in_dim(cells, cells.shape[dim] - width, cells.shape[dim], axis=dim)
        cells = jnp.concatenate(
            [
                lax.ppermute(tail, axis, [(i, (i + 1) % count) for i in range(ends)]),
                cells,
                lax.ppermute(head, axis, [((i + 1) % count, i) for i in range(ends)]),
            ],
            axis=dim,
        )
    return cells


def slant_table(frequency, freq_count):
    slopes = jnp.arange(P_SIZE, dtype=jnp.float32) - P_SIZE / 2
    offsets = jnp.arange(WIN, dtype=jnp.float32) - (WIN - 1) / 2
    factor = 2.0 + frequency.astype(jnp.float32) / freq_count
    phase_angle = jnp.pi * factor * slopes[:, None] * offsets[None, :] / WIN
    taper_row = jnp.exp(-0.5 * (offsets / (0.4 * WIN)) ** 2)
    taper_row = taper_row / jnp.sqrt(jnp.sum(taper_row * taper_row))
    return jnp.concatenate(
        [taper_row * jnp.cos(phase_angle), -taper_row * jnp.sin(phase_angle)], 0
    ).astype(jnp.bfloat16)


def rotate(stacked, code_row):
    real_part = stacked[..., :P_SIZE, :S] - stacked[..., P_SIZE:, S:]
    imag_part = stacked[..., :P_SIZE, S:] + stacked[..., P_SIZE:, :S]
    code_angle = 2.0 * jnp.pi * code_row.astype(jnp.float32) / 256.0
    cosine = jnp.cos(code_angle)
    sine_part = jnp.sin(code_angle)
    return jnp.concatenate(
        [real_part * cosine + imag_part * sine_part, imag_part * cosine - real_part * sine_part], -1
    ).astype(jnp.bfloat16)


def dip_apply(padded, dip_filter):
    depth_rows = padded.shape[2] - 4
    widened = jnp.pad(padded, ((0, 0), (0, 0), (0, 0), (2, 2)))
    result = jnp.zeros(padded.shape[:2] + (depth_rows, TX), jnp.float32)
    for down_step in range(5):
        for side_step in range(5):
            result = (
                result
                + dip_filter[down_step, side_step]
                * widened[:, :, down_step : down_step + depth_rows, side_step : side_step + TX]
            )
    return result


def per_device(traces, codes, routes, beam_matrix, dip_filter):
    tile_count = lax.axis_size("tile")
    my_tile = lax.axis_index("tile")
    half_win = WIN // 2
    row_width = BR * 2 * S
    local_traces = traces[0]
    next_rim = passed_along(local_traces[:half_win], "line", -1)
    extended = jnp.concatenate([local_traces, next_rim], 0)
    halves = extended.reshape(-1, half_win, 2 * S)
    windows = jnp.concatenate([halves[:-1], halves[1:]], 1)
    table_now = slant_table(my_tile, tile_count)
    stacked = jnp.einsum("pj,wjc->wpc", table_now, windows, preferred_element_type=jnp.float32)
    beam_rows = rotate(stacked, codes[0])
    blocks = beam_rows.reshape(-1, row_width)
    route_row = routes[0]
    peer_ids = jnp.arange(tile_count)
    member = (route_row[:, None] == peer_ids[None, :]).astype(jnp.int32)
    before = jnp.cumsum(member, 0) - member
    rank_in = jnp.sum(before * member, 1)
    send_slot = route_row * SEND_MOST + rank_in
    picker = (jnp.arange(tile_count * SEND_MOST)[:, None] == send_slot[None, :]).astype(
        jnp.bfloat16
    )
    outgoing = jnp.dot(picker, blocks, preferred_element_type=jnp.float32).astype(jnp.bfloat16)
    outgoing = outgoing.reshape(tile_count, SEND_MOST, row_width)
    sent_counts = jnp.sum(member, 0)[:, None]
    incoming, got_counts = (
        lax.all_to_all(outgoing, "tile", split_axis=0, concat_axis=0, tiled=True),
        lax.all_to_all(sent_counts, "tile", split_axis=0, concat_axis=0, tiled=True),
    )
    arrived = got_counts[:, 0]
    first_slot = jnp.cumsum(arrived) - arrived
    rank_list = jnp.arange(SEND_MOST)
    slot_ids = jnp.where(
        rank_list[None, :] < arrived[:, None], first_slot[:, None] + rank_list[None, :], MAXB
    ).reshape(-1)
    placer = (jnp.arange(MAXB)[:, None] == slot_ids[None, :]).astype(jnp.bfloat16)
    compact = jnp.dot(
        placer, incoming.reshape(-1, row_width), preferred_element_type=jnp.float32
    ).astype(jnp.bfloat16)
    matrices = beam_matrix[0, 0]
    slot_rows = compact.reshape(MAXB * BR, 2 * S)
    contract_dims = (((0,), (0,)), ((), ()))
    with_real = lax.dot_general(
        slot_rows, matrices[0], contract_dims, preferred_element_type=jnp.float32
    )
    with_imag = lax.dot_general(
        slot_rows, matrices[1], contract_dims, preferred_element_type=jnp.float32
    )
    image_re = with_real[:S] - with_imag[S:]
    image_im = with_real[S:] + with_imag[:S]
    partial_image = jnp.stack([image_re, image_im]).reshape(2, S, TZ, TX)
    summed = sent_and_summed(partial_image, "line", 1)
    rimmed = with_halo(summed, (("tile", 2),), 2)
    return dip_apply(rimmed, dip_filter)


def solution(mesh):
    in_specs = (
        P("tile", "line", None),
        P("tile", None),
        P("line", "tile"),
        P("line", "tile", None, None, None),
        P(),
    )
    out_specs = P(None, "line", "tile", None)
    return jax.shard_map(
        per_device, mesh=mesh, in_specs=in_specs, out_specs=out_specs, check_vma=False
    )
```

profile of v0, /device:TPU:96, one launch (start us, length us, event | category | flops | bytes accessed | tf_op | source)
XLA Modules:
  0.0 114.0 jit_solution(7334439527235484742)
XLA Ops:
  0.0 0.7 slice_bitcast_fusion
  0.7 1.3 %collective-permute-start = (bf16[64,128]{1,0:T(8,128)(2,1)S(1)}, bf16[64,128]{1,0:T(8,128)(2,1)S(1)}, u32[]{:S(2)}, u32[]{:S(2)}) collective-permute-start(bf16[64,128]{1,0:T(8,128)(2,1)S(1)} %slice_bitcast_fusion), channel_id=1, source_target_pairs={{16,0},{32,16},{48,32},{64,48},{80,64},{96,80},{112,96},{17,1},{33... | collective-permute-start | bytes 49160 | tf_op jit(solution)/shard_map/ppermute | solution.py:19
  2.0 0.7 fusion.46
  2.8 0.8 fusion.47
  4.3 7.0 %all-to-all-start = ((s32[16,1,1]{2,1,0:T(1,128)}), s32[16,1,1]{2,1,0:T(1,128)S(1)}, u32[]{:S(2)}, u32[]{:S(2)}) async-start(s32[16,1,1]{2,1,0:T(1,128)} %copy.20), calls=%async_computation | async-start | bytes 16384 | tf_op jit(solution)/shard_map/all_to_all | solution.py:116
  11.3 0.7 multiply_reduce_fusion
  12.8 0.7 cosine_bitcast_fusion
  14.7 1.1 copy.22
  15.8 0.9 pad_maximum_fusion.1
  18.9 2.2 %reshape.128 = bf16[16,4,16384]{2,1,0:T(4,128)(2,1)} reshape(bf16[64,16384]{1,0:T(8,128)(2,1)S(1)} %convolution_convert_fusion) | data formatting | bytes 4194304 | tf_op jit(solution)/shard_map/reshape | solution.py:112
  21.1 7.2 %all-to-all-start.1 = ((bf16[16,4,16384]{2,1,0:T(4,128)(2,1)}), bf16[16,4,16384]{2,1,0:T(4,128)(2,1)S(1)}, u32[]{:S(2)}, u32[]{:S(2)}) async-start(bf16[16,4,16384]{2,1,0:T(4,128)(2,1)} %reshape.128), calls=%async_computation.1 | async-start | bytes 4194304 | tf_op jit(solution)/shard_map/all_to_all | solution.py:115
  29.0 28.8 %all-to-all-done.1 = bf16[16,4,16384]{2,1,0:T(4,128)(2,1)S(1)} async-done(((bf16[16,4,16384]{2,1,0:T(4,128)(2,1)}), bf16[16,4,16384]{2,1,0:T(4,128)(2,1)S(1)}, u32[]{:S(2)}, u32[]{:S(2)}) %all-to-all-start.1) | async-done | bytes 2097184 | tf_op jit(solution)/shard_map/all_to_all | solution.py:115
  57.9 2.1 %reshape.129 = bf16[64,16384]{1,0:T(8,128)(2,1)} reshape(bf16[16,4,16384]{2,1,0:T(4,128)(2,1)S(1)} %all-to-all-done.1) | data formatting | bytes 4194304 | tf_op jit(solution)/shard_map/reshape | solution.py:126
  59.9 2.0 %convolution_convert_fusion.1 = bf16[32,16384]{1,0:T(8,128)(2,1)S(1)} fusion(bf16[64,16384]{1,0:T(8,128)(2,1)} %reshape.129, s32[64]{0:T(128)S(1)} %select_n.12), kind=kOutput, calls=%fused_computation.1 | convolution fusion | flops 67635200 | bytes 3145984 | tf_op jit(solution)/shard_map/dot_general | solution.py:125
  62.5 4.7 %fusion = f32[128,1024]{1,0:T(8,128)S(1)} fusion(bf16[4096,128]{1,0:T(8,128)(2,1)S(1)} %reshape.130, bf16[1,1,2,4096,1024]{4,3,2,1,0:T(8,128)(2,1)} %param.8), kind=kOutput, calls=%fused_computation.2 | convolution fusion | flops 1073741824 | bytes 9961472 | tf_op jit(solution)/shard_map/dot_general | solution.py:134
  67.1 4.7 %fusion.2 = f32[128,1024]{1,0:T(8,128)S(1)} fusion(bf16[4096,128]{1,0:T(8,128)(2,1)S(1)} %reshape.130, bf16[1,1,2,4096,1024]{4,3,2,1,0:T(8,128)(2,1)} %param.8), kind=kOutput, calls=%fused_computation.4 | convolution fusion | flops 1073741824 | bytes 9961472 | tf_op jit(solution)/shard_map/dot_general | solution.py:131
  71.9 0.8 maximum_bitcast_fusion
  72.7 3.5 %all-to-all-start.2 = ((f32[8,2,8,8,128]{4,2,3,1,0:T(8,128)}), f32[8,2,8,8,128]{4,2,3,1,0:T(8,128)S(1)}, u32[]{:S(2)}, u32[]{:S(2)}) async-start(f32[8,2,8,8,128]{4,2,3,1,0:T(8,128)} %maximum_bitcast_fusion), calls=%async_computation.2 | async-start | bytes 1048576 | tf_op jit(solution)/shard_map/all_to_all | solution.py:30
  76.2 0.7 fusion.52
  76.9 9.5 %all-to-all-done.2 = f32[8,2,8,8,128]{4,2,3,1,0:T(8,128)S(1)} async-done(((f32[8,2,8,8,128]{4,2,3,1,0:T(8,128)}), f32[8,2,8,8,128]{4,2,3,1,0:T(8,128)S(1)}, u32[]{:S(2)}, u32[]{:S(2)}) %all-to-all-start.2) | async-done | bytes 524320 | tf_op jit(solution)/shard_map/all_to_all | solution.py:30
  86.5 3.2 %collective-permute-start.1 = (f32[2,8,2,128]{3,1,2,0:T(8,128)S(1)}, f32[2,8,2,128]{3,1,2,0:T(8,128)S(1)}, u32[]{:S(2)}, u32[]{:S(2)}) collective-permute-start(f32[2,8,2,128]{3,1,2,0:T(8,128)S(1)} %get-tuple-element.11), channel_id=1, source_target_pairs={{0,1},{1,2},{2,3},{3,4},{4,5},{5,6},{6,7},{7,8},{8,9},{9,10},{10,1... | collective-permute-start | bytes 49160 | tf_op jit(solution)/shard_map/ppermute | solution.py:42
  89.7 2.7 %collective-permute-start.2 = (f32[2,8,2,128]{3,1,2,0:T(8,128)S(1)}, f32[2,8,2,128]{3,1,2,0:T(8,128)S(1)}, u32[]{:S(2)}, u32[]{:S(2)}) collective-permute-start(f32[2,8,2,128]{3,1,2,0:T(8,128)S(1)} %get-tuple-element.12), channel_id=1, source_target_pairs={{1,0},{2,1},{3,2},{4,3},{5,4},{6,5},{7,6},{8,7},{9,8},{10,9},{11,1... | collective-permute-start | bytes 49160 | tf_op jit(solution)/shard_map/ppermute | solution.py:44
  93.0 4.4 %collective-permute-done.2 = f32[2,8,2,128]{3,1,2,0:T(8,128)S(1)} collective-permute-done((f32[2,8,2,128]{3,1,2,0:T(8,128)S(1)}, f32[2,8,2,128]{3,1,2,0:T(8,128)S(1)}, u32[]{:S(2)}, u32[]{:S(2)}) %collective-permute-start.2) | collective-permute-done | bytes 16416 | tf_op jit(solution)/shard_map/ppermute | solution.py:44
  97.5 15.8 %fusion.23 = f32[2,8,8,128]{3,1,2,0:T(8,128)S(1)} fusion(f32[2,8,8,128]{3,1,2,0:T(8,128)S(1)} %reduce_sum.42, f32[2,8,2,128]{3,1,2,0:T(8,128)S(1)} %collective-permute-done.2, f32[2,8,2,128]{3,1,2,0:T(8,128)S(1)} %collective-permute-done.1, f32[2,8,12,132]{3,1,2,0:T(8,128)S(1)} %select_maximum_fusion, f32[]{:T(128)} %bitcast.44, f32[]{:T(128)} %bitcast.43, ...), kind=kLoop, calls=%fused_computation.47 | loop fusion | flops 868352 | bytes 1474660 | tf_op jit(solution)/shard_map/add | solution.py:81
  (32 shorter events, 6.9 us)
Async XLA Ops:
  0.7 15.1 %collective-permute-start = (bf16[64,128]{1,0:T(8,128)(2,1)S(1)}, bf16[64,128]{1,0:T(8,128)(2,1)S(1)}, u32[]{:S(2)}, u32[]{:S(2)}) collective-permute-start(bf16[64,128]{1,0:T(8,128)(2,1)S(1)} %slice_bitcast_fusion), channel_id=1, source_target_pairs={{16,0},{32,16},{48,32},{64,48},{80,64},{96,80},{112,96},{17,1},{33... | collective-permute-start | bytes 49160 | tf_op jit(solution)/shard_map/ppermute | solution.py:19
  4.3 16.8 %all-to-all-start = ((s32[16,1,1]{2,1,0:T(1,128)}), s32[16,1,1]{2,1,0:T(1,128)S(1)}, u32[]{:S(2)}, u32[]{:S(2)}) async-start(s32[16,1,1]{2,1,0:T(1,128)} %copy.20), calls=%async_computation | async-start | bytes 16384 | tf_op jit(solution)/shard_map/all_to_all | solution.py:116
  21.1 36.7 %all-to-all-start.1 = ((bf16[16,4,16384]{2,1,0:T(4,128)(2,1)}), bf16[16,4,16384]{2,1,0:T(4,128)(2,1)S(1)}, u32[]{:S(2)}, u32[]{:S(2)}) async-start(bf16[16,4,16384]{2,1,0:T(4,128)(2,1)} %reshape.128), calls=%async_computation.1 | async-start | bytes 4194304 | tf_op jit(solution)/shard_map/all_to_all | solution.py:115
  71.8 4.4 %copy-start = (f32[5,5]{1,0:T(8,128)S(1)}, f32[5,5]{1,0:T(8,128)}, u32[]{:S(2)}) copy-start(f32[5,5]{1,0:T(8,128)} %param.9) | copy-start | bytes 304
  72.7 13.7 %all-to-all-start.2 = ((f32[8,2,8,8,128]{4,2,3,1,0:T(8,128)}), f32[8,2,8,8,128]{4,2,3,1,0:T(8,128)S(1)}, u32[]{:S(2)}, u32[]{:S(2)}) async-start(f32[8,2,8,8,128]{4,2,3,1,0:T(8,128)} %maximum_bitcast_fusion), calls=%async_computation.2 | async-start | bytes 1048576 | tf_op jit(solution)/shard_map/all_to_all | solution.py:30
  86.5 6.5 %collective-permute-start.1 = (f32[2,8,2,128]{3,1,2,0:T(8,128)S(1)}, f32[2,8,2,128]{3,1,2,0:T(8,128)S(1)}, u32[]{:S(2)}, u32[]{:S(2)}) collective-permute-start(f32[2,8,2,128]{3,1,2,0:T(8,128)S(1)} %get-tuple-element.11), channel_id=1, source_target_pairs={{0,1},{1,2},{2,3},{3,4},{4,5},{5,6},{6,7},{7,8},{8,9},{9,10},{10,1... | collective-permute-start | bytes 49160 | tf_op jit(solution)/shard_map/ppermute | solution.py:42
  89.7 7.7 %collective-permute-start.2 = (f32[2,8,2,128]{3,1,2,0:T(8,128)S(1)}, f32[2,8,2,128]{3,1,2,0:T(8,128)S(1)}, u32[]{:S(2)}, u32[]{:S(2)}) collective-permute-start(f32[2,8,2,128]{3,1,2,0:T(8,128)S(1)} %get-tuple-element.12), channel_id=1, source_target_pairs={{1,0},{2,1},{3,2},{4,3},{5,4},{6,5},{7,6},{8,7},{9,8},{10,9},{11,1... | collective-permute-start | bytes 49160 | tf_op jit(solution)/shard_map/ppermute | solution.py:44
where the time goes:
time: 116 us; the launch traced here: 114 us
  waiting for transfers between devices  42.7 us (37%)
  starting transfers between devices  24.8 us (21%)
  other arithmetic  22.9 us (20%)
  matrix products  12.5 us (11%)
  local copies, waits for them, and re-layouts  10.1 us (9%)
    all_to_all x1, waiting for transfers between devices, per_device(): lax.all_to_all(outgoing, 'tile', split_axis=0, concat_axis=0, tiled=True)  28.8 us
    add x1, other arithmetic, dip_apply(): result + dip_filter[down_step, side_step] * widened[:, :, down_step:down_...  15.8 us
    all_to_all x1, waiting for transfers between devices, sent_and_summed(): lax.all_to_all(cut_along(array, dim, devices), axis, 0, 0, tiled=True)  9.51 us
    all_to_all x1, starting transfers between devices, per_device(): lax.all_to_all(outgoing, 'tile', split_axis=0, concat_axis=0, tiled=True)  7.22 us
    all_to_all x1, starting transfers between devices, per_device(): lax.all_to_all(sent_counts, 'tile', split_axis=0, concat_axis=0, tiled=True)  6.99 us
    dot_general x1, matrix products, per_device(): lax.dot_general(slot_rows, matrices[1], contract_dims, preferred_element_...  4.66 us
    dot_general x1, matrix products, per_device(): lax.dot_general(slot_rows, matrices[0], contract_dims, preferred_element_...  4.65 us
    ppermute x1, waiting for transfers between devices, with_halo(): lax.ppermute(head, axis, [((i + 1) % count, i) for i in range(ends)])  4.4 us
  transfers between devices with their start and end apart: 6, of which 3 were waited for; matrix products, arithmetic and copies ran while one was open for 12% of the time, Pallas kernels for 0%

commit v1 on v0

v1 whole, which is shorter than its diff:
```python
import jax
import jax.numpy as jnp
from jax import lax
from jax.experimental import pallas as pl
from jax.experimental.pallas import tpu as pltpu
from jax.sharding import PartitionSpec as P

S = 64
P_SIZE = 256
WIN = 128
BR = 128
TZ = 8
TX = 128
MAXB = 32
NB = 16
HALF = WIN // 2
LOCAL = 512
AUX = LOCAL + HALF
ROWS = AUX + 16
SIDE = 4
RING = (0, 1, 3, 2)
BOTH = ("line", "tile")
N_LINE = 8
N_TILE = 16
CHUNK = 256
CHUNKS = MAXB * BR // CHUNK


def hops(offset, x_first):
    pairs = []
    for line in range(N_LINE):
        along_x = x_first == (line % 2 == 0)
        for x in range(SIDE):
            for z in range(SIDE):
                to_x, to_z = ((x + offset) % SIDE, z) if along_x else (x, (z + offset) % SIDE)
                pairs.append((line * N_TILE + x * SIDE + z, line * N_TILE + to_x * SIDE + to_z))
    return pairs


def table_kernel(out_ref):
    rows = lax.broadcasted_iota(jnp.int32, (WIN, P_SIZE), 0)
    cols = lax.broadcasted_iota(jnp.int32, (WIN, P_SIZE), 1)
    turns = (cols - P_SIZE // 2) * (2 * rows - (WIN - 1))
    unit = 2.0 * jnp.pi / 8192.0
    step = (((turns + 4096) & 8191) - 4096).astype(jnp.float32) * unit
    base = (((32 * turns + 4096) & 8191) - 4096).astype(jnp.float32) * unit
    offsets = lax.broadcasted_iota(jnp.int32, (WIN, 1), 0).astype(jnp.float32) - (WIN - 1) / 2
    taper = jnp.exp(-0.5 * (offsets / (0.4 * WIN)) ** 2)
    taper = taper / jnp.sqrt(jnp.sum(taper * taper, axis=0, keepdims=True))
    step_c, step_s = jnp.cos(step), jnp.sin(step)
    now_c, now_s = taper * jnp.cos(base), -taper * jnp.sin(base)
    for f in range(N_TILE):
        for q in range(2):
            half = slice(q * BR, (q + 1) * BR)
            out_ref[2 * f + q, :, :BR] = now_c[:, half].astype(jnp.bfloat16)
            out_ref[2 * f + q, :, BR:] = now_s[:, half].astype(jnp.bfloat16)
        now_c, now_s = now_c * step_c + now_s * step_s, now_s * step_c - now_c * step_s


def slant_tables():
    return pl.pallas_call(
        table_kernel,
        out_shape=jax.ShapeDtypeStruct((2 * N_TILE, WIN, 2 * BR), jnp.bfloat16),
        out_specs=pl.BlockSpec(memory_space=pltpu.VMEM),
        compiler_params=pltpu.CompilerParams(vmem_limit_bytes=16 * 2**20),
        name="slant_tables",
    )()


def place_of(offset):
    return jnp.where(offset == 2, 3, jnp.where(offset == 3, 2, offset))


def image_kernel(
    where_ref, own_ref, one_ref, three_ref, two_ref, table_ref, matrix_ref, out_ref,
    gathered, cos_ref, sin_ref, slots_re, slots_im, total, list_v, list_s, matrix_v, part_sem, matrix_sem, list_sem,
):
    tile, x, z, parity = where_ref[0], where_ref[1], where_ref[2], where_ref[3]
    parts = (own_ref, one_ref, three_ref, two_ref)
    part_copies = [
        pltpu.make_async_copy(part, gathered.at[pl.ds(SIDE * j, SIDE)], part_sem.at[j]) for j, part in enumerate(parts)
    ]
    for copy in part_copies:
        copy.start()

    def matrix_copy(c):
        rows = pl.ds(pl.multiple_of(c * CHUNK, CHUNK), CHUNK)
        return pltpu.make_async_copy(matrix_ref.at[0, 0, :, rows, :], matrix_v.at[c], matrix_sem.at[c])

    for c in range(CHUNKS):
        matrix_copy(c).start()
    for copy in part_copies:
        copy.wait()

    def place(f):
        dx, dz = (x - f // SIDE) & 3, (z - f % SIDE) & 3
        px, pz = place_of(dx), place_of(dz)
        return jnp.where(parity == 0, px * SIDE + pz, pz * SIDE + px)

    route_rows = [gathered[place(jnp.int32(f)), AUX : AUX + 8, :].astype(jnp.float32) for f in range(N_TILE)]
    routes = jnp.concatenate([row[0:1] for row in route_rows], 0)
    codes = jnp.concatenate([row[1:2] for row in route_rows], 0)
    lane = lax.broadcasted_iota(jnp.int32, (N_TILE, WIN), 1)
    mine = jnp.where((lane < NB) & (routes == tile.astype(jnp.float32)), 1.0, 0.0)
    lane_r = lax.broadcasted_iota(jnp.int32, (WIN, WIN), 0)
    lane_c = lax.broadcasted_iota(jnp.int32, (WIN, WIN), 1)
    before_b = jnp.dot(mine, jnp.where(lane_r < lane_c, 1.0, 0.0), preferred_element_type=jnp.float32)
    counts = jnp.dot(mine, jnp.ones((WIN, WIN), jnp.float32), preferred_element_type=jnp.float32)
    f_r = lax.broadcasted_iota(jnp.int32, (N_TILE, N_TILE), 0)
    f_c = lax.broadcasted_iota(jnp.int32, (N_TILE, N_TILE), 1)
    before_f = jnp.dot(jnp.where(f_c < f_r, 1.0, 0.0), counts, preferred_element_type=jnp.float32)
    rank = jnp.where(mine > 0.0, before_b + before_f, -1.0)
    slot_row = lax.broadcasted_iota(jnp.int32, (MAXB, WIN), 0).astype(jnp.float32)
    lane_wide = lax.broadcasted_iota(jnp.int32, (MAXB, WIN), 1)
    found = jnp.zeros((MAXB, WIN), jnp.float32)
    for f in range(N_TILE):
        hit = rank[f : f + 1] == slot_row
        found = found + jnp.where(hit, (lane_wide + NB * f).astype(jnp.float32), 0.0)
    which = jnp.sum(found, 1, keepdims=True)
    total_count = jnp.sum(counts[:, 0:1], 0, keepdims=True)
    listed = jnp.concatenate([jnp.broadcast_to(which, (MAXB, WIN)), jnp.broadcast_to(total_count, (8, WIN))], 0)
    list_v[...] = listed.astype(jnp.int32)
    list_copy = pltpu.make_async_copy(list_v, list_s, list_sem)
    list_copy.start()

    code_cols = jnp.concatenate([codes, jnp.zeros((WIN - N_TILE, WIN), jnp.float32)], 0).T[:S]
    angles = code_cols * (2.0 * jnp.pi / 256.0)
    cosines, sines = jnp.cos(angles), jnp.sin(angles)
    for f in range(N_TILE):
        cos_ref[f] = jnp.broadcast_to(cosines[:, f : f + 1], (S, BR))
        sin_ref[f] = jnp.broadcast_to(sines[:, f : f + 1], (S, BR))
    list_copy.wait()
    count = list_s[MAXB, 0]

    def interleave(real, imag):
        pieces = []
        for d in range(N_LINE):
            pieces += [real[8 * d : 8 * d + 8], imag[8 * d : 8 * d + 8]]
        return jnp.concatenate(pieces, 0)

    def one_slot(n):
        block = list_s[n, 0]
        f, b = block // NB, block % NB
        rows = pl.ds(pl.multiple_of((b // 2) * HALF, HALF), WIN)
        window = gathered[place(f), rows, :]
        stacked = lax.dot_general(
            window, table_ref[2 * f + b % 2], (((0,), (0,)), ((), ())), preferred_element_type=jnp.float32
        )
        real = stacked[:S, :BR] - stacked[S:, BR:]
        imag = stacked[S:, :BR] + stacked[:S, BR:]
        cosine, sine = cos_ref[f], sin_ref[f]
        keep = n < count
        turned_re = jnp.where(keep, real * cosine + imag * sine, 0.0)
        turned_im = jnp.where(keep, imag * cosine - real * sine, 0.0)
        return interleave(turned_re, turned_im).astype(jnp.bfloat16), interleave(-turned_im, turned_re).astype(jnp.bfloat16)

    def one_chunk(c, carry):
        first = one_slot(2 * c)
        second = one_slot(2 * c + 1)
        for ref, k in ((slots_re, 0), (slots_im, 1)):
            ref[c, :, :BR] = first[k]
            ref[c, :, BR:] = second[k]
        return carry

    lax.fori_loop(0, CHUNKS, one_chunk, 0)
    total[...] = jnp.zeros_like(total)

    def multiply(c, carry):
        matrix_copy(c).wait()
        total[...] += jnp.dot(slots_re[c], matrix_v[c, 0], preferred_element_type=jnp.float32) + jnp.dot(
            slots_im[c], matrix_v[c, 1], preferred_element_type=jnp.float32
        )
        return carry

    lax.fori_loop(0, CHUNKS, multiply, 0)
    for d in range(N_LINE):
        for depth in range(TZ):
            out_ref[d, depth] = total[16 * d : 16 * d + 16, TX * depth : TX * depth + TX].astype(jnp.bfloat16)


def partial_image(where, own, one, three, two, tables, beam_matrix):
    any_space = pl.BlockSpec(memory_space=pl.ANY)
    return pl.pallas_call(
        image_kernel,
        out_shape=jax.ShapeDtypeStruct((N_LINE, TZ, 16, TX), jnp.bfloat16),
        in_specs=[pl.BlockSpec(memory_space=pltpu.SMEM)]
        + [any_space] * 4
        + [pl.BlockSpec(memory_space=pltpu.VMEM), any_space],
        out_specs=pl.BlockSpec(memory_space=pltpu.VMEM),
        scratch_shapes=[
            pltpu.VMEM((N_TILE, ROWS, WIN), jnp.bfloat16),
            pltpu.VMEM((N_TILE, S, BR), jnp.float32),
            pltpu.VMEM((N_TILE, S, BR), jnp.float32),
            pltpu.VMEM((CHUNKS, 2 * S, CHUNK), jnp.bfloat16),
            pltpu.VMEM((CHUNKS, 2 * S, CHUNK), jnp.bfloat16),
            pltpu.VMEM((2 * S, TZ * TX), jnp.float32),
            pltpu.VMEM((MAXB + 8, WIN), jnp.int32),
            pltpu.SMEM((MAXB + 8, WIN), jnp.int32),
            pltpu.VMEM((CHUNKS, 2, CHUNK, TZ * TX), jnp.bfloat16),
            pltpu.SemaphoreType.DMA((4,)),
            pltpu.SemaphoreType.DMA((CHUNKS,)),
            pltpu.SemaphoreType.DMA,
        ],
        compiler_params=pltpu.CompilerParams(vmem_limit_bytes=40 * 2**20),
        name="partial_image",
    )(where, own, one, three, two, tables, beam_matrix)


def sum_kernel(parts_ref, out_ref, top_ref, bottom_ref):
    for depth in range(TZ):
        total = parts_ref[0, depth].astype(jnp.float32)
        for line in range(1, N_LINE):
            total = total + parts_ref[line, depth].astype(jnp.float32)
        out_ref[depth] = total
        if depth < 2:
            top_ref[depth] = total
        if depth >= TZ - 2:
            bottom_ref[depth - TZ + 2] = total


def summed_lines(parts):
    shapes = [jax.ShapeDtypeStruct((rows, 16, TX), jnp.float32) for rows in (TZ, 2, 2)]
    return pl.pallas_call(
        sum_kernel,
        out_shape=shapes,
        in_specs=[pl.BlockSpec(memory_space=pltpu.VMEM)],
        out_specs=[pl.BlockSpec(memory_space=pltpu.VMEM)] * 3,
        compiler_params=pltpu.CompilerParams(vmem_limit_bytes=8 * 2**20),
        name="summed_lines",
    )(parts)


def dip_kernel(filter_ref, above_ref, image_ref, below_ref, out_ref):
    rows = [above_ref[0], above_ref[1]] + [image_ref[d] for d in range(TZ)] + [below_ref[0], below_ref[1]]
    lane = lax.broadcasted_iota(jnp.int32, (16, TX), 1)
    results = [jnp.zeros((16, TX), jnp.float32) for _ in range(TZ)]
    for side in range(5):
        move = side - 2
        for source in range(TZ + 4):
            row = rows[source]
            if move:
                inside = (lane + move >= 0) & (lane + move < TX)
                row = jnp.where(inside, pltpu.roll(row, (-move) % TX, 1), 0.0)
            for depth in range(max(0, source - 4), min(TZ, source + 1)):
                results[depth] = results[depth] + filter_ref[source - depth, side] * row
    for depth in range(TZ):
        for part in range(2):
            out_ref[pl.ds(part * 64 + depth, 8, stride=TZ), :] = results[depth][8 * part : 8 * part + 8]


def dip_filtered(dip_filter, above, image, below):
    vmem = pl.BlockSpec(memory_space=pltpu.VMEM)
    return pl.pallas_call(
        dip_kernel,
        out_shape=jax.ShapeDtypeStruct((2 * 8 * TZ, TX), jnp.float32),
        in_specs=[pl.BlockSpec(memory_space=pltpu.SMEM), vmem, vmem, vmem],
        out_specs=vmem,
        compiler_params=pltpu.CompilerParams(vmem_limit_bytes=8 * 2**20),
        name="dip_filtered",
    )(dip_filter, above, image, below)


def per_device(traces, codes, routes, beam_matrix, dip_filter):
    line, tile = lax.axis_index("line"), lax.axis_index("tile")
    where = jnp.stack([tile, tile // SIDE, tile % SIDE, line % 2]).astype(jnp.int32)
    local = traces[0]
    rim = lax.ppermute(local[:HALF], "line", [(i + 1, i) for i in range(N_LINE - 1)])
    routes_row = jnp.pad(routes.astype(jnp.bfloat16), ((0, 0), (0, WIN - NB)))
    codes_row = jnp.pad(codes.astype(jnp.bfloat16), ((0, 0), (0, WIN - S)))
    aux = jnp.concatenate([routes_row, codes_row, jnp.zeros((14, WIN), jnp.bfloat16)], 0)
    tables = slant_tables()
    own = jnp.concatenate([local, rim, aux], 0)
    near = [own] + [lax.ppermute(own, BOTH, hops(o, False)) for o in RING[1:]]
    stack = jnp.stack(near)
    far = [lax.ppermute(stack, BOTH, hops(o, True)) for o in RING[1:]]
    partial = partial_image(where, stack, *far, tables, beam_matrix)
    parts = lax.all_to_all(partial, "line", 0, 0, tiled=True)
    image, top, bottom = summed_lines(parts)
    above = lax.ppermute(bottom, "tile", [(i, i + 1) for i in range(N_TILE - 1)])
    below = lax.ppermute(top, "tile", [(i + 1, i) for i in range(N_TILE - 1)])
    return dip_filtered(dip_filter, above, image, below).reshape(2, 8, TZ, TX)


def solution(mesh):
    in_specs = (
        P("tile", "line", None),
        P("tile", None),
        P("line", "tile"),
        P("line", "tile", None, None, None),
        P(),
    )
    out_specs = P(None, "line", "tile", None)
    return jax.shard_map(per_device, mesh=mesh, in_specs=in_specs, out_specs=out_specs, check_vma=False)
```

time: 116 us -> 70.8 us (0.61); the launches traced: 114 us -> 70.5 us
  other arithmetic: 22.9 us -> 1.48 us
  waiting for transfers between devices: 42.7 us -> 22.2 us
  Pallas kernels: 0 us -> 15.9 us
  matrix products: 12.5 us -> 0 us
  blocking collectives: 0 us -> 12.4 us
  starting transfers between devices: 24.8 us -> 16.5 us
  local copies, waits for them, and re-layouts: 10.1 us -> 1.82 us
    all_to_all x3 -> x0, waiting for transfers between devices: 38.3 us -> none  [the longest x1 28.8 us: per_device(): lax.all_to_all(outgoing, 'tile', split_axis=0, concat_axis=0, tiled=True)]
    ppermute x3 -> x9, waiting for transfers between devices: 4.4 us -> 22.2 us  [the longest x3 11.5 us: per_device(): far = [lax.ppermute(stack, BOTH, hops(o, True)) for o in RING[1:]]]
    all_to_all x3 -> x0, starting transfers between devices: 17.7 us -> none  [the longest x1 7.22 us: per_device(): lax.all_to_all(outgoing, 'tile', split_axis=0, concat_axis=0, tiled=True)]
    pallas_call x0 -> x4, Pallas kernels: none -> 15.9 us  [the longest x1 12.8 us: partial_image(): pl.pallas_call(image_kernel, out_shape=jax.ShapeDtypeStruct((N_LINE, TZ,...]
    add x1 -> x0, other arithmetic: 15.8 us -> none  [dip_apply(): result + dip_filter[down_step, side_step] * widened[:, :, down_step:down_...]
    dot_general x5 -> x0, matrix products: 12.5 us -> none  [the longest x1 4.66 us: per_device(): lax.dot_general(slot_rows, matrices[1], contract_dims, preferred_element_...]
    all_to_all x0 -> x1, blocking collectives: none -> 12.4 us  [per_device(): parts = lax.all_to_all(partial, 'line', 0, 0, tiled=True)]
    ppermute x3 -> x9, starting transfers between devices: 7.12 us -> 16.5 us  [the longest x3 5.13 us: per_device(): far = [lax.ppermute(stack, BOTH, hops(o, True)) for o in RING[1:]]]
  transfers between devices with their start and end apart: 6 -> 9, of which waited for: 3 -> 6; matrix products, arithmetic and copies ran while one was open for 12% -> 2% of each run, Pallas kernels for 0% -> 2%
where the time goes in v1:
time: 70.8 us; the launch traced here: 70.5 us
  waiting for transfers between devices  22.2 us (31%)
  starting transfers between devices  16.5 us (23%)
  Pallas kernels  15.9 us (22%)
  blocking collectives  12.4 us (18%)
  local copies, waits for them, and re-layouts  1.82 us (3%)
  other arithmetic  1.48 us (2%)
    pallas_call x1, Pallas kernels, partial_image(): pl.pallas_call(image_kernel, out_shape=jax.ShapeDtypeStruct((N_LINE, TZ,...  12.8 us
    all_to_all x1, blocking collectives, per_device(): parts = lax.all_to_all(partial, 'line', 0, 0, tiled=True)  12.4 us
    ppermute x3, waiting for transfers between devices, per_device(): far = [lax.ppermute(stack, BOTH, hops(o, True)) for o in RING[1:]]  11.5 us
    ppermute x1, waiting for transfers between devices, per_device(): below = lax.ppermute(top, 'tile', [(i + 1, i) for i in range(N_TILE - 1)])  5.8 us
    ppermute x3, starting transfers between devices, per_device(): far = [lax.ppermute(stack, BOTH, hops(o, True)) for o in RING[1:]]  5.13 us
    ppermute x3, waiting for transfers between devices, per_device(): near = [own] + [lax.ppermute(own, BOTH, hops(o, False)) for o in RING[1:]]  4.53 us
    ppermute x1, starting transfers between devices, per_device(): lax.ppermute(bottom, 'tile', [(i, i + 1) for i in range(N_TILE - 1)])  4.26 us
    ppermute x3, starting transfers between devices, per_device(): near = [own] + [lax.ppermute(own, BOTH, hops(o, False)) for o in RING[1:]]  3.87 us
  transfers between devices with their start and end apart: 9, of which 6 were waited for; matrix products, arithmetic and copies ran while one was open for 2% of the time, Pallas kernels for 2%

profile of v1, /device:TPU:96, one launch (start us, length us, event | category | flops | bytes accessed | tf_op | source)
XLA Modules:
  0.0 70.5 jit_solution(14230267708266076768)
XLA Ops:
  0.0 0.7 %slice_bitcast_fusion = bf16[64,128]{1,0:T(8,128)(2,1)S(1)} fusion(bf16[1,512,128]{2,1,0:T(8,128)(2,1)} %param.5), kind=kLoop, calls=%fused_computation.1 | loop fusion | bytes 32768 | tf_op jit(solution)/shard_map/slice | solution.py:267
  0.7 1.3 %collective-permute-start = (bf16[64,128]{1,0:T(8,128)(2,1)S(1)}, bf16[64,128]{1,0:T(8,128)(2,1)S(1)}, u32[]{:S(2)}, u32[]{:S(2)}) collective-permute-start(bf16[64,128]{1,0:T(8,128)(2,1)S(1)} %slice_bitcast_fusion), channel_id=1, source_target_pairs={{16,0},{32,16},{48,32},{64,48},{80,64},{96,80},{112,96},{17,1},{33... | collective-permute-start | bytes 49160 | tf_op jit(solution)/shard_map/ppermute | solution.py:267
  2.0 0.7 convert_element_type.11
  2.7 0.7 convert_element_type.10
  3.4 0.4 collective-permute-done
  3.8 1.1 %concatenate.3 = bf16[592,128]{1,0:T(8,128)(2,1)S(1)} concatenate(bf16[512,128]{1,0:T(8,128)(2,1)} %bitcast.13, bf16[64,128]{1,0:T(8,128)(2,1)S(1)} %collective-permute-done, bf16[1,128]{1,0:T(2,128)(2,1)S(1)} %pad.8, bf16[1,128]{1,0:T(2,128)(2,1)S(1)} %pad.9, bf16[14,128]{1,0:T(8,128)(2,1)S(1)} %broadcast_in_dim.3), dimensions={0} | concatenate | bytes 303104 | tf_op jit(solution)/shard_map/concatenate | solution.py:272
  4.9 0.6 collective-permute-start.3
  5.5 3.2 %collective-permute-start.1 = (bf16[592,128]{1,0:T(8,128)(2,1)S(1)}, bf16[592,128]{1,0:T(8,128)(2,1)S(1)}, u32[]{:S(2)}, u32[]{:S(2)}) collective-permute-start(bf16[592,128]{1,0:T(8,128)(2,1)S(1)} %concatenate.3), channel_id=1, source_target_pairs={{0,1},{1,2},{2,3},{3,0},{4,5},{5,6},{6,7},{7,4},{8,9},{9,10},{10,1... | collective-permute-start | bytes 454664 | tf_op jit(solution)/shard_map/ppermute | solution.py:273
  8.8 3.0 %collective-permute-done.3 = bf16[592,128]{1,0:T(8,128)(2,1)S(1)} collective-permute-done((bf16[592,128]{1,0:T(8,128)(2,1)S(1)}, bf16[592,128]{1,0:T(8,128)(2,1)S(1)}, u32[]{:S(2)}, u32[]{:S(2)}) %collective-permute-start.3) | collective-permute-done | bytes 151584 | tf_op jit(solution)/shard_map/ppermute | solution.py:273
  11.8 1.5 %collective-permute-done.2 = bf16[592,128]{1,0:T(8,128)(2,1)S(1)} collective-permute-done((bf16[592,128]{1,0:T(8,128)(2,1)S(1)}, bf16[592,128]{1,0:T(8,128)(2,1)S(1)}, u32[]{:S(2)}, u32[]{:S(2)}) %collective-permute-start.2) | collective-permute-done | bytes 151584 | tf_op jit(solution)/shard_map/ppermute | solution.py:273
  13.3 0.1 pad_maximum_fusion.own_ref
  13.4 3.1 %collective-permute-start.6 = (bf16[4,592,128]{2,1,0:T(8,128)(2,1)S(1)}, bf16[4,592,128]{2,1,0:T(8,128)(2,1)S(1)}, u32[]{:S(2)}, u32[]{:S(2)}) collective-permute-start(bf16[4,592,128]{2,1,0:T(8,128)(2,1)S(1)} %pad_maximum_fusion.own_ref), channel_id=1, source_target_pairs={{0,8},{1,9},{2,10},{3,11},{4,12},{5,13},{6,14},{7,15},{8,0},{9,1},... | collective-permute-start | bytes 1818632 | tf_op jit(solution)/shard_map/ppermute | solution.py:275
  16.5 1.1 %collective-permute-start.5 = (bf16[4,592,128]{2,1,0:T(8,128)(2,1)S(1)}, bf16[4,592,128]{2,1,0:T(8,128)(2,1)}, u32[]{:S(2)}, u32[]{:S(2)}) collective-permute-start(bf16[4,592,128]{2,1,0:T(8,128)(2,1)S(1)} %pad_maximum_fusion.own_ref), channel_id=1, source_target_pairs={{0,12},{1,13},{2,14},{3,15},{4,0},{5,1},{6,2},{7,3},{8,4},{9,5},{1... | collective-permute-start | bytes 1818632 | tf_op jit(solution)/shard_map/ppermute | solution.py:275
  17.6 0.9 %collective-permute-start.4 = (bf16[4,592,128]{2,1,0:T(8,128)(2,1)S(1)}, bf16[4,592,128]{2,1,0:T(8,128)(2,1)}, u32[]{:S(2)}, u32[]{:S(2)}) collective-permute-start(bf16[4,592,128]{2,1,0:T(8,128)(2,1)S(1)} %pad_maximum_fusion.own_ref), channel_id=1, source_target_pairs={{0,4},{1,5},{2,6},{3,7},{4,8},{5,9},{6,10},{7,11},{8,12},{9,13},{1... | collective-permute-start | bytes 1818632 | tf_op jit(solution)/shard_map/ppermute | solution.py:275
  18.5 1.7 %slant_tables.1.table_ref = bf16[32,128,256]{2,1,0:T(8,128)(2,1)S(1)} custom-call(), custom_call_target="tpu_custom_call" | custom-call | tf_op jit(solution)/shard_map/slant_tables/pallas_call | solution.py:61
  20.2 0.1 pad_add_fusion.where_ref
  20.3 4.8 %collective-permute-done.6.two_ref = bf16[4,592,128]{2,1,0:T(8,128)(2,1)S(1)} collective-permute-done((bf16[4,592,128]{2,1,0:T(8,128)(2,1)S(1)}, bf16[4,592,128]{2,1,0:T(8,128)(2,1)S(1)}, u32[]{:S(2)}, u32[]{:S(2)}) %collective-permute-start.6) | collective-permute-done | bytes 606240 | tf_op jit(solution)/shard_map/ppermute | solution.py:275
  25.1 6.6 %collective-permute-done.5.three_ref = bf16[4,592,128]{2,1,0:T(8,128)(2,1)} collective-permute-done((bf16[4,592,128]{2,1,0:T(8,128)(2,1)S(1)}, bf16[4,592,128]{2,1,0:T(8,128)(2,1)}, u32[]{:S(2)}, u32[]{:S(2)}) %collective-permute-start.5) | collective-permute-done | bytes 606240 | tf_op jit(solution)/shard_map/ppermute | solution.py:275
  31.7 12.8 %partial_image.1 = bf16[8,8,16,128]{3,2,1,0:T(8,128)(2,1)S(1)} custom-call(s32[4]{0:T(128)S(1)} %pad_add_fusion.where_ref, bf16[4,592,128]{2,1,0:T(8,128)(2,1)S(1)} %pad_maximum_fusion.own_ref, bf16[4,592,128]{2,1,0:T(8,128)(2,1)} %collective-permute-done.4.one_ref, bf16[4,592,128]{2,1,0:T(8,128)(2,1)} %collective-permute-done.5.three_ref, ...), custom_call_target="tpu_custom_call" | custom-call | tf_op jit(solution)/shard_map/partial_image/pallas_call | solution.py:183
  44.6 12.4 %all_to_all.5.parts_ref = bf16[8,8,16,128]{3,2,1,0:T(8,128)(2,1)S(1)} all-to-all(bf16[8,8,16,128]{3,2,1,0:T(8,128)(2,1)S(1)} %partial_image.1), channel_id=1, replica_groups=mesh['line'=8,'tile'=16] {'line'}, dimensions={0} | all-to-all | bytes 524288 | tf_op jit(solution)/shard_map/all_to_all | solution.py:277
  57.0 4.3 %collective-permute-start.7 = (f32[2,16,128]{2,1,0:T(8,128)S(1)}, f32[2,16,128]{2,1,0:T(8,128)S(1)}, u32[]{:S(2)}, u32[]{:S(2)}) collective-permute-start(f32[2,16,128]{2,1,0:T(8,128)S(1)} %get-tuple-element.8), channel_id=1, source_target_pairs={{0,1},{1,2},{2,3},{3,4},{4,5},{5,6},{6,7},{7,8},{8,9},{9,10},{10,1... | collective-permute-start | bytes 49160 | tf_op jit(solution)/shard_map/ppermute | solution.py:279
  61.3 1.9 %collective-permute-start.8 = (f32[2,16,128]{2,1,0:T(8,128)S(1)}, f32[2,16,128]{2,1,0:T(8,128)S(1)}, u32[]{:S(2)}, u32[]{:S(2)}) collective-permute-start(f32[2,16,128]{2,1,0:T(8,128)S(1)} %get-tuple-element.10), channel_id=1, source_target_pairs={{1,0},{2,1},{3,2},{4,3},{5,4},{6,5},{7,6},{8,7},{9,8},{10,9},{11,1... | collective-permute-start | bytes 49160 | tf_op jit(solution)/shard_map/ppermute | solution.py:280
  63.2 5.8 %collective-permute-done.8.below_ref = f32[2,16,128]{2,1,0:T(8,128)S(1)} collective-permute-done((f32[2,16,128]{2,1,0:T(8,128)S(1)}, f32[2,16,128]{2,1,0:T(8,128)S(1)}, u32[]{:S(2)}, u32[]{:S(2)}) %collective-permute-start.8) | collective-permute-done | bytes 16416 | tf_op jit(solution)/shard_map/ppermute | solution.py:280
  69.1 1.4 %dip_filtered.1 = f32[128,128]{1,0:T(8,128)} custom-call(f32[5,5]{1,0:T(8,128)S(1)} %copy-done, f32[2,16,128]{2,1,0:T(8,128)S(1)} %collective-permute-done.7.above_ref, f32[8,16,128]{2,1,0:T(8,128)S(1)} %get-tuple-element.9.image_ref, f32[2,16,128]{2,1,0:T(8,128)S(1)} %collective-permute-done.8.below_ref), custom_call_target="tpu_custom_call" | custom-call | tf_op jit(solution)/shard_map/dip_filtered/pallas_call | solution.py:253
  (10 shorter events, 0.1 us)
Async XLA Ops:
  0.0 69.0 %copy-start = (f32[5,5]{1,0:T(8,128)S(1)}, f32[5,5]{1,0:T(8,128)}, u32[]{:S(2)}) copy-start(f32[5,5]{1,0:T(8,128)} %filter_ref.1) | copy-start | bytes 304
  0.7 3.1 %collective-permute-start = (bf16[64,128]{1,0:T(8,128)(2,1)S(1)}, bf16[64,128]{1,0:T(8,128)(2,1)S(1)}, u32[]{:S(2)}, u32[]{:S(2)}) collective-permute-start(bf16[64,128]{1,0:T(8,128)(2,1)S(1)} %slice_bitcast_fusion), channel_id=1, source_target_pairs={{16,0},{32,16},{48,32},{64,48},{80,64},{96,80},{112,96},{17,1},{33... | collective-permute-start | bytes 49160 | tf_op jit(solution)/shard_map/ppermute | solution.py:267
  4.9 6.9 %collective-permute-start.3 = (bf16[592,128]{1,0:T(8,128)(2,1)S(1)}, bf16[592,128]{1,0:T(8,128)(2,1)S(1)}, u32[]{:S(2)}, u32[]{:S(2)}) collective-permute-start(bf16[592,128]{1,0:T(8,128)(2,1)S(1)} %concatenate.3), channel_id=1, source_target_pairs={{0,2},{1,3},{2,0},{3,1},{4,6},{5,7},{6,4},{7,5},{8,10},{9,11},{10,... | collective-permute-start | bytes 454664 | tf_op jit(solution)/shard_map/ppermute | solution.py:273
  5.5 7.8 %collective-permute-start.2 = (bf16[592,128]{1,0:T(8,128)(2,1)S(1)}, bf16[592,128]{1,0:T(8,128)(2,1)S(1)}, u32[]{:S(2)}, u32[]{:S(2)}) collective-permute-start(bf16[592,128]{1,0:T(8,128)(2,1)S(1)} %concatenate.3), channel_id=1, source_target_pairs={{0,3},{1,0},{2,1},{3,2},{4,7},{5,4},{6,5},{7,6},{8,11},{9,8},{10,9... | collective-permute-start | bytes 454664 | tf_op jit(solution)/shard_map/ppermute | solution.py:273
  5.5 7.8 %collective-permute-start.1 = (bf16[592,128]{1,0:T(8,128)(2,1)S(1)}, bf16[592,128]{1,0:T(8,128)(2,1)S(1)}, u32[]{:S(2)}, u32[]{:S(2)}) collective-permute-start(bf16[592,128]{1,0:T(8,128)(2,1)S(1)} %concatenate.3), channel_id=1, source_target_pairs={{0,1},{1,2},{2,3},{3,0},{4,5},{5,6},{6,7},{7,4},{8,9},{9,10},{10,1... | collective-permute-start | bytes 454664 | tf_op jit(solution)/shard_map/ppermute | solution.py:273
  13.4 11.7 %collective-permute-start.6 = (bf16[4,592,128]{2,1,0:T(8,128)(2,1)S(1)}, bf16[4,592,128]{2,1,0:T(8,128)(2,1)S(1)}, u32[]{:S(2)}, u32[]{:S(2)}) collective-permute-start(bf16[4,592,128]{2,1,0:T(8,128)(2,1)S(1)} %pad_maximum_fusion.own_ref), channel_id=1, source_target_pairs={{0,8},{1,9},{2,10},{3,11},{4,12},{5,13},{6,14},{7,15},{8,0},{9,1},... | collective-permute-start | bytes 1818632 | tf_op jit(solution)/shard_map/ppermute | solution.py:275
  16.5 15.3 %collective-permute-start.5 = (bf16[4,592,128]{2,1,0:T(8,128)(2,1)S(1)}, bf16[4,592,128]{2,1,0:T(8,128)(2,1)}, u32[]{:S(2)}, u32[]{:S(2)}) collective-permute-start(bf16[4,592,128]{2,1,0:T(8,128)(2,1)S(1)} %pad_maximum_fusion.own_ref), channel_id=1, source_target_pairs={{0,12},{1,13},{2,14},{3,15},{4,0},{5,1},{6,2},{7,3},{8,4},{9,5},{1... | collective-permute-start | bytes 1818632 | tf_op jit(solution)/shard_map/ppermute | solution.py:275
  17.6 14.1 %collective-permute-start.4 = (bf16[4,592,128]{2,1,0:T(8,128)(2,1)S(1)}, bf16[4,592,128]{2,1,0:T(8,128)(2,1)}, u32[]{:S(2)}, u32[]{:S(2)}) collective-permute-start(bf16[4,592,128]{2,1,0:T(8,128)(2,1)S(1)} %pad_maximum_fusion.own_ref), channel_id=1, source_target_pairs={{0,4},{1,5},{2,6},{3,7},{4,8},{5,9},{6,10},{7,11},{8,12},{9,13},{1... | collective-permute-start | bytes 1818632 | tf_op jit(solution)/shard_map/ppermute | solution.py:275
  57.0 6.2 %collective-permute-start.7 = (f32[2,16,128]{2,1,0:T(8,128)S(1)}, f32[2,16,128]{2,1,0:T(8,128)S(1)}, u32[]{:S(2)}, u32[]{:S(2)}) collective-permute-start(f32[2,16,128]{2,1,0:T(8,128)S(1)} %get-tuple-element.8), channel_id=1, source_target_pairs={{0,1},{1,2},{2,3},{3,4},{4,5},{5,6},{6,7},{7,8},{8,9},{9,10},{10,1... | collective-permute-start | bytes 49160 | tf_op jit(solution)/shard_map/ppermute | solution.py:279
  61.3 7.7 %collective-permute-start.8 = (f32[2,16,128]{2,1,0:T(8,128)S(1)}, f32[2,16,128]{2,1,0:T(8,128)S(1)}, u32[]{:S(2)}, u32[]{:S(2)}) collective-permute-start(f32[2,16,128]{2,1,0:T(8,128)S(1)} %get-tuple-element.10), channel_id=1, source_target_pairs={{1,0},{2,1},{3,2},{4,3},{5,4},{6,5},{7,6},{8,7},{9,8},{10,9},{11,1... | collective-permute-start | bytes 49160 | tf_op jit(solution)/shard_map/ppermute | solution.py:280

commit v2 on v1

v2 whole, which is shorter than its diff:
```python
import functools

import jax
import jax.numpy as jnp
from jax import lax
from jax.experimental import pallas as pl
from jax.experimental.pallas import tpu as pltpu
from jax.sharding import PartitionSpec as P


S = 64
P_SIZE = 256
WIN = 128
BR = 128
TZ = 8
TX = 128
MAXB = 32
NB = 16
HALF = WIN // 2
SIDE = 4
RING = (0, 1, 3, 2)
BOTH = ("line", "tile")
N_LINE = 8
N_TILE = 16
PAIR = 2 * BR
WIDE = TZ * TX
STREAMS = 16


def hops(offset, x_first):
    pairs = []
    for line in range(N_LINE):
        along_x = x_first == (line % 2 == 0)
        for x in range(SIDE):
            for z in range(SIDE):
                to_x, to_z = ((x + offset) % SIDE, z) if along_x else (x, (z + offset) % SIDE)
                pairs.append((line * N_TILE + x * SIDE + z, line * N_TILE + to_x * SIDE + to_z))
    return pairs


def prepare_kernel(matrix_ref, table_ref, held_ref, sems):
    copies = []
    for k in range(2):
        for part in range(STREAMS // 2):
            rows = pl.ds(part * (2 * MAXB * BR // STREAMS), 2 * MAXB * BR // STREAMS)
            copies.append(
                pltpu.make_async_copy(
                    matrix_ref.at[0, 0, k, rows, :], held_ref.at[k, rows, :], sems.at[len(copies)]
                )
            )
    for copy in copies:
        copy.start()
    rows = lax.broadcasted_iota(jnp.int32, (WIN, P_SIZE), 0)
    cols = lax.broadcasted_iota(jnp.int32, (WIN, P_SIZE), 1)
    turns = (cols - P_SIZE // 2) * (2 * rows - (WIN - 1))
    unit = 2.0 * jnp.pi / 8192.0
    step = (((turns + 4096) & 8191) - 4096).astype(jnp.float32) * unit
    base = (((32 * turns + 4096) & 8191) - 4096).astype(jnp.float32) * unit
    offsets = lax.broadcasted_iota(jnp.int32, (WIN, 1), 0).astype(jnp.float32) - (WIN - 1) / 2
    taper = jnp.exp(-0.5 * (offsets / (0.4 * WIN)) ** 2)
    taper = taper / jnp.sqrt(jnp.sum(taper * taper, axis=0, keepdims=True))
    step_c, step_s = jnp.cos(step), jnp.sin(step)
    now_c, now_s = taper * jnp.cos(base), -taper * jnp.sin(base)
    for f in range(N_TILE):
        for q in range(2):
            half = slice(q * BR, (q + 1) * BR)
            table_ref[2 * f + q, :, :BR] = now_c[:, half].astype(jnp.bfloat16)
            table_ref[2 * f + q, :, BR:] = now_s[:, half].astype(jnp.bfloat16)
        now_c, now_s = now_c * step_c + now_s * step_s, now_s * step_c - now_c * step_s
    for copy in copies:
        copy.wait()


def prepared(beam_matrix):
    return pl.pallas_call(
        prepare_kernel,
        out_shape=[
            pltpu.VMEM((2 * N_TILE, WIN, 2 * BR), jnp.bfloat16),
            pltpu.VMEM((2, MAXB * BR, WIDE), jnp.bfloat16),
        ],
        in_specs=[pl.BlockSpec(memory_space=pltpu.HBM)],
        out_specs=[pl.BlockSpec(memory_space=pltpu.VMEM)] * 2,
        scratch_shapes=[pltpu.SemaphoreType.DMA((STREAMS,))],
        compiler_params=pltpu.CompilerParams(vmem_limit_bytes=4 * 2**20),
        name="prepared",
    )(pltpu.with_memory_space_constraint(beam_matrix, pltpu.HBM))


def offset_of(place):
    return jnp.where(place == 3, 2, jnp.where(place == 2, 3, place))


def plan_kernel(own_ref, one_ref, three_ref, two_ref, plan_ref, cos_ref, sin_ref):
    tile = lax.axis_index("tile")
    x, z, parity = tile >> 2, tile & 3, lax.axis_index("line") & 1
    rows = [ref[i, :8, :].astype(jnp.float32) for ref in (own_ref, one_ref, three_ref, two_ref) for i in range(SIDE)]
    routes = jnp.concatenate([row[0:1] for row in rows], 0)
    codes = jnp.concatenate([row[1:2] for row in rows], 0)

    def sender(place):
        far, near = offset_of(place >> 2), offset_of(place & 3)
        dx, dz = jnp.where(parity == 0, far, near), jnp.where(parity == 0, near, far)
        return (((x - dx) & 3) << 2) + ((z - dz) & 3)

    wide = (N_TILE, WIN)
    place_r, lane = lax.broadcasted_iota(jnp.int32, wide, 0), lax.broadcasted_iota(jnp.int32, wide, 1)
    sender_r = sender(place_r)
    mine = jnp.where((lane < NB) & (routes == tile.astype(jnp.float32)), 1.0, 0.0)
    lane_r, lane_c = (lax.broadcasted_iota(jnp.int32, (WIN, WIN), axis) for axis in (0, 1))
    before_b = jnp.dot(mine, jnp.where(lane_r < lane_c, 1.0, 0.0), preferred_element_type=jnp.float32)
    counts = jnp.dot(mine, jnp.ones((WIN, WIN), jnp.float32), preferred_element_type=jnp.float32)
    place_a, place_b = (lax.broadcasted_iota(jnp.int32, (N_TILE, N_TILE), axis) for axis in (0, 1))
    earlier = jnp.where(sender(place_b) < sender(place_a), 1.0, 0.0)
    before_sender = jnp.dot(earlier, counts, preferred_element_type=jnp.float32)
    before_place = jnp.dot(jnp.where(place_b < place_a, 1.0, 0.0), counts, preferred_element_type=jnp.float32)
    slot = before_sender + before_b
    spot = jnp.where(mine > 0.0, before_place + before_b, -1.0)
    entry = slot * 1024.0 + ((place_r & 3) * 256 + sender_r * NB + lane).astype(jnp.float32)
    lane_f = lane.astype(jnp.float32)
    entries = jnp.zeros(wide, jnp.float32)
    for b in range(NB):
        entries = entries + jnp.where(spot[:, b : b + 1] == lane_f, entry[:, b : b + 1], 0.0)
    starts = jnp.where(place_r == 4 * lane, before_place, 0.0) + jnp.where(lane == SIDE, counts, 0.0)
    both = [jnp.sum(v, 0, keepdims=True) for v in (entries, starts)]
    plan_ref[...] = jnp.concatenate(both + [jnp.zeros((6, WIN), jnp.float32)], 0).astype(jnp.int32)

    code_cols = jnp.concatenate([codes, jnp.zeros((WIN - N_TILE, WIN), jnp.float32)], 0).T[:S]
    angles = code_cols * (2.0 * jnp.pi / 256.0)
    cosines, sines = jnp.cos(angles), jnp.sin(angles)
    for place in range(N_TILE):
        cos_ref[place] = jnp.broadcast_to(cosines[:, place : place + 1], (S, BR))
        sin_ref[place] = jnp.broadcast_to(sines[:, place : place + 1], (S, BR))


def planned(own, one, three, two):
    vmem = pl.BlockSpec(memory_space=pltpu.VMEM)
    turn = jax.ShapeDtypeStruct((N_TILE, S, BR), jnp.float32)
    return pl.pallas_call(
        plan_kernel,
        out_shape=[jax.ShapeDtypeStruct((8, WIN), jnp.int32), turn, turn],
        in_specs=[vmem] * 4,
        out_specs=[vmem] * 3,
        compiler_params=pltpu.CompilerParams(vmem_limit_bytes=8 * 2**20),
        name="planned",
    )(own, one, three, two)


def interleave(real, imag):
    pieces = []
    for d in range(N_LINE):
        pieces += [real[8 * d : 8 * d + 8], imag[8 * d : 8 * d + 8]]
    return jnp.concatenate(pieces, 0)


def image_kernel(phase, plan_ref, main_ref, cos_ref, sin_ref, table_ref, held_ref, *rest):
    first, last = phase == 0, phase == SIDE - 1
    if first:
        out_ref, slots = rest
    else:
        before_ref, out_ref, slots = rest
    start, end = plan_ref[1, phase], plan_ref[1, phase + 1]
    pairs = (end - start + 1) >> 1

    def one_slot(n):
        entry = plan_ref[0, jnp.minimum(n, MAXB - 1)]
        i, f, b = (entry >> 8) & 3, (entry >> 4) & 15, entry & 15
        window = main_ref[i, pl.ds(pl.multiple_of((b >> 1) * HALF, HALF), WIN), :]
        stacked = lax.dot_general(
            window, table_ref[2 * f + (b & 1)], (((0,), (0,)), ((), ())), preferred_element_type=jnp.float32
        )
        real = stacked[:S, :BR] - stacked[S:, BR:]
        imag = stacked[S:, :BR] + stacked[:S, BR:]
        cosine, sine = cos_ref[SIDE * phase + i], sin_ref[SIDE * phase + i]
        keep = n < end
        turned_re = jnp.where(keep, real * cosine + imag * sine, 0.0)
        turned_im = jnp.where(keep, imag * cosine - real * sine, 0.0)
        return interleave(turned_re, turned_im).astype(jnp.bfloat16), interleave(-turned_im, turned_re).astype(jnp.bfloat16)

    def make_pair(c, carry):
        for k in range(2):
            plain, crossed = one_slot(start + 2 * c + k)
            slots[c, :, k * BR : (k + 1) * BR] = plain
            slots[c, :, PAIR + k * BR : PAIR + (k + 1) * BR] = crossed
        return carry

    lax.fori_loop(0, pairs, make_pair, 0)
    total = out_ref if not last else before_ref
    if first:
        out_ref[...] = jnp.zeros_like(out_ref)
    elif not last:
        out_ref[...] = before_ref[...]

    def multiply(c, carry):
        at = []
        for k in range(2):
            slot = plan_ref[0, jnp.minimum(start + 2 * c + k, MAXB - 1)] >> 10
            at.append(pl.ds(pl.multiple_of(slot * BR, BR), BR))
        matrix = jnp.concatenate([held_ref[k, rows, :] for k in range(2) for rows in at], 0)
        total[...] += jnp.dot(slots[c], matrix, preferred_element_type=jnp.float32)
        return carry

    lax.fori_loop(0, pairs, multiply, 0)
    if last:
        for d in range(N_LINE):
            for depth in range(TZ):
                out_ref[d, depth] = total[16 * d : 16 * d + 16, TX * depth : TX * depth + TX].astype(jnp.bfloat16)


def image_part(phase, plan, main, turns, tables, held, before):
    smem, vmem = pl.BlockSpec(memory_space=pltpu.SMEM), pl.BlockSpec(memory_space=pltpu.VMEM)
    last = phase == SIDE - 1
    fixed = [pltpu.with_memory_space_constraint(v, pltpu.VMEM) for v in (main, *turns, tables, held)]
    earlier = () if before is None else (pltpu.with_memory_space_constraint(before, pltpu.VMEM),)
    shape = (N_LINE, TZ, 16, TX) if last else (2 * S, WIDE)
    return pl.pallas_call(
        functools.partial(image_kernel, phase),
        out_shape=pltpu.VMEM(shape, jnp.bfloat16 if last else jnp.float32),
        in_specs=[smem] + [vmem] * (5 + len(earlier)),
        out_specs=vmem,
        scratch_shapes=[pltpu.VMEM((MAXB // 4, 2 * S, 2 * PAIR), jnp.bfloat16)],
        input_output_aliases={} if last or before is None else {6: 0},
        compiler_params=pltpu.CompilerParams(vmem_limit_bytes=6 * 2**20),
        cost_estimate=pl.CostEstimate(flops=2 * 8 * 2 * S * 2 * BR * WIDE, bytes_accessed=2**20, transcendentals=0),
    )(plan, *fixed, *earlier)


def sum_kernel(parts_ref, out_ref, top_ref, bottom_ref):
    for depth in range(TZ):
        total = parts_ref[0, depth].astype(jnp.float32)
        for line in range(1, N_LINE):
            total = total + parts_ref[line, depth].astype(jnp.float32)
        out_ref[depth] = total
        if depth < 2:
            top_ref[depth] = total
        if depth >= TZ - 2:
            bottom_ref[depth - TZ + 2] = total


def summed_lines(parts):
    shapes = [jax.ShapeDtypeStruct((rows, 16, TX), jnp.float32) for rows in (TZ, 2, 2)]
    return pl.pallas_call(
        sum_kernel,
        out_shape=shapes,
        in_specs=[pl.BlockSpec(memory_space=pltpu.VMEM)],
        out_specs=[pl.BlockSpec(memory_space=pltpu.VMEM)] * 3,
        compiler_params=pltpu.CompilerParams(vmem_limit_bytes=8 * 2**20),
        name="summed_lines",
    )(parts)


def dip_kernel(filter_ref, above_ref, image_ref, below_ref, out_ref):
    rows = [above_ref[0], above_ref[1]] + [image_ref[d] for d in range(TZ)] + [below_ref[0], below_ref[1]]
    lane = lax.broadcasted_iota(jnp.int32, (16, TX), 1)
    results = [jnp.zeros((16, TX), jnp.float32) for _ in range(TZ)]
    for side in range(5):
        move = side - 2
        for source in range(TZ + 4):
            row = rows[source]
            if move:
                inside = (lane + move >= 0) & (lane + move < TX)
                row = jnp.where(inside, pltpu.roll(row, (-move) % TX, 1), 0.0)
            for depth in range(max(0, source - 4), min(TZ, source + 1)):
                results[depth] = results[depth] + filter_ref[source - depth, side] * row
    for depth in range(TZ):
        for part in range(2):
            out_ref[pl.ds(part * 64 + depth, 8, stride=TZ), :] = results[depth][8 * part : 8 * part + 8]


def dip_filtered(dip_filter, above, image, below):
    vmem = pl.BlockSpec(memory_space=pltpu.VMEM)
    return pl.pallas_call(
        dip_kernel,
        out_shape=jax.ShapeDtypeStruct((2 * 8 * TZ, TX), jnp.float32),
        in_specs=[pl.BlockSpec(memory_space=pltpu.SMEM), vmem, vmem, vmem],
        out_specs=vmem,
        compiler_params=pltpu.CompilerParams(vmem_limit_bytes=8 * 2**20),
        name="dip_filtered",
    )(dip_filter, above, image, below)


def spread(value, x_first):
    return [lax.ppermute(value, BOTH, hops(offset, x_first)) for offset in RING[1:]]


def per_device(traces, codes, routes, beam_matrix, dip_filter):
    local = traces[0]
    rim = lax.ppermute(local[:HALF], "line", [(i + 1, i) for i in range(N_LINE - 1)])
    routes_row = jnp.pad(routes.astype(jnp.bfloat16), ((0, 0), (0, WIN - NB)))
    codes_row = jnp.pad(codes.astype(jnp.bfloat16), ((0, 0), (0, WIN - S)))
    aux = jnp.concatenate([routes_row, codes_row, jnp.zeros((14, WIN), jnp.bfloat16)], 0)
    near_aux = jnp.stack([aux] + spread(aux, False))
    main = jnp.concatenate([local, rim], 0)
    near_main = jnp.stack([main] + spread(main, False))
    all_aux = [near_aux] + spread(near_aux, True)
    mains = [near_main] + spread(near_main, True)
    tables, held = prepared(beam_matrix)
    plan, *turns = planned(*all_aux)
    image = None
    for phase in range(SIDE):
        image = image_part(phase, plan, mains[phase], turns, tables, held, image)
    parts = lax.all_to_all(image, "line", 0, 0, tiled=True)
    image, top, bottom = summed_lines(parts)
    above = lax.ppermute(bottom, "tile", [(i, i + 1) for i in range(N_TILE - 1)])
    below = lax.ppermute(top, "tile", [(i + 1, i) for i in range(N_TILE - 1)])
    return dip_filtered(dip_filter, above, image, below).reshape(2, 8, TZ, TX)


def solution(mesh):
    in_specs = (
        P("tile", "line", None),
        P("tile", None),
        P("line", "tile"),
        P("line", "tile", None, None, None),
        P(),
    )
    out_specs = P(None, "line", "tile", None)

    return jax.shard_map(per_device, mesh=mesh, in_specs=in_specs, out_specs=out_specs, check_vma=False)
```

time: 70.8 us -> 79.2 us (1.12)
  the two profiles are of different devices: /device:TPU:96 before, /device:TPU:34 now
where the time goes in v2:
time: 79.2 us; the launch traced here: 79 us
  starting transfers between devices  28.5 us (36%)
  blocking collectives  16 us (20%)
  Pallas kernels  15.8 us (20%)
  waiting for transfers between devices  15.2 us (19%)
  other arithmetic  2.49 us (3%)
  local copies, waits for them, and re-layouts  0.81 us (1%)
    ppermute x12, starting transfers between devices, spread(): lax.ppermute(value, BOTH, hops(offset, x_first))  17.1 us
    all_to_all x1, blocking collectives, per_device(): parts = lax.all_to_all(image, 'line', 0, 0, tiled=True)  16 us
    ppermute x12, waiting for transfers between devices, spread(): lax.ppermute(value, BOTH, hops(offset, x_first))  9.77 us
    ppermute x1, starting transfers between devices, per_device(): lax.ppermute(bottom, 'tile', [(i, i + 1) for i in range(N_TILE - 1)])  8.17 us
    pallas_call x4, Pallas kernels, image_part(): pl.pallas_call(functools.partial(image_kernel, phase), out_shape=pltpu.VM...  7.76 us
    pallas_call x1, Pallas kernels, prepared(): pl.pallas_call(prepare_kernel, out_shape=[pltpu.VMEM((2 * N_TILE, WIN, 2...  5.93 us
    ppermute x1, waiting for transfers between devices, per_device(): below = lax.ppermute(top, 'tile', [(i + 1, i) for i in range(N_TILE - 1)])  3.69 us
    ppermute x1, starting transfers between devices, per_device(): below = lax.ppermute(top, 'tile', [(i + 1, i) for i in range(N_TILE - 1)])  1.92 us
  transfers between devices with their start and end apart: 15, of which 7 were waited for; matrix products, arithmetic and copies ran while one was open for 2% of the time, Pallas kernels for 16%

profile of v2, /device:TPU:34, one launch (start us, length us, event | category | flops | bytes accessed | tf_op | source)
XLA Modules:
  0.0 79.0 jit_solution(3210520192311673165)
XLA Ops:
  0.7 1.3 %collective-permute-start.6 = (bf16[64,128]{1,0:T(8,128)(2,1)S(1)}, bf16[64,128]{1,0:T(8,128)(2,1)S(1)}, u32[]{:S(2)}, u32[]{:S(2)}) collective-permute-start(bf16[64,128]{1,0:T(8,128)(2,1)S(1)} %slice_bitcast_fusion), channel_id=1, source_target_pairs={{16,0},{32,16},{48,32},{64,48},{80,64},{96,80},{112,96},{17,1},{33... | collective-permute-start | bytes 49160 | tf_op jit(solution)/shard_map/ppermute | solution.py:287
  2.0 1.8 %collective-permute-done.6 = bf16[64,128]{1,0:T(8,128)(2,1)S(1)} collective-permute-done((bf16[64,128]{1,0:T(8,128)(2,1)S(1)}, bf16[64,128]{1,0:T(8,128)(2,1)S(1)}, u32[]{:S(2)}, u32[]{:S(2)}) %collective-permute-start.6) | collective-permute-done | bytes 16416 | tf_op jit(solution)/shard_map/ppermute | solution.py:287
  4.7 2.0 %collective-permute-start.7 = (bf16[576,128]{1,0:T(8,128)(2,1)S(1)}, bf16[576,128]{1,0:T(8,128)(2,1)S(1)}, u32[]{:S(2)}, u32[]{:S(2)}) collective-permute-start(bf16[576,128]{1,0:T(8,128)(2,1)S(1)} %get-tuple-element.22), channel_id=1, source_target_pairs={{0,1},{1,2},{2,3},{3,0},{4,5},{5,6},{6,7},{7,4},{8,9},{9,10},{10,1... | collective-permute-start | bytes 442376 | tf_op jit(solution)/shard_map/ppermute | solution.py:282
  6.8 3.0 %collective-permute-start.9 = (bf16[576,128]{1,0:T(8,128)(2,1)S(1)}, bf16[576,128]{1,0:T(8,128)(2,1)S(1)}, u32[]{:S(2)}, u32[]{:S(2)}) collective-permute-start(bf16[576,128]{1,0:T(8,128)(2,1)S(1)} %get-tuple-element.22), channel_id=1, source_target_pairs={{0,2},{1,3},{2,0},{3,1},{4,6},{5,7},{6,4},{7,5},{8,10},{9,11},{10,... | collective-permute-start | bytes 442376 | tf_op jit(solution)/shard_map/ppermute | solution.py:282
  11.9 2.6 %collective-permute-done.9 = bf16[576,128]{1,0:T(8,128)(2,1)S(1)} collective-permute-done((bf16[576,128]{1,0:T(8,128)(2,1)S(1)}, bf16[576,128]{1,0:T(8,128)(2,1)S(1)}, u32[]{:S(2)}, u32[]{:S(2)}) %collective-permute-start.9) | collective-permute-done | bytes 147488 | tf_op jit(solution)/shard_map/ppermute | solution.py:282
  14.6 1.6 %collective-permute-start.12 = (bf16[4,576,128]{2,1,0:T(8,128)(2,1)S(1)}, bf16[4,576,128]{2,1,0:T(8,128)(2,1)S(1)}, u32[]{:S(2)}, u32[]{:S(2)}) collective-permute-start(bf16[4,576,128]{2,1,0:T(8,128)(2,1)S(1)} %pad_maximum_fusion.main_ref), channel_id=1, source_target_pairs={{0,4},{1,5},{2,6},{3,7},{4,8},{5,9},{6,10},{7,11},{8,12},{9,13},{1... | collective-permute-start | bytes 1769480 | tf_op jit(solution)/shard_map/ppermute | solution.py:282
  16.7 2.1 %collective-permute-start.10 = (bf16[4,576,128]{2,1,0:T(8,128)(2,1)S(1)}, bf16[4,576,128]{2,1,0:T(8,128)(2,1)S(1)}, u32[]{:S(2)}, u32[]{:S(2)}) collective-permute-start(bf16[4,576,128]{2,1,0:T(8,128)(2,1)S(1)} %pad_maximum_fusion.main_ref), channel_id=1, source_target_pairs={{0,8},{1,9},{2,10},{3,11},{4,12},{5,13},{6,14},{7,15},{8,0},{9,1},... | collective-permute-start | bytes 1769480 | tf_op jit(solution)/shard_map/ppermute | solution.py:282
  19.8 1.1 %collective-permute-start.1 = (bf16[16,128]{1,0:T(8,128)(2,1)S(1)}, bf16[16,128]{1,0:T(8,128)(2,1)S(1)}, u32[]{:S(2)}, u32[]{:S(2)}) collective-permute-start(bf16[16,128]{1,0:T(8,128)(2,1)S(1)} %fusion.4), channel_id=1, source_target_pairs={{0,3},{1,0},{2,1},{3,2},{4,7},{5,4},{6,5},{7,6},{8,11},{9,8},{10,9... | collective-permute-start | bytes 12296 | tf_op jit(solution)/shard_map/ppermute | solution.py:282
  20.9 1.6 %collective-permute-done = bf16[16,128]{1,0:T(8,128)(2,1)S(1)} collective-permute-done((bf16[16,128]{1,0:T(8,128)(2,1)S(1)}, bf16[16,128]{1,0:T(8,128)(2,1)S(1)}, u32[]{:S(2)}, u32[]{:S(2)}) %collective-permute-start) | collective-permute-done | bytes 4128 | tf_op jit(solution)/shard_map/ppermute | solution.py:282
  22.5 2.0 %collective-permute-start.2 = (bf16[16,128]{1,0:T(8,128)(2,1)S(1)}, bf16[16,128]{1,0:T(8,128)(2,1)S(1)}, u32[]{:S(2)}, u32[]{:S(2)}) collective-permute-start(bf16[16,128]{1,0:T(8,128)(2,1)S(1)} %fusion.4), channel_id=1, source_target_pairs={{0,2},{1,3},{2,0},{3,1},{4,6},{5,7},{6,4},{7,5},{8,10},{9,11},{10,... | collective-permute-start | bytes 12296 | tf_op jit(solution)/shard_map/ppermute | solution.py:282
  24.6 3.1 %collective-permute-done.2 = bf16[16,128]{1,0:T(8,128)(2,1)S(1)} collective-permute-done((bf16[16,128]{1,0:T(8,128)(2,1)S(1)}, bf16[16,128]{1,0:T(8,128)(2,1)S(1)}, u32[]{:S(2)}, u32[]{:S(2)}) %collective-permute-start.2) | collective-permute-done | bytes 4128 | tf_op jit(solution)/shard_map/ppermute | solution.py:282
  27.7 1.1 %collective-permute-start.3 = (bf16[4,16,128]{2,1,0:T(8,128)(2,1)S(1)}, bf16[4,16,128]{2,1,0:T(8,128)(2,1)S(1)}, u32[]{:S(2)}, u32[]{:S(2)}) collective-permute-start(bf16[4,16,128]{2,1,0:T(8,128)(2,1)S(1)} %pad_maximum_fusion.2.own_ref), channel_id=1, source_target_pairs={{0,4},{1,5},{2,6},{3,7},{4,8},{5,9},{6,10},{7,11},{8,12},{9,13},{1... | collective-permute-start | bytes 49160 | tf_op jit(solution)/shard_map/ppermute | solution.py:282
  29.7 1.7 %collective-permute-done.3.one_ref = bf16[4,16,128]{2,1,0:T(8,128)(2,1)S(1)} collective-permute-done((bf16[4,16,128]{2,1,0:T(8,128)(2,1)S(1)}, bf16[4,16,128]{2,1,0:T(8,128)(2,1)S(1)}, u32[]{:S(2)}, u32[]{:S(2)}) %collective-permute-start.3) | collective-permute-done | bytes 16416 | tf_op jit(solution)/shard_map/ppermute | solution.py:282
  31.4 1.8 %collective-permute-start.5 = (bf16[4,16,128]{2,1,0:T(8,128)(2,1)S(1)}, bf16[4,16,128]{2,1,0:T(8,128)(2,1)S(1)}, u32[]{:S(2)}, u32[]{:S(2)}) collective-permute-start(bf16[4,16,128]{2,1,0:T(8,128)(2,1)S(1)} %pad_maximum_fusion.2.own_ref), channel_id=1, source_target_pairs={{0,8},{1,9},{2,10},{3,11},{4,12},{5,13},{6,14},{7,15},{8,0},{9,1},... | collective-permute-start | bytes 49160 | tf_op jit(solution)/shard_map/ppermute | solution.py:282
  33.2 5.9 %prepared.1 = (bf16[32,128,256]{2,1,0:T(8,128)(2,1)S(1)}, bf16[2,4096,1024]{2,1,0:T(8,128)(2,1)S(1)}) custom-call(bf16[1,1,2,4096,1024]{4,3,2,1,0:T(8,128)(2,1)} %matrix_ref.1), custom_call_target="tpu_custom_call" | custom-call | tf_op jit(solution)/shard_map/prepared/pallas_call | solution.py:75
  39.8 2.4 %shard_map.55.rest_0_ = f32[128,1024]{1,0:T(8,128)S(1)} custom-call(s32[8,128]{1,0:T(8,128)S(1)} %get-tuple-element.13.plan_ref, bf16[4,576,128]{2,1,0:T(8,128)(2,1)S(1)} %pad_maximum_fusion.main_ref, f32[16,64,128]{2,1,0:T(8,128)S(1)} %get-tuple-element.14.cos_ref, f32[16,64,128]{2,1,0:T(8,128)S(1)} %get-tuple-element.15.sin_ref, ...), custom_call_target="tpu_custom_call" | custom-call | flops 536870912 | bytes 1048576 | tf_op jit(solution)/shard_map/pallas_call | solution.py:215
  42.2 1.8 %shard_map.56.rest_0_ = f32[128,1024]{1,0:T(8,128)S(1)} custom-call(s32[8,128]{1,0:T(8,128)S(1)} %get-tuple-element.13.plan_ref, bf16[4,576,128]{2,1,0:T(8,128)(2,1)S(1)} %collective-permute-done.12.main_ref, f32[16,64,128]{2,1,0:T(8,128)S(1)} %get-tuple-element.14.cos_ref, ...), custom_call_target="tpu_custom_call", output_to_operand_aliasing={{}: (6, {})} | custom-call | flops 536870912 | bytes 1048576 | tf_op jit(solution)/shard_map/pallas_call | solution.py:215
  44.0 1.8 %shard_map.57.rest_0_ = f32[128,1024]{1,0:T(8,128)S(1)} custom-call(s32[8,128]{1,0:T(8,128)S(1)} %get-tuple-element.13.plan_ref, bf16[4,576,128]{2,1,0:T(8,128)(2,1)S(1)} %collective-permute-done.11.main_ref, f32[16,64,128]{2,1,0:T(8,128)S(1)} %get-tuple-element.14.cos_ref, ...), custom_call_target="tpu_custom_call", output_to_operand_aliasing={{}: (6, {})} | custom-call | flops 536870912 | bytes 1048576 | tf_op jit(solution)/shard_map/pallas_call | solution.py:215
  45.9 1.8 %shard_map.58 = bf16[8,8,16,128]{3,2,1,0:T(8,128)(2,1)S(1)} custom-call(s32[8,128]{1,0:T(8,128)S(1)} %get-tuple-element.13.plan_ref, bf16[4,576,128]{2,1,0:T(8,128)(2,1)S(1)} %collective-permute-done.10.main_ref, f32[16,64,128]{2,1,0:T(8,128)S(1)} %get-tuple-element.14.cos_ref, f32[16,64,128]{2,1,0:T(8,128)S(1)} %get-tuple-element.15.sin_ref, ...), custom_call_target="tpu_custom_call" | custom-call | flops 536870912 | bytes 1048576 | tf_op jit(solution)/shard_map/pallas_call | solution.py:215
  47.7 16.0 %all_to_all.5.parts_ref = bf16[8,8,16,128]{3,2,1,0:T(8,128)(2,1)S(1)} all-to-all(bf16[8,8,16,128]{3,2,1,0:T(8,128)(2,1)S(1)} %shard_map.58), channel_id=1, replica_groups=mesh['line'=8,'tile'=16] {'line'}, dimensions={0} | all-to-all | bytes 524288 | tf_op jit(solution)/shard_map/all_to_all | solution.py:301
  63.7 8.2 %collective-permute-start.13 = (f32[2,16,128]{2,1,0:T(8,128)S(1)}, f32[2,16,128]{2,1,0:T(8,128)S(1)}, u32[]{:S(2)}, u32[]{:S(2)}) collective-permute-start(f32[2,16,128]{2,1,0:T(8,128)S(1)} %get-tuple-element.18), channel_id=1, source_target_pairs={{0,1},{1,2},{2,3},{3,4},{4,5},{5,6},{6,7},{7,8},{8,9},{9,10},{10,1... | collective-permute-start | bytes 49160 | tf_op jit(solution)/shard_map/ppermute | solution.py:303
  71.9 1.9 %collective-permute-start.14 = (f32[2,16,128]{2,1,0:T(8,128)S(1)}, f32[2,16,128]{2,1,0:T(8,128)S(1)}, u32[]{:S(2)}, u32[]{:S(2)}) collective-permute-start(f32[2,16,128]{2,1,0:T(8,128)S(1)} %get-tuple-element.20), channel_id=1, source_target_pairs={{1,0},{2,1},{3,2},{4,3},{5,4},{6,5},{7,6},{8,7},{9,8},{10,9},{11,1... | collective-permute-start | bytes 49160 | tf_op jit(solution)/shard_map/ppermute | solution.py:304
  73.8 3.7 %collective-permute-done.14.below_ref = f32[2,16,128]{2,1,0:T(8,128)S(1)} collective-permute-done((f32[2,16,128]{2,1,0:T(8,128)S(1)}, f32[2,16,128]{2,1,0:T(8,128)S(1)}, u32[]{:S(2)}, u32[]{:S(2)}) %collective-permute-start.14) | collective-permute-done | bytes 16416 | tf_op jit(solution)/shard_map/ppermute | solution.py:304
  77.5 1.4 %dip_filtered.1 = f32[128,128]{1,0:T(8,128)} custom-call(f32[5,5]{1,0:T(8,128)S(1)} %copy-done, f32[2,16,128]{2,1,0:T(8,128)S(1)} %collective-permute-done.13.above_ref, f32[8,16,128]{2,1,0:T(8,128)S(1)} %get-tuple-element.19.image_ref, f32[2,16,128]{2,1,0:T(8,128)S(1)} %collective-permute-done.14.below_ref), custom_call_target="tpu_custom_call" | custom-call | tf_op jit(solution)/shard_map/dip_filtered/pallas_call | solution.py:271
  (27 shorter events, 7.1 us)
Async XLA Ops:
  0.7 3.1 %collective-permute-start.6 = (bf16[64,128]{1,0:T(8,128)(2,1)S(1)}, bf16[64,128]{1,0:T(8,128)(2,1)S(1)}, u32[]{:S(2)}, u32[]{:S(2)}) collective-permute-start(bf16[64,128]{1,0:T(8,128)(2,1)S(1)} %slice_bitcast_fusion), channel_id=1, source_target_pairs={{16,0},{32,16},{48,32},{64,48},{80,64},{96,80},{112,96},{17,1},{33... | collective-permute-start | bytes 49160 | tf_op jit(solution)/shard_map/ppermute | solution.py:287
  4.7 6.5 %collective-permute-start.7 = (bf16[576,128]{1,0:T(8,128)(2,1)S(1)}, bf16[576,128]{1,0:T(8,128)(2,1)S(1)}, u32[]{:S(2)}, u32[]{:S(2)}) collective-permute-start(bf16[576,128]{1,0:T(8,128)(2,1)S(1)} %get-tuple-element.22), channel_id=1, source_target_pairs={{0,1},{1,2},{2,3},{3,0},{4,5},{5,6},{6,7},{7,4},{8,9},{9,10},{10,1... | collective-permute-start | bytes 442376 | tf_op jit(solution)/shard_map/ppermute | solution.py:282
  6.7 5.1 %collective-permute-start.8 = (bf16[576,128]{1,0:T(8,128)(2,1)S(1)}, bf16[576,128]{1,0:T(8,128)(2,1)S(1)}, u32[]{:S(2)}, u32[]{:S(2)}) collective-permute-start(bf16[576,128]{1,0:T(8,128)(2,1)S(1)} %get-tuple-element.22), channel_id=1, source_target_pairs={{0,3},{1,0},{2,1},{3,2},{4,7},{5,4},{6,5},{7,6},{8,11},{9,8},{10,9... | collective-permute-start | bytes 442376 | tf_op jit(solution)/shard_map/ppermute | solution.py:282
  6.8 7.7 %collective-permute-start.9 = (bf16[576,128]{1,0:T(8,128)(2,1)S(1)}, bf16[576,128]{1,0:T(8,128)(2,1)S(1)}, u32[]{:S(2)}, u32[]{:S(2)}) collective-permute-start(bf16[576,128]{1,0:T(8,128)(2,1)S(1)} %get-tuple-element.22), channel_id=1, source_target_pairs={{0,2},{1,3},{2,0},{3,1},{4,6},{5,7},{6,4},{7,5},{8,10},{9,11},{10,... | collective-permute-start | bytes 442376 | tf_op jit(solution)/shard_map/ppermute | solution.py:282
  14.6 27.6 %collective-permute-start.12 = (bf16[4,576,128]{2,1,0:T(8,128)(2,1)S(1)}, bf16[4,576,128]{2,1,0:T(8,128)(2,1)S(1)}, u32[]{:S(2)}, u32[]{:S(2)}) collective-permute-start(bf16[4,576,128]{2,1,0:T(8,128)(2,1)S(1)} %pad_maximum_fusion.main_ref), channel_id=1, source_target_pairs={{0,4},{1,5},{2,6},{3,7},{4,8},{5,9},{6,10},{7,11},{8,12},{9,13},{1... | collective-permute-start | bytes 1769480 | tf_op jit(solution)/shard_map/ppermute | solution.py:282
  16.1 27.9 %collective-permute-start.11 = (bf16[4,576,128]{2,1,0:T(8,128)(2,1)S(1)}, bf16[4,576,128]{2,1,0:T(8,128)(2,1)S(1)}, u32[]{:S(2)}, u32[]{:S(2)}) collective-permute-start(bf16[4,576,128]{2,1,0:T(8,128)(2,1)S(1)} %pad_maximum_fusion.main_ref), channel_id=1, source_target_pairs={{0,12},{1,13},{2,14},{3,15},{4,0},{5,1},{6,2},{7,3},{8,4},{9,5},{1... | collective-permute-start | bytes 1769480 | tf_op jit(solution)/shard_map/ppermute | solution.py:282
  16.7 29.2 %collective-permute-start.10 = (bf16[4,576,128]{2,1,0:T(8,128)(2,1)S(1)}, bf16[4,576,128]{2,1,0:T(8,128)(2,1)S(1)}, u32[]{:S(2)}, u32[]{:S(2)}) collective-permute-start(bf16[4,576,128]{2,1,0:T(8,128)(2,1)S(1)} %pad_maximum_fusion.main_ref), channel_id=1, source_target_pairs={{0,8},{1,9},{2,10},{3,11},{4,12},{5,13},{6,14},{7,15},{8,0},{9,1},... | collective-permute-start | bytes 1769480 | tf_op jit(solution)/shard_map/ppermute | solution.py:282
  18.9 3.7 %collective-permute-start = (bf16[16,128]{1,0:T(8,128)(2,1)S(1)}, bf16[16,128]{1,0:T(8,128)(2,1)S(1)}, u32[]{:S(2)}, u32[]{:S(2)}) collective-permute-start(bf16[16,128]{1,0:T(8,128)(2,1)S(1)} %fusion.4), channel_id=1, source_target_pairs={{0,1},{1,2},{2,3},{3,0},{4,5},{5,6},{6,7},{7,4},{8,9},{9,10},{10,1... | collective-permute-start | bytes 12296 | tf_op jit(solution)/shard_map/ppermute | solution.py:282
  19.8 4.8 %collective-permute-start.1 = (bf16[16,128]{1,0:T(8,128)(2,1)S(1)}, bf16[16,128]{1,0:T(8,128)(2,1)S(1)}, u32[]{:S(2)}, u32[]{:S(2)}) collective-permute-start(bf16[16,128]{1,0:T(8,128)(2,1)S(1)} %fusion.4), channel_id=1, source_target_pairs={{0,3},{1,0},{2,1},{3,2},{4,7},{5,4},{6,5},{7,6},{8,11},{9,8},{10,9... | collective-permute-start | bytes 12296 | tf_op jit(solution)/shard_map/ppermute | solution.py:282
  22.5 5.2 %collective-permute-start.2 = (bf16[16,128]{1,0:T(8,128)(2,1)S(1)}, bf16[16,128]{1,0:T(8,128)(2,1)S(1)}, u32[]{:S(2)}, u32[]{:S(2)}) collective-permute-start(bf16[16,128]{1,0:T(8,128)(2,1)S(1)} %fusion.4), channel_id=1, source_target_pairs={{0,2},{1,3},{2,0},{3,1},{4,6},{5,7},{6,4},{7,5},{8,10},{9,11},{10,... | collective-permute-start | bytes 12296 | tf_op jit(solution)/shard_map/ppermute | solution.py:282
  27.7 3.7 %collective-permute-start.3 = (bf16[4,16,128]{2,1,0:T(8,128)(2,1)S(1)}, bf16[4,16,128]{2,1,0:T(8,128)(2,1)S(1)}, u32[]{:S(2)}, u32[]{:S(2)}) collective-permute-start(bf16[4,16,128]{2,1,0:T(8,128)(2,1)S(1)} %pad_maximum_fusion.2.own_ref), channel_id=1, source_target_pairs={{0,4},{1,5},{2,6},{3,7},{4,8},{5,9},{6,10},{7,11},{8,12},{9,13},{1... | collective-permute-start | bytes 49160 | tf_op jit(solution)/shard_map/ppermute | solution.py:282
  28.8 10.4 %collective-permute-start.4 = (bf16[4,16,128]{2,1,0:T(8,128)(2,1)S(1)}, bf16[4,16,128]{2,1,0:T(8,128)(2,1)S(1)}, u32[]{:S(2)}, u32[]{:S(2)}) collective-permute-start(bf16[4,16,128]{2,1,0:T(8,128)(2,1)S(1)} %pad_maximum_fusion.2.own_ref), channel_id=1, source_target_pairs={{0,12},{1,13},{2,14},{3,15},{4,0},{5,1},{6,2},{7,3},{8,4},{9,5},{1... | collective-permute-start | bytes 49160 | tf_op jit(solution)/shard_map/ppermute | solution.py:282
  31.4 7.8 %collective-permute-start.5 = (bf16[4,16,128]{2,1,0:T(8,128)(2,1)S(1)}, bf16[4,16,128]{2,1,0:T(8,128)(2,1)S(1)}, u32[]{:S(2)}, u32[]{:S(2)}) collective-permute-start(bf16[4,16,128]{2,1,0:T(8,128)(2,1)S(1)} %pad_maximum_fusion.2.own_ref), channel_id=1, source_target_pairs={{0,8},{1,9},{2,10},{3,11},{4,12},{5,13},{6,14},{7,15},{8,0},{9,1},... | collective-permute-start | bytes 49160 | tf_op jit(solution)/shard_map/ppermute | solution.py:282
  44.0 33.5 %copy-start = (f32[5,5]{1,0:T(8,128)S(1)}, f32[5,5]{1,0:T(8,128)}, u32[]{:S(2)}) copy-start(f32[5,5]{1,0:T(8,128)} %filter_ref.1) | copy-start | bytes 304
  63.7 10.1 %collective-permute-start.13 = (f32[2,16,128]{2,1,0:T(8,128)S(1)}, f32[2,16,128]{2,1,0:T(8,128)S(1)}, u32[]{:S(2)}, u32[]{:S(2)}) collective-permute-start(f32[2,16,128]{2,1,0:T(8,128)S(1)} %get-tuple-element.18), channel_id=1, source_target_pairs={{0,1},{1,2},{2,3},{3,4},{4,5},{5,6},{6,7},{7,8},{8,9},{9,10},{10,1... | collective-permute-start | bytes 49160 | tf_op jit(solution)/shard_map/ppermute | solution.py:303
  71.9 5.6 %collective-permute-start.14 = (f32[2,16,128]{2,1,0:T(8,128)S(1)}, f32[2,16,128]{2,1,0:T(8,128)S(1)}, u32[]{:S(2)}, u32[]{:S(2)}) collective-permute-start(f32[2,16,128]{2,1,0:T(8,128)S(1)} %get-tuple-element.20), channel_id=1, source_target_pairs={{1,0},{2,1},{3,2},{4,3},{5,4},{6,5},{7,6},{8,7},{9,8},{10,9},{11,1... | collective-permute-start | bytes 49160 | tf_op jit(solution)/shard_map/ppermute | solution.py:304

commit v3 on v2

v3 whole, which is shorter than its diff:
```python
import jax
import jax.numpy as jnp
from jax import lax
from jax.experimental import pallas as pl
from jax.experimental.pallas import tpu as pltpu
from jax.sharding import PartitionSpec as P


S = 64
P_SIZE = 256
WIN = 128
BR = 128
TZ = 8
TX = 128
MAXB = 32
NB = 16
HALF = WIN // 2
LOCAL = 512
ROWS = LOCAL + 16
SIDE = 4
RING = (0, 1, 3, 2)
BOTH = ("line", "tile")
N_LINE = 8
N_TILE = 16
QUAD = 4
STREAMS = 16
WIDE = TZ * TX


def hops(offset, x_first):
    pairs = []
    for line in range(N_LINE):
        along_x = x_first == (line % 2 == 0)
        for x in range(SIDE):
            for z in range(SIDE):
                to_x, to_z = ((x + offset) % SIDE, z) if along_x else (x, (z + offset) % SIDE)
                pairs.append((line * N_TILE + x * SIDE + z, line * N_TILE + to_x * SIDE + to_z))
    return pairs


def first_kernel(traces_ref, routes_ref, codes_ref, main_ref, rows, routes_v, codes_v, sems):
    copies = (
        pltpu.make_async_copy(traces_ref.at[0], main_ref.at[pl.ds(0, LOCAL)], sems.at[0]),
        pltpu.make_async_copy(routes_ref, routes_v, sems.at[1]),
        pltpu.make_async_copy(codes_ref, codes_v, sems.at[2]),
    )
    for copy in copies:
        copy.start()
    rows[...] = jnp.zeros_like(rows)
    for copy in copies:
        copy.wait()
    rows[0:1, :NB] = routes_v[...].astype(jnp.float32)
    rows[1:2, :S] = codes_v[...].astype(jnp.float32)
    main_ref[LOCAL:] = rows[...].astype(jnp.bfloat16)


def first_rows(traces, routes, codes):
    return pl.pallas_call(
        first_kernel,
        out_shape=pltpu.VMEM((ROWS, WIN), jnp.bfloat16),
        in_specs=[pl.BlockSpec(memory_space=pltpu.HBM)] * 3,
        out_specs=pl.BlockSpec(memory_space=pltpu.VMEM),
        scratch_shapes=[
            pltpu.VMEM((16, WIN), jnp.float32),
            pltpu.VMEM((1, NB), jnp.int32),
            pltpu.VMEM((1, S), jnp.int32),
            pltpu.SemaphoreType.DMA((3,)),
        ],
        compiler_params=pltpu.CompilerParams(vmem_limit_bytes=2 * 2**20),
        name="first_rows",
    )(*(pltpu.with_memory_space_constraint(v, pltpu.HBM) for v in (traces, routes, codes)))


def table_kernel(table_ref):
    rows = lax.broadcasted_iota(jnp.int32, (WIN, P_SIZE), 0)
    cols = lax.broadcasted_iota(jnp.int32, (WIN, P_SIZE), 1)
    turns = (cols - P_SIZE // 2) * (2 * rows - (WIN - 1))
    unit = 2.0 * jnp.pi / 8192.0
    step = (((turns + 4096) & 8191) - 4096).astype(jnp.float32) * unit
    base = (((32 * turns + 4096) & 8191) - 4096).astype(jnp.float32) * unit
    offsets = lax.broadcasted_iota(jnp.int32, (WIN, 1), 0).astype(jnp.float32) - (WIN - 1) / 2
    taper = jnp.exp(-0.5 * (offsets / (0.4 * WIN)) ** 2)
    taper = taper / jnp.sqrt(jnp.sum(taper * taper, axis=0, keepdims=True))
    step_c, step_s = jnp.cos(step), jnp.sin(step)
    now_c, now_s = taper * jnp.cos(base), -taper * jnp.sin(base)
    for f in range(N_TILE):
        for q in range(2):
            half = slice(q * BR, (q + 1) * BR)
            table_ref[2 * f + q, :, :BR] = now_c[:, half].astype(jnp.bfloat16)
            table_ref[2 * f + q, :, BR:] = now_s[:, half].astype(jnp.bfloat16)
        now_c, now_s = now_c * step_c + now_s * step_s, now_s * step_c - now_c * step_s


def slant_tables():
    return pl.pallas_call(
        table_kernel,
        out_shape=pltpu.VMEM((2 * N_TILE, WIN, 2 * BR), jnp.bfloat16),
        out_specs=pl.BlockSpec(memory_space=pltpu.VMEM),
        compiler_params=pltpu.CompilerParams(vmem_limit_bytes=4 * 2**20),
        name="slant_tables",
    )()


def hold_kernel(matrix_ref, held_ref, sems):
    copies = []
    for part in range(2):
        for piece in range(STREAMS // 2):
            rows = pl.ds(piece * (2 * MAXB * BR // STREAMS), 2 * MAXB * BR // STREAMS)
            source, target = matrix_ref.at[0, 0, part, rows, :], held_ref.at[part, rows, :]
            copies.append(pltpu.make_async_copy(source, target, sems.at[len(copies)]))
    for copy in copies:
        copy.start()
    for copy in copies:
        copy.wait()


def held_matrices(beam_matrix):
    return pl.pallas_call(
        hold_kernel,
        out_shape=pltpu.VMEM((2, MAXB * BR, WIDE), jnp.bfloat16),
        in_specs=[pl.BlockSpec(memory_space=pltpu.HBM)],
        out_specs=pl.BlockSpec(memory_space=pltpu.VMEM),
        scratch_shapes=[pltpu.SemaphoreType.DMA((STREAMS,))],
        compiler_params=pltpu.CompilerParams(vmem_limit_bytes=2 * 2**20),
        name="held_matrices",
    )(pltpu.with_memory_space_constraint(beam_matrix, pltpu.HBM))


def offset_of(place):
    return jnp.where(place == 3, 2, jnp.where(place == 2, 3, place))


def plan_kernel(own_ref, one_ref, three_ref, two_ref, plan_ref, cos_ref, sin_ref):
    tile = lax.axis_index("tile")
    x, z, parity = tile >> 2, tile & 3, lax.axis_index("line") & 1
    rows = [ref[i, LOCAL : LOCAL + 8, :].astype(jnp.float32) for ref in (own_ref, one_ref, three_ref, two_ref) for i in range(SIDE)]
    routes, codes = (jnp.concatenate([row[k : k + 1] for row in rows], 0) for k in range(2))

    def sender(place):
        far, near = offset_of(place >> 2), offset_of(place & 3)
        dx, dz = jnp.where(parity == 0, far, near), jnp.where(parity == 0, near, far)
        return (((x - dx) & 3) << 2) + ((z - dz) & 3)

    wide = (N_TILE, WIN)
    place_r, lane = lax.broadcasted_iota(jnp.int32, wide, 0), lax.broadcasted_iota(jnp.int32, wide, 1)
    sender_r = sender(place_r)
    mine = jnp.where((lane < NB) & (routes == tile.astype(jnp.float32)), 1.0, 0.0)
    lane_r, lane_c = (lax.broadcasted_iota(jnp.int32, (WIN, WIN), axis) for axis in (0, 1))
    before_b = jnp.dot(mine, jnp.where(lane_r < lane_c, 1.0, 0.0), preferred_element_type=jnp.float32)
    counts = jnp.dot(mine, jnp.ones((WIN, WIN), jnp.float32), preferred_element_type=jnp.float32)
    place_a, place_b = (lax.broadcasted_iota(jnp.int32, (N_TILE, N_TILE), axis) for axis in (0, 1))
    earlier = jnp.where(sender(place_b) < sender(place_a), 1.0, 0.0)
    before_sender = jnp.dot(earlier, counts, preferred_element_type=jnp.float32)
    before_place = jnp.dot(jnp.where(place_b < place_a, 1.0, 0.0), counts, preferred_element_type=jnp.float32)
    slot, spot = before_sender + before_b, before_place + before_b
    spot = jnp.where(mine > 0.0, spot, -1.0)
    entry = slot * 4096.0 + (place_r * 256 + sender_r * NB + lane).astype(jnp.float32)
    lane_f = lane.astype(jnp.float32)
    entries = jnp.zeros(wide, jnp.float32)
    for b in range(NB):
        entries = entries + jnp.where(spot[:, b : b + 1] == lane_f, entry[:, b : b + 1], 0.0)
    starts = jnp.where(place_r == SIDE * lane, before_place, 0.0) + jnp.where(lane == SIDE, counts, 0.0)
    starts = jnp.sum(starts, 0, keepdims=True)
    entries = jnp.sum(entries, 0, keepdims=True)
    plan_ref[...] = jnp.concatenate([entries, starts, jnp.zeros((6, WIN), jnp.float32)], 0).astype(jnp.int32)

    code_cols = jnp.concatenate([codes, jnp.zeros((WIN - N_TILE, WIN), jnp.float32)], 0).T[:S]
    angles = code_cols * (2.0 * jnp.pi / 256.0)
    cosines, sines = jnp.cos(angles), jnp.sin(angles)
    for place in range(N_TILE):
        cos_ref[place] = jnp.broadcast_to(cosines[:, place : place + 1], (S, BR))
        sin_ref[place] = jnp.broadcast_to(sines[:, place : place + 1], (S, BR))


def planned(*mains):
    vmem = pl.BlockSpec(memory_space=pltpu.VMEM)
    turn = jax.ShapeDtypeStruct((N_TILE, S, BR), jnp.float32)
    return pl.pallas_call(
        plan_kernel,
        out_shape=[jax.ShapeDtypeStruct((8, WIN), jnp.int32), turn, turn],
        in_specs=[vmem] * SIDE,
        out_specs=[vmem] * 3,
        compiler_params=pltpu.CompilerParams(vmem_limit_bytes=8 * 2**20),
        name="planned",
    )(*(pltpu.with_memory_space_constraint(v, pltpu.VMEM) for v in mains))


def interleave(real, imag):
    pieces = []
    for d in range(N_LINE):
        pieces += [real[8 * d : 8 * d + 8], imag[8 * d : 8 * d + 8]]
    return jnp.concatenate(pieces, 0)


def image_kernel(plan_ref, *refs):
    main_refs = refs[:SIDE]
    rim_ref, cos_ref, sin_ref, table_ref, held_ref, out_ref, slots_re, slots_im, total = refs[SIDE:]
    count = plan_ref[1, SIDE]

    def make_slot(group, n):
        entry = plan_ref[0, jnp.minimum(n, MAXB - 1)]
        place, f, b = (entry >> 8) & 15, (entry >> 4) & 15, entry & 15
        w, i, main_ref = b >> 1, place & 3, main_refs[group]
        head = main_ref[i, pl.ds(pl.multiple_of(w * HALF, HALF), HALF), :]
        tail = main_ref[i, pl.ds(pl.multiple_of(jnp.minimum(w + 1, 7) * HALF, HALF), HALF), :]
        window = jnp.concatenate([head, jnp.where(w == 7, rim_ref[i, group], tail)], 0)
        stacked = lax.dot_general(
            window, table_ref[2 * f + (b & 1)], (((0,), (0,)), ((), ())), preferred_element_type=jnp.float32
        )
        real = stacked[:S, :BR] - stacked[S:, BR:]
        imag = stacked[S:, :BR] + stacked[:S, BR:]
        cosine, sine = cos_ref[SIDE * group + i], sin_ref[SIDE * group + i]
        turned_re = real * cosine + imag * sine
        turned_im = imag * cosine - real * sine
        return interleave(turned_re, turned_im).astype(jnp.bfloat16), interleave(-turned_im, turned_re).astype(jnp.bfloat16)

    for group in range(SIDE):
        start, end = plan_ref[1, group], plan_ref[1, group + 1]

        def make_quad(c, carry, group=group, start=start):
            made = [make_slot(group, start + QUAD * c + k) for k in range(QUAD)]
            for k in range(QUAD):
                slots_re[start + QUAD * c + k], slots_im[start + QUAD * c + k] = made[k]
            return carry

        lax.fori_loop(0, (end - start + QUAD - 1) >> 2, make_quad, 0)
    for k in range(QUAD):
        slots_re[count + k] = jnp.zeros((2 * S, BR), jnp.bfloat16)
        slots_im[count + k] = jnp.zeros((2 * S, BR), jnp.bfloat16)
    total[...] = jnp.zeros_like(total)

    def multiply(c, carry):
        at = []
        for k in range(QUAD):
            slot = plan_ref[0, jnp.minimum(QUAD * c + k, count - 1)] >> 12
            at.append(pl.ds(pl.multiple_of(slot * BR, BR), BR))
        matrix = jnp.concatenate([held_ref[part, rows, :] for part in range(2) for rows in at], 0)
        beams = [ref[QUAD * c + k] for ref in (slots_re, slots_im) for k in range(QUAD)]
        total[...] += jnp.dot(jnp.concatenate(beams, 1), matrix, preferred_element_type=jnp.float32)
        return carry

    lax.fori_loop(0, (count + QUAD - 1) >> 2, multiply, 0)
    for d in range(N_LINE):
        for depth in range(TZ):
            out_ref[d, depth] = total[16 * d : 16 * d + 16, TX * depth : TX * depth + TX].astype(jnp.bfloat16)


def partial_image(plan, mains, rims, turns, tables, held):
    smem, vmem = pl.BlockSpec(memory_space=pltpu.SMEM), pl.BlockSpec(memory_space=pltpu.VMEM)
    fixed = [pltpu.with_memory_space_constraint(v, pltpu.VMEM) for v in (*mains, rims, *turns, tables, held)]
    room = MAXB + QUAD * 2
    return pl.pallas_call(
        image_kernel,
        out_shape=pltpu.VMEM((N_LINE, TZ, 16, TX), jnp.bfloat16),
        in_specs=[smem] + [vmem] * len(fixed),
        out_specs=vmem,
        scratch_shapes=[
            pltpu.VMEM((room, 2 * S, BR), jnp.bfloat16),
            pltpu.VMEM((room, 2 * S, BR), jnp.bfloat16),
            pltpu.VMEM((2 * S, WIDE), jnp.float32),
        ],
        compiler_params=pltpu.CompilerParams(vmem_limit_bytes=6 * 2**20),
        name="partial_image",
    )(plan, *fixed)


def sum_kernel(parts_ref, out_ref, top_ref, bottom_ref):
    for depth in range(TZ):
        total = parts_ref[0, depth].astype(jnp.float32)
        for line in range(1, N_LINE):
            total = total + parts_ref[line, depth].astype(jnp.float32)
        out_ref[depth] = total
        if depth < 2:
            top_ref[depth] = total
        if depth >= TZ - 2:
            bottom_ref[depth - TZ + 2] = total


def summed_lines(parts):
    shapes = [jax.ShapeDtypeStruct((rows, 16, TX), jnp.float32) for rows in (TZ, 2, 2)]
    return pl.pallas_call(
        sum_kernel,
        out_shape=shapes,
        in_specs=[pl.BlockSpec(memory_space=pltpu.VMEM)],
        out_specs=[pl.BlockSpec(memory_space=pltpu.VMEM)] * 3,
        compiler_params=pltpu.CompilerParams(vmem_limit_bytes=8 * 2**20),
        name="summed_lines",
    )(parts)


def add_filtered(filter_ref, results, sources):
    lane = lax.broadcasted_iota(jnp.int32, (16, TX), 1)
    for side in range(5):
        move = side - 2
        inside = (lane + move >= 0) & (lane + move < TX)
        for source, row in sources:
            if move:
                row = jnp.where(inside, pltpu.roll(row, (-move) % TX, 1), 0.0)
            for depth in range(max(0, source - 4), min(TZ, source + 1)):
                results[depth] = results[depth] + filter_ref[source - depth, side] * row
    return results


def inner_kernel(filter_ref, image_ref, out_ref):
    results = [jnp.zeros((16, TX), jnp.float32) for _ in range(TZ)]
    results = add_filtered(filter_ref, results, [(depth + 2, image_ref[depth]) for depth in range(TZ)])
    for depth in range(TZ):
        out_ref[depth] = results[depth]


def outer_kernel(filter_ref, above_ref, inner_ref, below_ref, out_ref):
    sources = [(0, above_ref[0]), (1, above_ref[1]), (TZ + 2, below_ref[0]), (TZ + 3, below_ref[1])]
    results = add_filtered(filter_ref, [inner_ref[depth] for depth in range(TZ)], sources)
    for depth in range(TZ):
        for part in range(2):
            out_ref[pl.ds(part * 64 + depth, 8, stride=TZ), :] = results[depth][8 * part : 8 * part + 8]


def dip_call(kernel, shape, dip_filter, *arrays):
    vmem = pl.BlockSpec(memory_space=pltpu.VMEM)
    return pl.pallas_call(
        kernel,
        out_shape=jax.ShapeDtypeStruct(shape, jnp.float32),
        in_specs=[pl.BlockSpec(memory_space=pltpu.SMEM)] + [vmem] * len(arrays),
        out_specs=vmem,
        compiler_params=pltpu.CompilerParams(vmem_limit_bytes=2 * 2**20),
    )(dip_filter, *arrays)


def spread(value, x_first, offsets=RING[1:]):
    received = []
    for offset in offsets:
        received.append(lax.ppermute(value, BOTH, hops(offset, x_first)))
    return received


def per_device(traces, codes, routes, beam_matrix, dip_filter):
    main = first_rows(traces, routes, codes)
    near = jnp.stack([main] + spread(main, False))
    mains = [near] + spread(near, True)
    plan, *turns = planned(*mains)
    tables = slant_tables()
    rim = lax.ppermute(near[:, :HALF], "line", [(i + 1, i) for i in range(N_LINE - 1)])
    rims = jnp.stack([rim] + spread(rim, False))
    held = held_matrices(beam_matrix)
    image = partial_image(plan, mains, rims, turns, tables, held)
    parts = lax.all_to_all(image, "line", 0, 0, tiled=True)
    image, top, bottom = summed_lines(parts)
    inner = dip_call(inner_kernel, (TZ, 16, TX), dip_filter, image)
    above = lax.ppermute(bottom, "tile", [(i, i + 1) for i in range(N_TILE - 1)])
    below = lax.ppermute(top, "tile", [(i + 1, i) for i in range(N_TILE - 1)])
    return dip_call(outer_kernel, (2 * 8 * TZ, TX), dip_filter, above, inner, below).reshape(2, 8, TZ, TX)


def solution(mesh):
    in_specs = (
        P("tile", "line", None),
        P("tile", None),
        P("line", "tile"),
        P("line", "tile", None, None, None),
        P(),
    )
    out_specs = P(None, "line", "tile", None)

    return jax.shard_map(per_device, mesh=mesh, in_specs=in_specs, out_specs=out_specs, check_vma=False)
```

time: 79.2 us -> 64 us (0.81)
  the two profiles are of different devices: /device:TPU:34 before, /device:TPU:0 now
where the time goes in v3:
time: 64 us; the launch traced here: 63.7 us
  starting transfers between devices  21.4 us (33%)
  Pallas kernels  15.3 us (24%)
  waiting for transfers between devices  14 us (22%)
  blocking collectives  12.8 us (20%)
    ppermute x9, starting transfers between devices, spread(): received.append(lax.ppermute(value, BOTH, hops(offset, x_first)))  14.1 us
    all_to_all x1, blocking collectives, per_device(): parts = lax.all_to_all(image, 'line', 0, 0, tiled=True)  12.8 us
    ppermute x9, waiting for transfers between devices, spread(): received.append(lax.ppermute(value, BOTH, hops(offset, x_first)))  8.62 us
    pallas_call x1, Pallas kernels, held_matrices(): pl.pallas_call(hold_kernel, out_shape=pltpu.VMEM((2, MAXB * BR, WIDE), jn...  5.93 us
    ppermute x1, starting transfers between devices, per_device(): lax.ppermute(bottom, 'tile', [(i, i + 1) for i in range(N_TILE - 1)])  4.69 us
    pallas_call x1, Pallas kernels, partial_image(): pl.pallas_call(image_kernel, out_shape=pltpu.VMEM((N_LINE, TZ, 16, TX), j...  3.99 us
    ppermute x1, waiting for transfers between devices, per_device(): below = lax.ppermute(top, 'tile', [(i + 1, i) for i in range(N_TILE - 1)])  3.55 us
    pallas_call x2, Pallas kernels, dip_call(): pl.pallas_call(kernel, out_shape=jax.ShapeDtypeStruct(shape, jnp.float32)...  2.09 us
  transfers between devices with their start and end apart: 12, of which 6 were waited for; matrix products, arithmetic and copies ran while one was open for 0% of the time, Pallas kernels for 13%

profile of v3, /device:TPU:0, one launch (start us, length us, event | category | flops | bytes accessed | tf_op | source)
XLA Modules:
  0.0 63.7 jit_solution(10281849244451890148)
XLA Ops:
  0.0 0.9 %first_rows.1 = bf16[528,128]{1,0:T(8,128)(2,1)S(1)} custom-call(bf16[1,512,128]{2,1,0:T(8,128)(2,1)} %traces_ref.1, s32[1,16]{1,0:T(1,128)} %routes_ref.1, s32[1,64]{1,0:T(1,128)} %codes_ref.1), custom_call_target="tpu_custom_call" | custom-call | tf_op jit(solution)/shard_map/first_rows/pallas_call | solution.py:58
  1.0 4.1 %collective-permute-start.2 = (bf16[528,128]{1,0:T(8,128)(2,1)S(1)}, bf16[528,128]{1,0:T(8,128)(2,1)S(1)}, u32[]{:S(2)}, u32[]{:S(2)}) collective-permute-start(bf16[528,128]{1,0:T(8,128)(2,1)S(1)} %first_rows.1), channel_id=1, source_target_pairs={{0,2},{1,3},{2,0},{3,1},{4,6},{5,7},{6,4},{7,5},{8,10},{9,11},{10,... | collective-permute-start | bytes 405512 | tf_op jit(solution)/shard_map/ppermute | solution.py:333
  5.0 0.7 %collective-permute-start.1 = (bf16[528,128]{1,0:T(8,128)(2,1)S(1)}, bf16[528,128]{1,0:T(8,128)(2,1)S(1)}, u32[]{:S(2)}, u32[]{:S(2)}) collective-permute-start(bf16[528,128]{1,0:T(8,128)(2,1)S(1)} %first_rows.1), channel_id=1, source_target_pairs={{0,3},{1,0},{2,1},{3,2},{4,7},{5,4},{6,5},{7,6},{8,11},{9,8},{10,9... | collective-permute-start | bytes 405512 | tf_op jit(solution)/shard_map/ppermute | solution.py:333
  5.7 1.3 %collective-permute-start = (bf16[528,128]{1,0:T(8,128)(2,1)S(1)}, bf16[528,128]{1,0:T(8,128)(2,1)S(1)}, u32[]{:S(2)}, u32[]{:S(2)}) collective-permute-start(bf16[528,128]{1,0:T(8,128)(2,1)S(1)} %first_rows.1), channel_id=1, source_target_pairs={{0,1},{1,2},{2,3},{3,0},{4,5},{5,6},{6,7},{7,4},{8,9},{9,10},{10,1... | collective-permute-start | bytes 405512 | tf_op jit(solution)/shard_map/ppermute | solution.py:333
  7.0 1.0 %collective-permute-done.2 = bf16[528,128]{1,0:T(8,128)(2,1)S(1)} collective-permute-done((bf16[528,128]{1,0:T(8,128)(2,1)S(1)}, bf16[528,128]{1,0:T(8,128)(2,1)S(1)}, u32[]{:S(2)}, u32[]{:S(2)}) %collective-permute-start.2) | collective-permute-done | bytes 135200 | tf_op jit(solution)/shard_map/ppermute | solution.py:333
  8.0 2.5 %collective-permute-done.1 = bf16[528,128]{1,0:T(8,128)(2,1)S(1)} collective-permute-done((bf16[528,128]{1,0:T(8,128)(2,1)S(1)}, bf16[528,128]{1,0:T(8,128)(2,1)S(1)}, u32[]{:S(2)}, u32[]{:S(2)}) %collective-permute-start.1) | collective-permute-done | bytes 135200 | tf_op jit(solution)/shard_map/ppermute | solution.py:333
  10.5 1.5 %collective-permute-done = bf16[528,128]{1,0:T(8,128)(2,1)S(1)} collective-permute-done((bf16[528,128]{1,0:T(8,128)(2,1)S(1)}, bf16[528,128]{1,0:T(8,128)(2,1)S(1)}, u32[]{:S(2)}, u32[]{:S(2)}) %collective-permute-start) | collective-permute-done | bytes 135200 | tf_op jit(solution)/shard_map/ppermute | solution.py:333
  12.0 3.1 %collective-permute-start.5 = (bf16[4,528,128]{2,1,0:T(8,128)(2,1)S(1)}, bf16[4,528,128]{2,1,0:T(8,128)(2,1)S(1)}, u32[]{:S(2)}, u32[]{:S(2)}) collective-permute-start(bf16[4,528,128]{2,1,0:T(8,128)(2,1)S(1)} %pad_maximum_fusion.own_ref.refs_0_), channel_id=1, source_target_pairs={{0,8},{1,9},{2,10},{3,11},{4,12},{5,13},{6,14},{7,15},{8,0},{9,1},... | collective-permute-start | bytes 1622024 | tf_op jit(solution)/shard_map/ppermute | solution.py:333
  15.1 1.1 %collective-permute-start.4 = (bf16[4,528,128]{2,1,0:T(8,128)(2,1)S(1)}, bf16[4,528,128]{2,1,0:T(8,128)(2,1)S(1)}, u32[]{:S(2)}, u32[]{:S(2)}) collective-permute-start(bf16[4,528,128]{2,1,0:T(8,128)(2,1)S(1)} %pad_maximum_fusion.own_ref.refs_0_), channel_id=1, source_target_pairs={{0,12},{1,13},{2,14},{3,15},{4,0},{5,1},{6,2},{7,3},{8,4},{9,5},{1... | collective-permute-start | bytes 1622024 | tf_op jit(solution)/shard_map/ppermute | solution.py:333
  16.3 0.9 %collective-permute-start.3 = (bf16[4,528,128]{2,1,0:T(8,128)(2,1)S(1)}, bf16[4,528,128]{2,1,0:T(8,128)(2,1)S(1)}, u32[]{:S(2)}, u32[]{:S(2)}) collective-permute-start(bf16[4,528,128]{2,1,0:T(8,128)(2,1)S(1)} %pad_maximum_fusion.own_ref.refs_0_), channel_id=1, source_target_pairs={{0,4},{1,5},{2,6},{3,7},{4,8},{5,9},{6,10},{7,11},{8,12},{9,13},{1... | collective-permute-start | bytes 1622024 | tf_op jit(solution)/shard_map/ppermute | solution.py:333
  17.2 1.3 %collective-permute-start.6 = (bf16[4,64,128]{2,1,0:T(8,128)(2,1)S(1)}, bf16[4,64,128]{2,1,0:T(8,128)(2,1)S(1)}, u32[]{:S(2)}, u32[]{:S(2)}) collective-permute-start(bf16[4,64,128]{2,1,0:T(8,128)(2,1)S(1)} %slice.4), channel_id=1, source_target_pairs={{16,0},{32,16},{48,32},{64,48},{80,64},{96,80},{112,96},{17,1},{33... | collective-permute-start | bytes 196616 | tf_op jit(solution)/shard_map/ppermute | solution.py:343
  18.5 1.8 %collective-permute-done.6 = bf16[4,64,128]{2,1,0:T(8,128)(2,1)S(1)} collective-permute-done((bf16[4,64,128]{2,1,0:T(8,128)(2,1)S(1)}, bf16[4,64,128]{2,1,0:T(8,128)(2,1)S(1)}, u32[]{:S(2)}, u32[]{:S(2)}) %collective-permute-start.6) | collective-permute-done | bytes 65568 | tf_op jit(solution)/shard_map/ppermute | solution.py:343
  20.3 1.2 %collective-permute-start.9 = (bf16[4,64,128]{2,1,0:T(8,128)(2,1)S(1)}, bf16[4,64,128]{2,1,0:T(8,128)(2,1)S(1)}, u32[]{:S(2)}, u32[]{:S(2)}) collective-permute-start(bf16[4,64,128]{2,1,0:T(8,128)(2,1)S(1)} %collective-permute-done.6), channel_id=1, source_target_pairs={{0,2},{1,3},{2,0},{3,1},{4,6},{5,7},{6,4},{7,5},{8,10},{9,11},{10,... | collective-permute-start | bytes 196616 | tf_op jit(solution)/shard_map/ppermute | solution.py:333
  21.5 1.6 %collective-permute-start.8 = (bf16[4,64,128]{2,1,0:T(8,128)(2,1)S(1)}, bf16[4,64,128]{2,1,0:T(8,128)(2,1)S(1)}, u32[]{:S(2)}, u32[]{:S(2)}) collective-permute-start(bf16[4,64,128]{2,1,0:T(8,128)(2,1)S(1)} %collective-permute-done.6), channel_id=1, source_target_pairs={{0,3},{1,0},{2,1},{3,2},{4,7},{5,4},{6,5},{7,6},{8,11},{9,8},{10,9... | collective-permute-start | bytes 196616 | tf_op jit(solution)/shard_map/ppermute | solution.py:333
  23.1 3.7 %collective-permute-done.9 = bf16[4,64,128]{2,1,0:T(8,128)(2,1)S(1)} collective-permute-done((bf16[4,64,128]{2,1,0:T(8,128)(2,1)S(1)}, bf16[4,64,128]{2,1,0:T(8,128)(2,1)S(1)}, u32[]{:S(2)}, u32[]{:S(2)}) %collective-permute-start.9) | collective-permute-done | bytes 65568 | tf_op jit(solution)/shard_map/ppermute | solution.py:333
  26.9 1.7 %slant_tables.1.refs_7_ = bf16[32,128,256]{2,1,0:T(8,128)(2,1)S(1)} custom-call(), custom_call_target="tpu_custom_call" | custom-call | tf_op jit(solution)/shard_map/slant_tables/pallas_call | solution.py:95
  28.6 5.9 %held_matrices.1.refs_8_ = bf16[2,4096,1024]{2,1,0:T(8,128)(2,1)S(1)} custom-call(bf16[1,1,2,4096,1024]{4,3,2,1,0:T(8,128)(2,1)} %matrix_ref.1), custom_call_target="tpu_custom_call" | custom-call | tf_op jit(solution)/shard_map/held_matrices/pallas_call | solution.py:118
  35.2 4.0 %partial_image.1 = bf16[8,8,16,128]{3,2,1,0:T(8,128)(2,1)S(1)} custom-call(s32[8,128]{1,0:T(8,128)S(1)} %get-tuple-element.11.plan_ref, bf16[4,528,128]{2,1,0:T(8,128)(2,1)S(1)} %pad_maximum_fusion.own_ref.refs_0_, bf16[4,528,128]{2,1,0:T(8,128)(2,1)S(1)} %collective-permute-done.3.one_ref.refs_1_, ...), custom_call_target="tpu_custom_call" | custom-call | tf_op jit(solution)/shard_map/partial_image/pallas_call | solution.py:252
  39.2 12.8 %all_to_all.5.parts_ref = bf16[8,8,16,128]{3,2,1,0:T(8,128)(2,1)S(1)} all-to-all(bf16[8,8,16,128]{3,2,1,0:T(8,128)(2,1)S(1)} %partial_image.1), channel_id=1, replica_groups=mesh['line'=8,'tile'=16] {'line'}, dimensions={0} | all-to-all | bytes 524288 | tf_op jit(solution)/shard_map/all_to_all | solution.py:347
  52.1 4.7 %collective-permute-start.10 = (f32[2,16,128]{2,1,0:T(8,128)S(1)}, f32[2,16,128]{2,1,0:T(8,128)S(1)}, u32[]{:S(2)}, u32[]{:S(2)}) collective-permute-start(f32[2,16,128]{2,1,0:T(8,128)S(1)} %get-tuple-element.14), channel_id=1, source_target_pairs={{0,1},{1,2},{2,3},{3,4},{4,5},{5,6},{6,7},{7,8},{8,9},{9,10},{10,1... | collective-permute-start | bytes 49160 | tf_op jit(solution)/shard_map/ppermute | solution.py:350
  56.8 1.3 %collective-permute-start.11 = (f32[2,16,128]{2,1,0:T(8,128)S(1)}, f32[2,16,128]{2,1,0:T(8,128)S(1)}, u32[]{:S(2)}, u32[]{:S(2)}) collective-permute-start(f32[2,16,128]{2,1,0:T(8,128)S(1)} %get-tuple-element.16), channel_id=1, source_target_pairs={{1,0},{2,1},{3,2},{4,3},{5,4},{6,5},{7,6},{8,7},{9,8},{10,9},{11,1... | collective-permute-start | bytes 49160 | tf_op jit(solution)/shard_map/ppermute | solution.py:351
  58.1 0.8 %shard_map.55.inner_ref = f32[8,16,128]{2,1,0:T(8,128)S(1)} custom-call(f32[5,5]{1,0:T(8,128)S(1)} %copy-done, f32[8,16,128]{2,1,0:T(8,128)S(1)} %get-tuple-element.15.image_ref), custom_call_target="tpu_custom_call" | custom-call | tf_op jit(solution)/shard_map/pallas_call | solution.py:321
  58.9 3.5 %collective-permute-done.11.below_ref = f32[2,16,128]{2,1,0:T(8,128)S(1)} collective-permute-done((f32[2,16,128]{2,1,0:T(8,128)S(1)}, f32[2,16,128]{2,1,0:T(8,128)S(1)}, u32[]{:S(2)}, u32[]{:S(2)}) %collective-permute-start.11) | collective-permute-done | bytes 16416 | tf_op jit(solution)/shard_map/ppermute | solution.py:351
  62.4 1.3 %shard_map.56 = f32[128,128]{1,0:T(8,128)} custom-call(f32[5,5]{1,0:T(8,128)S(1)} %copy-done, f32[2,16,128]{2,1,0:T(8,128)S(1)} %collective-permute-done.10.above_ref, f32[8,16,128]{2,1,0:T(8,128)S(1)} %shard_map.55.inner_ref, f32[2,16,128]{2,1,0:T(8,128)S(1)} %collective-permute-done.11.below_ref), custom_call_target="tpu_custom_call" | custom-call | tf_op jit(solution)/shard_map/pallas_call | solution.py:321
  (14 shorter events, 0.9 us)
Async XLA Ops:
  1.0 7.1 %collective-permute-start.2 = (bf16[528,128]{1,0:T(8,128)(2,1)S(1)}, bf16[528,128]{1,0:T(8,128)(2,1)S(1)}, u32[]{:S(2)}, u32[]{:S(2)}) collective-permute-start(bf16[528,128]{1,0:T(8,128)(2,1)S(1)} %first_rows.1), channel_id=1, source_target_pairs={{0,2},{1,3},{2,0},{3,1},{4,6},{5,7},{6,4},{7,5},{8,10},{9,11},{10,... | collective-permute-start | bytes 405512 | tf_op jit(solution)/shard_map/ppermute | solution.py:333
  5.0 5.5 %collective-permute-start.1 = (bf16[528,128]{1,0:T(8,128)(2,1)S(1)}, bf16[528,128]{1,0:T(8,128)(2,1)S(1)}, u32[]{:S(2)}, u32[]{:S(2)}) collective-permute-start(bf16[528,128]{1,0:T(8,128)(2,1)S(1)} %first_rows.1), channel_id=1, source_target_pairs={{0,3},{1,0},{2,1},{3,2},{4,7},{5,4},{6,5},{7,6},{8,11},{9,8},{10,9... | collective-permute-start | bytes 405512 | tf_op jit(solution)/shard_map/ppermute | solution.py:333
  5.7 6.2 %collective-permute-start = (bf16[528,128]{1,0:T(8,128)(2,1)S(1)}, bf16[528,128]{1,0:T(8,128)(2,1)S(1)}, u32[]{:S(2)}, u32[]{:S(2)}) collective-permute-start(bf16[528,128]{1,0:T(8,128)(2,1)S(1)} %first_rows.1), channel_id=1, source_target_pairs={{0,1},{1,2},{2,3},{3,0},{4,5},{5,6},{6,7},{7,4},{8,9},{9,10},{10,1... | collective-permute-start | bytes 405512 | tf_op jit(solution)/shard_map/ppermute | solution.py:333
  12.0 22.5 %collective-permute-start.5 = (bf16[4,528,128]{2,1,0:T(8,128)(2,1)S(1)}, bf16[4,528,128]{2,1,0:T(8,128)(2,1)S(1)}, u32[]{:S(2)}, u32[]{:S(2)}) collective-permute-start(bf16[4,528,128]{2,1,0:T(8,128)(2,1)S(1)} %pad_maximum_fusion.own_ref.refs_0_), channel_id=1, source_target_pairs={{0,8},{1,9},{2,10},{3,11},{4,12},{5,13},{6,14},{7,15},{8,0},{9,1},... | collective-permute-start | bytes 1622024 | tf_op jit(solution)/shard_map/ppermute | solution.py:333
  15.1 19.5 %collective-permute-start.4 = (bf16[4,528,128]{2,1,0:T(8,128)(2,1)S(1)}, bf16[4,528,128]{2,1,0:T(8,128)(2,1)S(1)}, u32[]{:S(2)}, u32[]{:S(2)}) collective-permute-start(bf16[4,528,128]{2,1,0:T(8,128)(2,1)S(1)} %pad_maximum_fusion.own_ref.refs_0_), channel_id=1, source_target_pairs={{0,12},{1,13},{2,14},{3,15},{4,0},{5,1},{6,2},{7,3},{8,4},{9,5},{1... | collective-permute-start | bytes 1622024 | tf_op jit(solution)/shard_map/ppermute | solution.py:333
  16.3 18.3 %collective-permute-start.3 = (bf16[4,528,128]{2,1,0:T(8,128)(2,1)S(1)}, bf16[4,528,128]{2,1,0:T(8,128)(2,1)S(1)}, u32[]{:S(2)}, u32[]{:S(2)}) collective-permute-start(bf16[4,528,128]{2,1,0:T(8,128)(2,1)S(1)} %pad_maximum_fusion.own_ref.refs_0_), channel_id=1, source_target_pairs={{0,4},{1,5},{2,6},{3,7},{4,8},{5,9},{6,10},{7,11},{8,12},{9,13},{1... | collective-permute-start | bytes 1622024 | tf_op jit(solution)/shard_map/ppermute | solution.py:333
  17.2 3.1 %collective-permute-start.6 = (bf16[4,64,128]{2,1,0:T(8,128)(2,1)S(1)}, bf16[4,64,128]{2,1,0:T(8,128)(2,1)S(1)}, u32[]{:S(2)}, u32[]{:S(2)}) collective-permute-start(bf16[4,64,128]{2,1,0:T(8,128)(2,1)S(1)} %slice.4), channel_id=1, source_target_pairs={{16,0},{32,16},{48,32},{64,48},{80,64},{96,80},{112,96},{17,1},{33... | collective-permute-start | bytes 196616 | tf_op jit(solution)/shard_map/ppermute | solution.py:343
  20.3 6.5 %collective-permute-start.9 = (bf16[4,64,128]{2,1,0:T(8,128)(2,1)S(1)}, bf16[4,64,128]{2,1,0:T(8,128)(2,1)S(1)}, u32[]{:S(2)}, u32[]{:S(2)}) collective-permute-start(bf16[4,64,128]{2,1,0:T(8,128)(2,1)S(1)} %collective-permute-done.6), channel_id=1, source_target_pairs={{0,2},{1,3},{2,0},{3,1},{4,6},{5,7},{6,4},{7,5},{8,10},{9,11},{10,... | collective-permute-start | bytes 196616 | tf_op jit(solution)/shard_map/ppermute | solution.py:333
  21.5 13.0 %collective-permute-start.8 = (bf16[4,64,128]{2,1,0:T(8,128)(2,1)S(1)}, bf16[4,64,128]{2,1,0:T(8,128)(2,1)S(1)}, u32[]{:S(2)}, u32[]{:S(2)}) collective-permute-start(bf16[4,64,128]{2,1,0:T(8,128)(2,1)S(1)} %collective-permute-done.6), channel_id=1, source_target_pairs={{0,3},{1,0},{2,1},{3,2},{4,7},{5,4},{6,5},{7,6},{8,11},{9,8},{10,9... | collective-permute-start | bytes 196616 | tf_op jit(solution)/shard_map/ppermute | solution.py:333
  26.8 7.7 %collective-permute-start.7 = (bf16[4,64,128]{2,1,0:T(8,128)(2,1)S(1)}, bf16[4,64,128]{2,1,0:T(8,128)(2,1)S(1)}, u32[]{:S(2)}, u32[]{:S(2)}) collective-permute-start(bf16[4,64,128]{2,1,0:T(8,128)(2,1)S(1)} %collective-permute-done.6), channel_id=1, source_target_pairs={{0,1},{1,2},{2,3},{3,0},{4,5},{5,6},{6,7},{7,4},{8,9},{9,10},{10,1... | collective-permute-start | bytes 196616 | tf_op jit(solution)/shard_map/ppermute | solution.py:333
  34.5 23.6 %copy-start = (f32[5,5]{1,0:T(8,128)S(1)}, f32[5,5]{1,0:T(8,128)}, u32[]{:S(2)}) copy-start(f32[5,5]{1,0:T(8,128)} %filter_ref.3) | copy-start | bytes 304
  52.1 6.8 %collective-permute-start.10 = (f32[2,16,128]{2,1,0:T(8,128)S(1)}, f32[2,16,128]{2,1,0:T(8,128)S(1)}, u32[]{:S(2)}, u32[]{:S(2)}) collective-permute-start(f32[2,16,128]{2,1,0:T(8,128)S(1)} %get-tuple-element.14), channel_id=1, source_target_pairs={{0,1},{1,2},{2,3},{3,4},{4,5},{5,6},{6,7},{7,8},{8,9},{9,10},{10,1... | collective-permute-start | bytes 49160 | tf_op jit(solution)/shard_map/ppermute | solution.py:350
  56.8 5.6 %collective-permute-start.11 = (f32[2,16,128]{2,1,0:T(8,128)S(1)}, f32[2,16,128]{2,1,0:T(8,128)S(1)}, u32[]{:S(2)}, u32[]{:S(2)}) collective-permute-start(f32[2,16,128]{2,1,0:T(8,128)S(1)} %get-tuple-element.16), channel_id=1, source_target_pairs={{1,0},{2,1},{3,2},{4,3},{5,4},{6,5},{7,6},{8,7},{9,8},{10,9},{11,1... | collective-permute-start | bytes 49160 | tf_op jit(solution)/shard_map/ppermute | solution.py:351

commit v4 on v3

--- a/solution.py
+++ b/solution.py
@@ -23,7 +23,8 @@
 N_LINE = 8
 N_TILE = 16
 QUAD = 4
-STREAMS = 16
+PIECES = (0, 1792, 2816, MAXB * BR)
+STREAMS = 4
 WIDE = TZ * TX
 
 
@@ -71,7 +72,10 @@
     )(*(pltpu.with_memory_space_constraint(v, pltpu.HBM) for v in (traces, routes, codes)))
 
 
-def table_kernel(table_ref):
+def table_kernel(matrix_ref, table_ref, held_ref, sems):
+    copies = piece_copies(0, matrix_ref, held_ref, sems)
+    for copy in copies:
+        copy.start()
     rows = lax.broadcasted_iota(jnp.int32, (WIN, P_SIZE), 0)
     cols = lax.broadcasted_iota(jnp.int32, (WIN, P_SIZE), 1)
     turns = (cols - P_SIZE // 2) * (2 * rows - (WIN - 1))
@@ -89,41 +93,57 @@
             table_ref[2 * f + q, :, :BR] = now_c[:, half].astype(jnp.bfloat16)
             table_ref[2 * f + q, :, BR:] = now_s[:, half].astype(jnp.bfloat16)
         now_c, now_s = now_c * step_c + now_s * step_s, now_s * step_c - now_c * step_s
-
-
-def slant_tables():
+    for copy in copies:
+        copy.wait()
+
+
+def slant_tables(beam_matrix):
+    vmem = pl.BlockSpec(memory_space=pltpu.VMEM)
     return pl.pallas_call(
         table_kernel,
-        out_shape=pltpu.VMEM((2 * N_TILE, WIN, 2 * BR), jnp.bfloat16),
-        out_specs=pl.BlockSpec(memory_space=pltpu.VMEM),
+        out_shape=[
+            pltpu.VMEM((2 * N_TILE, WIN, 2 * BR), jnp.bfloat16),
+            pltpu.VMEM((2, MAXB * BR, WIDE), jnp.bfloat16),
+        ],
+        in_specs=[pl.BlockSpec(memory_space=pltpu.HBM)],
+        out_specs=[vmem] * 2,
+        scratch_shapes=[pltpu.SemaphoreType.DMA((2 * STREAMS,))],
         compiler_params=pltpu.CompilerParams(vmem_limit_bytes=4 * 2**20),
         name="slant_tables",
-    )()
-
-
-def hold_kernel(matrix_ref, held_ref, sems):
+    )(pltpu.with_memory_space_constraint(beam_matrix, pltpu.HBM))
+
+
+def piece_copies(piece, matrix_ref, held_ref, sems):
     copies = []
+    first, rows = PIECES[piece], (PIECES[piece + 1] - PIECES[piece]) // STREAMS
     for part in range(2):
-        for piece in range(STREAMS // 2):
-            rows = pl.ds(piece * (2 * MAXB * BR // STREAMS), 2 * MAXB * BR // STREAMS)
-            source, target = matrix_ref.at[0, 0, part, rows, :], held_ref.at[part, rows, :]
+        for k in range(STREAMS):
+            at = pl.ds(first + k * rows, rows)
+            source, target = matrix_ref.at[0, 0, part, at, :], held_ref.at[part, at, :]
             copies.append(pltpu.make_async_copy(source, target, sems.at[len(copies)]))
+    return copies
+
+
+def hold_kernel(matrix_ref, before_ref, held_ref, sems):
+    copies = piece_copies(1, matrix_ref, held_ref, sems)
     for copy in copies:
         copy.start()
     for copy in copies:
         copy.wait()
 
 
-def held_matrices(beam_matrix):
+def held_more(beam_matrix, held):
+    hbm, vmem = pl.BlockSpec(memory_space=pltpu.HBM), pl.BlockSpec(memory_space=pltpu.VMEM)
     return pl.pallas_call(
         hold_kernel,
         out_shape=pltpu.VMEM((2, MAXB * BR, WIDE), jnp.bfloat16),
-        in_specs=[pl.BlockSpec(memory_space=pltpu.HBM)],
-        out_specs=pl.BlockSpec(memory_space=pltpu.VMEM),
-        scratch_shapes=[pltpu.SemaphoreType.DMA((STREAMS,))],
+        in_specs=[hbm, vmem],
+        out_specs=vmem,
+        scratch_shapes=[pltpu.SemaphoreType.DMA((2 * STREAMS,))],
+        input_output_aliases={1: 0},
         compiler_params=pltpu.CompilerParams(vmem_limit_bytes=2 * 2**20),
-        name="held_matrices",
-    )(pltpu.with_memory_space_constraint(beam_matrix, pltpu.HBM))
+        name="held_more",
+    )(pltpu.with_memory_space_constraint(beam_matrix, pltpu.HBM), pltpu.with_memory_space_constraint(held, pltpu.VMEM))
 
 
 def offset_of(place):
@@ -194,7 +214,11 @@
 
 def image_kernel(plan_ref, *refs):
     main_refs = refs[:SIDE]
-    rim_ref, cos_ref, sin_ref, table_ref, held_ref, out_ref, slots_re, slots_im, total = refs[SIDE:]
+    rim_ref, cos_ref, sin_ref, table_ref, matrix_ref, _, out_ref, held_ref = refs[SIDE : SIDE + 8]
+    slots_re, slots_im, total, sems = refs[SIDE + 8 :]
+    copies = piece_copies(2, matrix_ref, held_ref, sems)
+    for copy in copies:
+        copy.start()
     count = plan_ref[1, SIDE]
 
     def make_slot(group, n):
@@ -228,6 +252,8 @@
         slots_re[count + k] = jnp.zeros((2 * S, BR), jnp.bfloat16)
         slots_im[count + k] = jnp.zeros((2 * S, BR), jnp.bfloat16)
     total[...] = jnp.zeros_like(total)
+    for copy in copies:
+        copy.wait()
 
     def multiply(c, carry):
         at = []
@@ -245,35 +271,44 @@
             out_ref[d, depth] = total[16 * d : 16 * d + 16, TX * depth : TX * depth + TX].astype(jnp.bfloat16)
 
 
-def partial_image(plan, mains, rims, turns, tables, held):
+def partial_image(plan, mains, rims, turns, tables, beam_matrix, held):
     smem, vmem = pl.BlockSpec(memory_space=pltpu.SMEM), pl.BlockSpec(memory_space=pltpu.VMEM)
-    fixed = [pltpu.with_memory_space_constraint(v, pltpu.VMEM) for v in (*mains, rims, *turns, tables, held)]
+    fixed = [pltpu.with_memory_space_constraint(v, pltpu.VMEM) for v in (*mains, rims, *turns, tables)]
+    fixed.append(pltpu.with_memory_space_constraint(beam_matrix, pltpu.HBM))
     room = MAXB + QUAD * 2
     return pl.pallas_call(
         image_kernel,
-        out_shape=pltpu.VMEM((N_LINE, TZ, 16, TX), jnp.bfloat16),
-        in_specs=[smem] + [vmem] * len(fixed),
-        out_specs=vmem,
+        out_shape=[
+            pltpu.VMEM((N_LINE, TZ, 16, TX), jnp.bfloat16),
+            pltpu.VMEM((2, MAXB * BR, WIDE), jnp.bfloat16),
+        ],
+        in_specs=[smem] + [vmem] * (len(fixed) - 1) + [pl.BlockSpec(memory_space=pltpu.HBM), vmem],
+        out_specs=[vmem] * 2,
         scratch_shapes=[
             pltpu.VMEM((room, 2 * S, BR), jnp.bfloat16),
             pltpu.VMEM((room, 2 * S, BR), jnp.bfloat16),
             pltpu.VMEM((2 * S, WIDE), jnp.float32),
+            pltpu.SemaphoreType.DMA((2 * STREAMS,)),
         ],
+        input_output_aliases={1 + len(fixed): 1},
         compiler_params=pltpu.CompilerParams(vmem_limit_bytes=6 * 2**20),
         name="partial_image",
-    )(plan, *fixed)
-
-
-def sum_kernel(parts_ref, out_ref, top_ref, bottom_ref):
+    )(plan, *fixed, pltpu.with_memory_space_constraint(held, pltpu.VMEM))[0]
+
+
+def sum_kernel(parts_ref, out_ref, first_ref, second_ref):
+    odd = (lax.axis_index("tile") & 1) == 1
+    totals = []
     for depth in range(TZ):
         total = parts_ref[0, depth].astype(jnp.float32)
         for line in range(1, N_LINE):
             total = total + parts_ref[line, depth].astype(jnp.float32)
         out_ref[depth] = total
-        if depth < 2:
-            top_ref[depth] = total
-        if depth >= TZ - 2:
-            bottom_ref[depth - TZ + 2] = total
+        totals.append(total)
+    for row in range(2):
+        top, bottom = totals[row], totals[TZ - 2 + row]
+        first_ref[row] = jnp.where(odd, top, bottom)
+        second_ref[row] = jnp.where(odd, bottom, top)
 
 
 def summed_lines(parts):
@@ -308,8 +343,10 @@
         out_ref[depth] = results[depth]
 
 
-def outer_kernel(filter_ref, above_ref, inner_ref, below_ref, out_ref):
-    sources = [(0, above_ref[0]), (1, above_ref[1]), (TZ + 2, below_ref[0]), (TZ + 3, below_ref[1])]
+def outer_kernel(filter_ref, first_ref, inner_ref, second_ref, out_ref):
+    odd = (lax.axis_index("tile") & 1) == 1
+    sources = [(row, jnp.where(odd, first_ref[row], second_ref[row])) for row in range(2)]
+    sources += [(TZ + 2 + row, jnp.where(odd, second_ref[row], first_ref[row])) for row in range(2)]
     results = add_filtered(filter_ref, [inner_ref[depth] for depth in range(TZ)], sources)
     for depth in range(TZ):
         for part in range(2):
@@ -339,17 +376,17 @@
     near = jnp.stack([main] + spread(main, False))
     mains = [near] + spread(near, True)
     plan, *turns = planned(*mains)
-    tables = slant_tables()
+    tables, held = slant_tables(beam_matrix)
     rim = lax.ppermute(near[:, :HALF], "line", [(i + 1, i) for i in range(N_LINE - 1)])
     rims = jnp.stack([rim] + spread(rim, False))
-    held = held_matrices(beam_matrix)
-    image = partial_image(plan, mains, rims, turns, tables, held)
+    held = held_more(beam_matrix, held)
+    image = partial_image(plan, mains, rims, turns, tables, beam_matrix, held)
     parts = lax.all_to_all(image, "line", 0, 0, tiled=True)
-    image, top, bottom = summed_lines(parts)
+    image, first, second = summed_lines(parts)
     inner = dip_call(inner_kernel, (TZ, 16, TX), dip_filter, image)
-    above = lax.ppermute(bottom, "tile", [(i, i + 1) for i in range(N_TILE - 1)])
-    below = lax.ppermute(top, "tile", [(i + 1, i) for i in range(N_TILE - 1)])
-    return dip_call(outer_kernel, (2 * 8 * TZ, TX), dip_filter, above, inner, below).reshape(2, 8, TZ, TX)
+    first = lax.ppermute(first, "tile", [(i, i ^ 1) for i in range(N_TILE)])
+    second = lax.ppermute(second, "tile", [(i, ((i - 1) ^ 1) + 1) for i in range(1, N_TILE - 1)])
+    return dip_call(outer_kernel, (2 * 8 * TZ, TX), dip_filter, first, inner, second).reshape(2, 8, TZ, TX)
 
 
 def solution(mesh):

time: 64 us -> 61.8 us (0.966)
  the two profiles are of different devices: /device:TPU:0 before, /device:TPU:2 now
where the time goes in v4:
time: 61.8 us; the launch traced here: 61.6 us
  starting transfers between devices  21.2 us (34%)
  Pallas kernels  14.6 us (24%)
  waiting for transfers between devices  13.4 us (22%)
  blocking collectives  12 us (19%)
    ppermute x9, starting transfers between devices, spread(): received.append(lax.ppermute(value, BOTH, hops(offset, x_first)))  13.6 us
    all_to_all x1, blocking collectives, per_device(): parts = lax.all_to_all(image, 'line', 0, 0, tiled=True)  12 us
    ppermute x9, waiting for transfers between devices, spread(): received.append(lax.ppermute(value, BOTH, hops(offset, x_first)))  8.09 us
    pallas_call x1, Pallas kernels, partial_image(): pl.pallas_call(image_kernel, out_shape=[pltpu.VMEM((N_LINE, TZ, 16, TX),...  5.52 us
    ppermute x1, waiting for transfers between devices, per_device(): lax.ppermute(second, 'tile', [(i, (i - 1 ^ 1) + 1) for i in range(1, N_TI...  3.47 us
    ppermute x1, starting transfers between devices, per_device(): lax.ppermute(second, 'tile', [(i, (i - 1 ^ 1) + 1) for i in range(1, N_TI...  3.47 us
    pallas_call x1, Pallas kernels, slant_tables(): pl.pallas_call(table_kernel, out_shape=[pltpu.VMEM((2 * N_TILE, WIN, 2 *...  3.17 us
    ppermute x1, starting transfers between devices, per_device(): first = lax.ppermute(first, 'tile', [(i, i ^ 1) for i in range(N_TILE)])  2.88 us
  transfers between devices with their start and end apart: 12, of which 6 were waited for; matrix products, arithmetic and copies ran while one was open for 0% of the time, Pallas kernels for 10%

profile of v4, /device:TPU:2, one launch (start us, length us, event | category | flops | bytes accessed | tf_op | source)
XLA Modules:
  0.0 61.6 jit_solution(14276098435823716914)
XLA Ops:
  0.0 0.9 %first_rows.1 = bf16[528,128]{1,0:T(8,128)(2,1)S(1)} custom-call(bf16[1,512,128]{2,1,0:T(8,128)(2,1)} %traces_ref.1, s32[1,16]{1,0:T(1,128)} %routes_ref.1, s32[1,64]{1,0:T(1,128)} %codes_ref.1), custom_call_target="tpu_custom_call" | custom-call | tf_op jit(solution)/shard_map/first_rows/pallas_call | solution.py:59
  1.0 4.0 %collective-permute-start.2 = (bf16[528,128]{1,0:T(8,128)(2,1)S(1)}, bf16[528,128]{1,0:T(8,128)(2,1)S(1)}, u32[]{:S(2)}, u32[]{:S(2)}) collective-permute-start(bf16[528,128]{1,0:T(8,128)(2,1)S(1)} %first_rows.1), channel_id=1, source_target_pairs={{0,2},{1,3},{2,0},{3,1},{4,6},{5,7},{6,4},{7,5},{8,10},{9,11},{10,... | collective-permute-start | bytes 405512 | tf_op jit(solution)/shard_map/ppermute | solution.py:370
  4.9 0.7 %collective-permute-start.1 = (bf16[528,128]{1,0:T(8,128)(2,1)S(1)}, bf16[528,128]{1,0:T(8,128)(2,1)S(1)}, u32[]{:S(2)}, u32[]{:S(2)}) collective-permute-start(bf16[528,128]{1,0:T(8,128)(2,1)S(1)} %first_rows.1), channel_id=1, source_target_pairs={{0,3},{1,0},{2,1},{3,2},{4,7},{5,4},{6,5},{7,6},{8,11},{9,8},{10,9... | collective-permute-start | bytes 405512 | tf_op jit(solution)/shard_map/ppermute | solution.py:370
  5.6 1.3 %collective-permute-start = (bf16[528,128]{1,0:T(8,128)(2,1)S(1)}, bf16[528,128]{1,0:T(8,128)(2,1)S(1)}, u32[]{:S(2)}, u32[]{:S(2)}) collective-permute-start(bf16[528,128]{1,0:T(8,128)(2,1)S(1)} %first_rows.1), channel_id=1, source_target_pairs={{0,1},{1,2},{2,3},{3,0},{4,5},{5,6},{6,7},{7,4},{8,9},{9,10},{10,1... | collective-permute-start | bytes 405512 | tf_op jit(solution)/shard_map/ppermute | solution.py:370
  6.9 1.0 %collective-permute-done.2 = bf16[528,128]{1,0:T(8,128)(2,1)S(1)} collective-permute-done((bf16[528,128]{1,0:T(8,128)(2,1)S(1)}, bf16[528,128]{1,0:T(8,128)(2,1)S(1)}, u32[]{:S(2)}, u32[]{:S(2)}) %collective-permute-start.2) | collective-permute-done | bytes 135200 | tf_op jit(solution)/shard_map/ppermute | solution.py:370
  7.9 2.5 %collective-permute-done.1 = bf16[528,128]{1,0:T(8,128)(2,1)S(1)} collective-permute-done((bf16[528,128]{1,0:T(8,128)(2,1)S(1)}, bf16[528,128]{1,0:T(8,128)(2,1)S(1)}, u32[]{:S(2)}, u32[]{:S(2)}) %collective-permute-start.1) | collective-permute-done | bytes 135200 | tf_op jit(solution)/shard_map/ppermute | solution.py:370
  10.4 1.5 %collective-permute-done = bf16[528,128]{1,0:T(8,128)(2,1)S(1)} collective-permute-done((bf16[528,128]{1,0:T(8,128)(2,1)S(1)}, bf16[528,128]{1,0:T(8,128)(2,1)S(1)}, u32[]{:S(2)}, u32[]{:S(2)}) %collective-permute-start) | collective-permute-done | bytes 135200 | tf_op jit(solution)/shard_map/ppermute | solution.py:370
  11.9 2.2 %collective-permute-start.5 = (bf16[4,528,128]{2,1,0:T(8,128)(2,1)S(1)}, bf16[4,528,128]{2,1,0:T(8,128)(2,1)S(1)}, u32[]{:S(2)}, u32[]{:S(2)}) collective-permute-start(bf16[4,528,128]{2,1,0:T(8,128)(2,1)S(1)} %pad_maximum_fusion.own_ref.refs_0_), channel_id=1, source_target_pairs={{0,8},{1,9},{2,10},{3,11},{4,12},{5,13},{6,14},{7,15},{8,0},{9,1},... | collective-permute-start | bytes 1622024 | tf_op jit(solution)/shard_map/ppermute | solution.py:370
  14.1 1.4 %collective-permute-start.4 = (bf16[4,528,128]{2,1,0:T(8,128)(2,1)S(1)}, bf16[4,528,128]{2,1,0:T(8,128)(2,1)S(1)}, u32[]{:S(2)}, u32[]{:S(2)}) collective-permute-start(bf16[4,528,128]{2,1,0:T(8,128)(2,1)S(1)} %pad_maximum_fusion.own_ref.refs_0_), channel_id=1, source_target_pairs={{0,12},{1,13},{2,14},{3,15},{4,0},{5,1},{6,2},{7,3},{8,4},{9,5},{1... | collective-permute-start | bytes 1622024 | tf_op jit(solution)/shard_map/ppermute | solution.py:370
  16.2 1.3 %collective-permute-start.6 = (bf16[4,64,128]{2,1,0:T(8,128)(2,1)S(1)}, bf16[4,64,128]{2,1,0:T(8,128)(2,1)S(1)}, u32[]{:S(2)}, u32[]{:S(2)}) collective-permute-start(bf16[4,64,128]{2,1,0:T(8,128)(2,1)S(1)} %slice.4), channel_id=1, source_target_pairs={{16,0},{32,16},{48,32},{64,48},{80,64},{96,80},{112,96},{17,1},{33... | collective-permute-start | bytes 196616 | tf_op jit(solution)/shard_map/ppermute | solution.py:380
  17.4 1.8 %collective-permute-done.6 = bf16[4,64,128]{2,1,0:T(8,128)(2,1)S(1)} collective-permute-done((bf16[4,64,128]{2,1,0:T(8,128)(2,1)S(1)}, bf16[4,64,128]{2,1,0:T(8,128)(2,1)S(1)}, u32[]{:S(2)}, u32[]{:S(2)}) %collective-permute-start.6) | collective-permute-done | bytes 65568 | tf_op jit(solution)/shard_map/ppermute | solution.py:380
  19.3 1.2 %collective-permute-start.9 = (bf16[4,64,128]{2,1,0:T(8,128)(2,1)S(1)}, bf16[4,64,128]{2,1,0:T(8,128)(2,1)S(1)}, u32[]{:S(2)}, u32[]{:S(2)}) collective-permute-start(bf16[4,64,128]{2,1,0:T(8,128)(2,1)S(1)} %collective-permute-done.6), channel_id=1, source_target_pairs={{0,2},{1,3},{2,0},{3,1},{4,6},{5,7},{6,4},{7,5},{8,10},{9,11},{10,... | collective-permute-start | bytes 196616 | tf_op jit(solution)/shard_map/ppermute | solution.py:370
  20.5 1.6 %collective-permute-start.8 = (bf16[4,64,128]{2,1,0:T(8,128)(2,1)S(1)}, bf16[4,64,128]{2,1,0:T(8,128)(2,1)S(1)}, u32[]{:S(2)}, u32[]{:S(2)}) collective-permute-start(bf16[4,64,128]{2,1,0:T(8,128)(2,1)S(1)} %collective-permute-done.6), channel_id=1, source_target_pairs={{0,3},{1,0},{2,1},{3,2},{4,7},{5,4},{6,5},{7,6},{8,11},{9,8},{10,9... | collective-permute-start | bytes 196616 | tf_op jit(solution)/shard_map/ppermute | solution.py:370
  22.1 3.2 %collective-permute-done.9 = bf16[4,64,128]{2,1,0:T(8,128)(2,1)S(1)} collective-permute-done((bf16[4,64,128]{2,1,0:T(8,128)(2,1)S(1)}, bf16[4,64,128]{2,1,0:T(8,128)(2,1)S(1)}, u32[]{:S(2)}, u32[]{:S(2)}) %collective-permute-start.9) | collective-permute-done | bytes 65568 | tf_op jit(solution)/shard_map/ppermute | solution.py:370
  25.2 0.6 %collective-permute-start.7 = (bf16[4,64,128]{2,1,0:T(8,128)(2,1)S(1)}, bf16[4,64,128]{2,1,0:T(8,128)(2,1)S(1)}, u32[]{:S(2)}, u32[]{:S(2)}) collective-permute-start(bf16[4,64,128]{2,1,0:T(8,128)(2,1)S(1)} %collective-permute-done.6), channel_id=1, source_target_pairs={{0,1},{1,2},{2,3},{3,0},{4,5},{5,6},{6,7},{7,4},{8,9},{9,10},{10,1... | collective-permute-start | bytes 196616 | tf_op jit(solution)/shard_map/ppermute | solution.py:370
  25.9 3.2 %slant_tables.1 = (bf16[32,128,256]{2,1,0:T(8,128)(2,1)S(1)}, bf16[2,4096,1024]{2,1,0:T(8,128)(2,1)S(1)}) custom-call(bf16[1,1,2,4096,1024]{4,3,2,1,0:T(8,128)(2,1)} %refs_8_.1), custom_call_target="tpu_custom_call" | custom-call | tf_op jit(solution)/shard_map/slant_tables/pallas_call | solution.py:102
  29.0 2.2 %held_more.1.refs_9_ = bf16[2,4096,1024]{2,1,0:T(8,128)(2,1)S(1)} custom-call(bf16[1,1,2,4096,1024]{4,3,2,1,0:T(8,128)(2,1)} %refs_8_.1, bf16[2,4096,1024]{2,1,0:T(8,128)(2,1)S(1)} %get-tuple-element.18.before_ref), custom_call_target="tpu_custom_call", output_to_operand_aliasing={{}: (1, {})} | custom-call | tf_op jit(solution)/shard_map/held_more/pallas_call | solution.py:137
  32.0 5.5 %partial_image.1 = (bf16[8,8,16,128]{3,2,1,0:T(8,128)(2,1)S(1)}, bf16[2,4096,1024]{2,1,0:T(8,128)(2,1)S(1)}) custom-call(s32[8,128]{1,0:T(8,128)S(1)} %get-tuple-element.14.plan_ref, bf16[4,528,128]{2,1,0:T(8,128)(2,1)S(1)} %pad_maximum_fusion.own_ref.refs_0_, ...), custom_call_target="tpu_custom_call", output_to_operand_aliasing={{1}: (10, {})} | custom-call | tf_op jit(solution)/shard_map/partial_image/pallas_call | solution.py:279
  37.5 12.0 %all_to_all.5.parts_ref = bf16[8,8,16,128]{3,2,1,0:T(8,128)(2,1)S(1)} all-to-all(bf16[8,8,16,128]{3,2,1,0:T(8,128)(2,1)S(1)} %get-tuple-element.19), channel_id=1, replica_groups=mesh['line'=8,'tile'=16] {'line'}, dimensions={0} | all-to-all | bytes 524288 | tf_op jit(solution)/shard_map/all_to_all | solution.py:384
  49.6 2.9 %collective-permute-start.10 = (f32[2,16,128]{2,1,0:T(8,128)S(1)}, f32[2,16,128]{2,1,0:T(8,128)S(1)}, u32[]{:S(2)}, u32[]{:S(2)}) collective-permute-start(f32[2,16,128]{2,1,0:T(8,128)S(1)} %get-tuple-element.20), channel_id=1, source_target_pairs={{0,1},{1,0},{2,3},{3,2},{4,5},{5,4},{6,7},{7,6},{8,9},{9,8},{10,11... | collective-permute-start | bytes 49160 | tf_op jit(solution)/shard_map/ppermute | solution.py:387
  52.5 3.5 %collective-permute-start.11 = (f32[2,16,128]{2,1,0:T(8,128)S(1)}, f32[2,16,128]{2,1,0:T(8,128)S(1)}, u32[]{:S(2)}, u32[]{:S(2)}) collective-permute-start(f32[2,16,128]{2,1,0:T(8,128)S(1)} %get-tuple-element.22), channel_id=1, source_target_pairs={{1,2},{2,1},{3,4},{4,3},{5,6},{6,5},{7,8},{8,7},{9,10},{10,9},{11,... | collective-permute-start | bytes 49160 | tf_op jit(solution)/shard_map/ppermute | solution.py:388
  56.0 0.8 %shard_map.55.inner_ref = f32[8,16,128]{2,1,0:T(8,128)S(1)} custom-call(f32[5,5]{1,0:T(8,128)S(1)} %copy-done, f32[8,16,128]{2,1,0:T(8,128)S(1)} %get-tuple-element.21.image_ref), custom_call_target="tpu_custom_call" | custom-call | tf_op jit(solution)/shard_map/pallas_call | solution.py:358
  56.8 3.5 %collective-permute-done.11.second_ref = f32[2,16,128]{2,1,0:T(8,128)S(1)} collective-permute-done((f32[2,16,128]{2,1,0:T(8,128)S(1)}, f32[2,16,128]{2,1,0:T(8,128)S(1)}, u32[]{:S(2)}, u32[]{:S(2)}) %collective-permute-start.11) | collective-permute-done | bytes 16416 | tf_op jit(solution)/shard_map/ppermute | solution.py:388
  60.2 1.3 %shard_map.56 = f32[128,128]{1,0:T(8,128)} custom-call(f32[5,5]{1,0:T(8,128)S(1)} %copy-done, f32[2,16,128]{2,1,0:T(8,128)S(1)} %collective-permute-done.10.first_ref, f32[8,16,128]{2,1,0:T(8,128)S(1)} %shard_map.55.inner_ref, f32[2,16,128]{2,1,0:T(8,128)S(1)} %collective-permute-done.11.second_ref), custom_call_target="tpu_custom_call" | custom-call | tf_op jit(solution)/shard_map/pallas_call | solution.py:358
  (14 shorter events, 1.4 us)
Async XLA Ops:
  1.0 6.9 %collective-permute-start.2 = (bf16[528,128]{1,0:T(8,128)(2,1)S(1)}, bf16[528,128]{1,0:T(8,128)(2,1)S(1)}, u32[]{:S(2)}, u32[]{:S(2)}) collective-permute-start(bf16[528,128]{1,0:T(8,128)(2,1)S(1)} %first_rows.1), channel_id=1, source_target_pairs={{0,2},{1,3},{2,0},{3,1},{4,6},{5,7},{6,4},{7,5},{8,10},{9,11},{10,... | collective-permute-start | bytes 405512 | tf_op jit(solution)/shard_map/ppermute | solution.py:370
  4.9 5.5 %collective-permute-start.1 = (bf16[528,128]{1,0:T(8,128)(2,1)S(1)}, bf16[528,128]{1,0:T(8,128)(2,1)S(1)}, u32[]{:S(2)}, u32[]{:S(2)}) collective-permute-start(bf16[528,128]{1,0:T(8,128)(2,1)S(1)} %first_rows.1), channel_id=1, source_target_pairs={{0,3},{1,0},{2,1},{3,2},{4,7},{5,4},{6,5},{7,6},{8,11},{9,8},{10,9... | collective-permute-start | bytes 405512 | tf_op jit(solution)/shard_map/ppermute | solution.py:370
  5.6 6.2 %collective-permute-start = (bf16[528,128]{1,0:T(8,128)(2,1)S(1)}, bf16[528,128]{1,0:T(8,128)(2,1)S(1)}, u32[]{:S(2)}, u32[]{:S(2)}) collective-permute-start(bf16[528,128]{1,0:T(8,128)(2,1)S(1)} %first_rows.1), channel_id=1, source_target_pairs={{0,1},{1,2},{2,3},{3,0},{4,5},{5,6},{6,7},{7,4},{8,9},{9,10},{10,1... | collective-permute-start | bytes 405512 | tf_op jit(solution)/shard_map/ppermute | solution.py:370
  11.9 19.4 %collective-permute-start.5 = (bf16[4,528,128]{2,1,0:T(8,128)(2,1)S(1)}, bf16[4,528,128]{2,1,0:T(8,128)(2,1)S(1)}, u32[]{:S(2)}, u32[]{:S(2)}) collective-permute-start(bf16[4,528,128]{2,1,0:T(8,128)(2,1)S(1)} %pad_maximum_fusion.own_ref.refs_0_), channel_id=1, source_target_pairs={{0,8},{1,9},{2,10},{3,11},{4,12},{5,13},{6,14},{7,15},{8,0},{9,1},... | collective-permute-start | bytes 1622024 | tf_op jit(solution)/shard_map/ppermute | solution.py:370
  14.1 17.2 %collective-permute-start.4 = (bf16[4,528,128]{2,1,0:T(8,128)(2,1)S(1)}, bf16[4,528,128]{2,1,0:T(8,128)(2,1)S(1)}, u32[]{:S(2)}, u32[]{:S(2)}) collective-permute-start(bf16[4,528,128]{2,1,0:T(8,128)(2,1)S(1)} %pad_maximum_fusion.own_ref.refs_0_), channel_id=1, source_target_pairs={{0,12},{1,13},{2,14},{3,15},{4,0},{5,1},{6,2},{7,3},{8,4},{9,5},{1... | collective-permute-start | bytes 1622024 | tf_op jit(solution)/shard_map/ppermute | solution.py:370
  15.6 15.8 %collective-permute-start.3 = (bf16[4,528,128]{2,1,0:T(8,128)(2,1)S(1)}, bf16[4,528,128]{2,1,0:T(8,128)(2,1)S(1)}, u32[]{:S(2)}, u32[]{:S(2)}) collective-permute-start(bf16[4,528,128]{2,1,0:T(8,128)(2,1)S(1)} %pad_maximum_fusion.own_ref.refs_0_), channel_id=1, source_target_pairs={{0,4},{1,5},{2,6},{3,7},{4,8},{5,9},{6,10},{7,11},{8,12},{9,13},{1... | collective-permute-start | bytes 1622024 | tf_op jit(solution)/shard_map/ppermute | solution.py:370
  16.2 3.1 %collective-permute-start.6 = (bf16[4,64,128]{2,1,0:T(8,128)(2,1)S(1)}, bf16[4,64,128]{2,1,0:T(8,128)(2,1)S(1)}, u32[]{:S(2)}, u32[]{:S(2)}) collective-permute-start(bf16[4,64,128]{2,1,0:T(8,128)(2,1)S(1)} %slice.4), channel_id=1, source_target_pairs={{16,0},{32,16},{48,32},{64,48},{80,64},{96,80},{112,96},{17,1},{33... | collective-permute-start | bytes 196616 | tf_op jit(solution)/shard_map/ppermute | solution.py:380
  19.3 5.9 %collective-permute-start.9 = (bf16[4,64,128]{2,1,0:T(8,128)(2,1)S(1)}, bf16[4,64,128]{2,1,0:T(8,128)(2,1)S(1)}, u32[]{:S(2)}, u32[]{:S(2)}) collective-permute-start(bf16[4,64,128]{2,1,0:T(8,128)(2,1)S(1)} %collective-permute-done.6), channel_id=1, source_target_pairs={{0,2},{1,3},{2,0},{3,1},{4,6},{5,7},{6,4},{7,5},{8,10},{9,11},{10,... | collective-permute-start | bytes 196616 | tf_op jit(solution)/shard_map/ppermute | solution.py:370
  20.5 10.8 %collective-permute-start.8 = (bf16[4,64,128]{2,1,0:T(8,128)(2,1)S(1)}, bf16[4,64,128]{2,1,0:T(8,128)(2,1)S(1)}, u32[]{:S(2)}, u32[]{:S(2)}) collective-permute-start(bf16[4,64,128]{2,1,0:T(8,128)(2,1)S(1)} %collective-permute-done.6), channel_id=1, source_target_pairs={{0,3},{1,0},{2,1},{3,2},{4,7},{5,4},{6,5},{7,6},{8,11},{9,8},{10,9... | collective-permute-start | bytes 196616 | tf_op jit(solution)/shard_map/ppermute | solution.py:370
  25.2 6.0 %collective-permute-start.7 = (bf16[4,64,128]{2,1,0:T(8,128)(2,1)S(1)}, bf16[4,64,128]{2,1,0:T(8,128)(2,1)S(1)}, u32[]{:S(2)}, u32[]{:S(2)}) collective-permute-start(bf16[4,64,128]{2,1,0:T(8,128)(2,1)S(1)} %collective-permute-done.6), channel_id=1, source_target_pairs={{0,1},{1,2},{2,3},{3,0},{4,5},{5,6},{6,7},{7,4},{8,9},{9,10},{10,1... | collective-permute-start | bytes 196616 | tf_op jit(solution)/shard_map/ppermute | solution.py:370
  32.0 24.0 %copy-start = (f32[5,5]{1,0:T(8,128)S(1)}, f32[5,5]{1,0:T(8,128)}, u32[]{:S(2)}) copy-start(f32[5,5]{1,0:T(8,128)} %filter_ref.3) | copy-start | bytes 304
  49.6 7.1 %collective-permute-start.10 = (f32[2,16,128]{2,1,0:T(8,128)S(1)}, f32[2,16,128]{2,1,0:T(8,128)S(1)}, u32[]{:S(2)}, u32[]{:S(2)}) collective-permute-start(f32[2,16,128]{2,1,0:T(8,128)S(1)} %get-tuple-element.20), channel_id=1, source_target_pairs={{0,1},{1,0},{2,3},{3,2},{4,5},{5,4},{6,7},{7,6},{8,9},{9,8},{10,11... | collective-permute-start | bytes 49160 | tf_op jit(solution)/shard_map/ppermute | solution.py:387
  52.5 7.7 %collective-permute-start.11 = (f32[2,16,128]{2,1,0:T(8,128)S(1)}, f32[2,16,128]{2,1,0:T(8,128)S(1)}, u32[]{:S(2)}, u32[]{:S(2)}) collective-permute-start(f32[2,16,128]{2,1,0:T(8,128)S(1)} %get-tuple-element.22), channel_id=1, source_target_pairs={{1,2},{2,1},{3,4},{4,3},{5,6},{6,5},{7,8},{8,7},{9,10},{10,9},{11,... | collective-permute-start | bytes 49160 | tf_op jit(solution)/shard_map/ppermute | solution.py:388

commit v5 on v4

--- a/solution.py
+++ b/solution.py
@@ -16,14 +16,15 @@
 NB = 16
 HALF = WIN // 2
 LOCAL = 512
-ROWS = LOCAL + 16
+ROWS = LOCAL + 8
 SIDE = 4
 RING = (0, 1, 3, 2)
 BOTH = ("line", "tile")
 N_LINE = 8
 N_TILE = 16
 QUAD = 4
-PIECES = (0, 1792, 2816, MAXB * BR)
+OCT = 8
+PIECES = (0, 1408, 2432, MAXB * BR)
 STREAMS = 4
 WIDE = TZ * TX
 
@@ -62,7 +63,7 @@
         in_specs=[pl.BlockSpec(memory_space=pltpu.HBM)] * 3,
         out_specs=pl.BlockSpec(memory_space=pltpu.VMEM),
         scratch_shapes=[
-            pltpu.VMEM((16, WIN), jnp.float32),
+            pltpu.VMEM((8, WIN), jnp.float32),
             pltpu.VMEM((1, NB), jnp.int32),
             pltpu.VMEM((1, S), jnp.int32),
             pltpu.SemaphoreType.DMA((3,)),
@@ -150,10 +151,10 @@
     return jnp.where(place == 3, 2, jnp.where(place == 2, 3, place))
 
 
-def plan_kernel(own_ref, one_ref, three_ref, two_ref, plan_ref, cos_ref, sin_ref):
+def write_plan(main_refs, plan_ref, cos_ref, sin_ref, plan_copy):
     tile = lax.axis_index("tile")
     x, z, parity = tile >> 2, tile & 3, lax.axis_index("line") & 1
-    rows = [ref[i, LOCAL : LOCAL + 8, :].astype(jnp.float32) for ref in (own_ref, one_ref, three_ref, two_ref) for i in range(SIDE)]
+    rows = [ref[i, LOCAL : LOCAL + 8, :].astype(jnp.float32) for ref in main_refs for i in range(SIDE)]
     routes, codes = (jnp.concatenate([row[k : k + 1] for row in rows], 0) for k in range(2))
 
     def sender(place):
@@ -184,25 +185,14 @@
     entries = jnp.sum(entries, 0, keepdims=True)
     plan_ref[...] = jnp.concatenate([entries, starts, jnp.zeros((6, WIN), jnp.float32)], 0).astype(jnp.int32)
 
+    plan_copy.start()
     code_cols = jnp.concatenate([codes, jnp.zeros((WIN - N_TILE, WIN), jnp.float32)], 0).T[:S]
     angles = code_cols * (2.0 * jnp.pi / 256.0)
     cosines, sines = jnp.cos(angles), jnp.sin(angles)
     for place in range(N_TILE):
         cos_ref[place] = jnp.broadcast_to(cosines[:, place : place + 1], (S, BR))
         sin_ref[place] = jnp.broadcast_to(sines[:, place : place + 1], (S, BR))
-
-
-def planned(*mains):
-    vmem = pl.BlockSpec(memory_space=pltpu.VMEM)
-    turn = jax.ShapeDtypeStruct((N_TILE, S, BR), jnp.float32)
-    return pl.pallas_call(
-        plan_kernel,
-        out_shape=[jax.ShapeDtypeStruct((8, WIN), jnp.int32), turn, turn],
-        in_specs=[vmem] * SIDE,
-        out_specs=[vmem] * 3,
-        compiler_params=pltpu.CompilerParams(vmem_limit_bytes=8 * 2**20),
-        name="planned",
-    )(*(pltpu.with_memory_space_constraint(v, pltpu.VMEM) for v in mains))
+    plan_copy.wait()
 
 
 def interleave(real, imag):
@@ -212,13 +202,14 @@
     return jnp.concatenate(pieces, 0)
 
 
-def image_kernel(plan_ref, *refs):
+def image_kernel(*refs):
     main_refs = refs[:SIDE]
-    rim_ref, cos_ref, sin_ref, table_ref, matrix_ref, _, out_ref, held_ref = refs[SIDE : SIDE + 8]
-    slots_re, slots_im, total, sems = refs[SIDE + 8 :]
+    rim_ref, table_ref, matrix_ref, _, out_ref, held_ref = refs[SIDE : SIDE + 6]
+    slots_re, slots_im, total, plan_v, plan_ref, cos_ref, sin_ref, plan_sem, sems = refs[SIDE + 6 :]
     copies = piece_copies(2, matrix_ref, held_ref, sems)
     for copy in copies:
         copy.start()
+    write_plan(main_refs, plan_v, cos_ref, sin_ref, pltpu.make_async_copy(plan_v, plan_ref, plan_sem))
     count = plan_ref[1, SIDE]
 
     def make_slot(group, n):
@@ -248,52 +239,61 @@
             return carry
 
         lax.fori_loop(0, (end - start + QUAD - 1) >> 2, make_quad, 0)
-    for k in range(QUAD):
-        slots_re[count + k] = jnp.zeros((2 * S, BR), jnp.bfloat16)
-        slots_im[count + k] = jnp.zeros((2 * S, BR), jnp.bfloat16)
+
+    @pl.when((count & (OCT - 1)) != 0)
+    def _():
+        for k in range(OCT):
+            slots_re[count + k] = jnp.zeros((2 * S, BR), jnp.bfloat16)
+            slots_im[count + k] = jnp.zeros((2 * S, BR), jnp.bfloat16)
+
     total[...] = jnp.zeros_like(total)
     for copy in copies:
         copy.wait()
 
     def multiply(c, carry):
         at = []
-        for k in range(QUAD):
-            slot = plan_ref[0, jnp.minimum(QUAD * c + k, count - 1)] >> 12
+        for k in range(OCT):
+            slot = plan_ref[0, jnp.minimum(OCT * c + k, count - 1)] >> 12
             at.append(pl.ds(pl.multiple_of(slot * BR, BR), BR))
         matrix = jnp.concatenate([held_ref[part, rows, :] for part in range(2) for rows in at], 0)
-        beams = [ref[QUAD * c + k] for ref in (slots_re, slots_im) for k in range(QUAD)]
+        beams = [ref[OCT * c + k] for ref in (slots_re, slots_im) for k in range(OCT)]
         total[...] += jnp.dot(jnp.concatenate(beams, 1), matrix, preferred_element_type=jnp.float32)
         return carry
 
-    lax.fori_loop(0, (count + QUAD - 1) >> 2, multiply, 0)
+    lax.fori_loop(0, (count + OCT - 1) >> 3, multiply, 0)
     for d in range(N_LINE):
         for depth in range(TZ):
             out_ref[d, depth] = total[16 * d : 16 * d + 16, TX * depth : TX * depth + TX].astype(jnp.bfloat16)
 
 
-def partial_image(plan, mains, rims, turns, tables, beam_matrix, held):
-    smem, vmem = pl.BlockSpec(memory_space=pltpu.SMEM), pl.BlockSpec(memory_space=pltpu.VMEM)
-    fixed = [pltpu.with_memory_space_constraint(v, pltpu.VMEM) for v in (*mains, rims, *turns, tables)]
+def partial_image(mains, rims, tables, beam_matrix, held):
+    vmem = pl.BlockSpec(memory_space=pltpu.VMEM)
+    fixed = [pltpu.with_memory_space_constraint(v, pltpu.VMEM) for v in (*mains, rims, tables)]
     fixed.append(pltpu.with_memory_space_constraint(beam_matrix, pltpu.HBM))
-    room = MAXB + QUAD * 2
+    room = MAXB + OCT
     return pl.pallas_call(
         image_kernel,
         out_shape=[
             pltpu.VMEM((N_LINE, TZ, 16, TX), jnp.bfloat16),
             pltpu.VMEM((2, MAXB * BR, WIDE), jnp.bfloat16),
         ],
-        in_specs=[smem] + [vmem] * (len(fixed) - 1) + [pl.BlockSpec(memory_space=pltpu.HBM), vmem],
+        in_specs=[vmem] * (len(fixed) - 1) + [pl.BlockSpec(memory_space=pltpu.HBM), vmem],
         out_specs=[vmem] * 2,
         scratch_shapes=[
             pltpu.VMEM((room, 2 * S, BR), jnp.bfloat16),
             pltpu.VMEM((room, 2 * S, BR), jnp.bfloat16),
             pltpu.VMEM((2 * S, WIDE), jnp.float32),
+            pltpu.VMEM((8, WIN), jnp.int32),
+            pltpu.SMEM((8, WIN), jnp.int32),
+            pltpu.VMEM((N_TILE, S, BR), jnp.float32),
+            pltpu.VMEM((N_TILE, S, BR), jnp.float32),
+            pltpu.SemaphoreType.DMA,
             pltpu.SemaphoreType.DMA((2 * STREAMS,)),
         ],
-        input_output_aliases={1 + len(fixed): 1},
-        compiler_params=pltpu.CompilerParams(vmem_limit_bytes=6 * 2**20),
+        input_output_aliases={len(fixed): 1},
+        compiler_params=pltpu.CompilerParams(vmem_limit_bytes=8 * 2**20),
         name="partial_image",
-    )(plan, *fixed, pltpu.with_memory_space_constraint(held, pltpu.VMEM))[0]
+    )(*fixed, pltpu.with_memory_space_constraint(held, pltpu.VMEM))[0]
 
 
 def sum_kernel(parts_ref, out_ref, first_ref, second_ref):
@@ -312,7 +312,7 @@
 
 
 def summed_lines(parts):
-    shapes = [jax.ShapeDtypeStruct((rows, 16, TX), jnp.float32) for rows in (TZ, 2, 2)]
+    shapes = [pltpu.VMEM((rows, 16, TX), jnp.float32) for rows in (TZ, 2, 2)]
     return pl.pallas_call(
         sum_kernel,
         out_shape=shapes,
@@ -320,10 +320,10 @@
         out_specs=[pl.BlockSpec(memory_space=pltpu.VMEM)] * 3,
         compiler_params=pltpu.CompilerParams(vmem_limit_bytes=8 * 2**20),
         name="summed_lines",
-    )(parts)
-
-
-def add_filtered(filter_ref, results, sources):
+    )(pltpu.with_memory_space_constraint(parts, pltpu.VMEM))
+
+
+def add_filtered(tap, results, sources):
     lane = lax.broadcasted_iota(jnp.int32, (16, TX), 1)
     for side in range(5):
         move = side - 2
@@ -332,36 +332,57 @@
             if move:
                 row = jnp.where(inside, pltpu.roll(row, (-move) % TX, 1), 0.0)
             for depth in range(max(0, source - 4), min(TZ, source + 1)):
-                results[depth] = results[depth] + filter_ref[source - depth, side] * row
+                results[depth] = results[depth] + tap(source - depth, side) * row
     return results
 
 
-def inner_kernel(filter_ref, image_ref, out_ref):
+def inner_kernel(filter_ref, image_ref, out_ref, taps_ref):
     results = [jnp.zeros((16, TX), jnp.float32) for _ in range(TZ)]
-    results = add_filtered(filter_ref, results, [(depth + 2, image_ref[depth]) for depth in range(TZ)])
+    sources = [(depth + 2, image_ref[depth]) for depth in range(TZ)]
+    results = add_filtered(lambda down, side: filter_ref[down, side], results, sources)
     for depth in range(TZ):
         out_ref[depth] = results[depth]
-
-
-def outer_kernel(filter_ref, first_ref, inner_ref, second_ref, out_ref):
+    for down in range(5):
+        for side in range(5):
+            taps_ref[5 * down + side : 5 * down + side + 1] = jnp.full((1, TX), filter_ref[down, side], jnp.float32)
+
+
+def outer_kernel(taps_ref, first_ref, inner_ref, second_ref, out_ref):
     odd = (lax.axis_index("tile") & 1) == 1
     sources = [(row, jnp.where(odd, first_ref[row], second_ref[row])) for row in range(2)]
     sources += [(TZ + 2 + row, jnp.where(odd, second_ref[row], first_ref[row])) for row in range(2)]
-    results = add_filtered(filter_ref, [inner_ref[depth] for depth in range(TZ)], sources)
+    results = add_filtered(
+        lambda down, side: taps_ref[5 * down + side : 5 * down + side + 1],
+        [inner_ref[depth] for depth in range(TZ)],
+        sources,
+    )
     for depth in range(TZ):
         for part in range(2):
             out_ref[pl.ds(part * 64 + depth, 8, stride=TZ), :] = results[depth][8 * part : 8 * part + 8]
 
 
-def dip_call(kernel, shape, dip_filter, *arrays):
+def inner_filtered(dip_filter, image):
     vmem = pl.BlockSpec(memory_space=pltpu.VMEM)
     return pl.pallas_call(
-        kernel,
-        out_shape=jax.ShapeDtypeStruct(shape, jnp.float32),
-        in_specs=[pl.BlockSpec(memory_space=pltpu.SMEM)] + [vmem] * len(arrays),
+        inner_kernel,
+        out_shape=[pltpu.VMEM((TZ, 16, TX), jnp.float32), pltpu.VMEM((32, TX), jnp.float32)],
+        in_specs=[pl.BlockSpec(memory_space=pltpu.SMEM), vmem],
+        out_specs=[vmem] * 2,
+        compiler_params=pltpu.CompilerParams(vmem_limit_bytes=2 * 2**20),
+        name="inner_filtered",
+    )(dip_filter, pltpu.with_memory_space_constraint(image, pltpu.VMEM))
+
+
+def outer_filtered(*arrays):
+    vmem = pl.BlockSpec(memory_space=pltpu.VMEM)
+    return pl.pallas_call(
+        outer_kernel,
+        out_shape=jax.ShapeDtypeStruct((2 * 8 * TZ, TX), jnp.float32),
+        in_specs=[vmem] * len(arrays),
         out_specs=vmem,
         compiler_params=pltpu.CompilerParams(vmem_limit_bytes=2 * 2**20),
-    )(dip_filter, *arrays)
+        name="outer_filtered",
+    )(*(pltpu.with_memory_space_constraint(v, pltpu.VMEM) for v in arrays))
 
 
 def spread(value, x_first, offsets=RING[1:]):
@@ -375,18 +396,17 @@
     main = first_rows(traces, routes, codes)
     near = jnp.stack([main] + spread(main, False))
     mains = [near] + spread(near, True)
-    plan, *turns = planned(*mains)
     tables, held = slant_tables(beam_matrix)
     rim = lax.ppermute(near[:, :HALF], "line", [(i + 1, i) for i in range(N_LINE - 1)])
     rims = jnp.stack([rim] + spread(rim, False))
     held = held_more(beam_matrix, held)
-    image = partial_image(plan, mains, rims, turns, tables, beam_matrix, held)
+    image = partial_image(mains, rims, tables, beam_matrix, held)
     parts = lax.all_to_all(image, "line", 0, 0, tiled=True)
     image, first, second = summed_lines(parts)
-    inner = dip_call(inner_kernel, (TZ, 16, TX), dip_filter, image)
+    inner, taps = inner_filtered(dip_filter, image)
     first = lax.ppermute(first, "tile", [(i, i ^ 1) for i in range(N_TILE)])
     second = lax.ppermute(second, "tile", [(i, ((i - 1) ^ 1) + 1) for i in range(1, N_TILE - 1)])
-    return dip_call(outer_kernel, (2 * 8 * TZ, TX), dip_filter, first, inner, second).reshape(2, 8, TZ, TX)
+    return outer_filtered(taps, first, inner, second).reshape(2, 8, TZ, TX)
 
 
 def solution(mesh):

time: 61.8 us -> 59.6 us (0.964)
  Pallas kernels: 14.6 us -> 12.7 us
    pallas_call x3 -> x2, Pallas kernels: 2.72 us -> 1.49 us  [the longest x1 0.76 us: inner_filtered(): pl.pallas_call(inner_kernel, out_shape=[pltpu.VMEM((TZ, 16, TX), jnp.floa...]
where the time goes in v5:
time: 59.6 us; the launch traced here: 59.4 us
  starting transfers between devices  21.7 us (36%)
  waiting for transfers between devices  13.1 us (22%)
  Pallas kernels  12.7 us (21%)
  blocking collectives  11.8 us (20%)
    ppermute x9, starting transfers between devices, spread(): received.append(lax.ppermute(value, BOTH, hops(offset, x_first)))  13.8 us
    all_to_all x1, blocking collectives, per_device(): parts = lax.all_to_all(image, 'line', 0, 0, tiled=True)  11.8 us
    ppermute x9, waiting for transfers between devices, spread(): received.append(lax.ppermute(value, BOTH, hops(offset, x_first)))  7.89 us
    pallas_call x1, Pallas kernels, partial_image(): pl.pallas_call(image_kernel, out_shape=[pltpu.VMEM((N_LINE, TZ, 16, TX),...  5.28 us
    ppermute x1, starting transfers between devices, per_device(): lax.ppermute(second, 'tile', [(i, (i - 1 ^ 1) + 1) for i in range(1, N_TI...  3.63 us
    ppermute x1, waiting for transfers between devices, per_device(): lax.ppermute(second, 'tile', [(i, (i - 1 ^ 1) + 1) for i in range(1, N_TI...  3.3 us
    ppermute x1, starting transfers between devices, per_device(): first = lax.ppermute(first, 'tile', [(i, i ^ 1) for i in range(N_TILE)])  2.95 us
    pallas_call x1, Pallas kernels, slant_tables(): pl.pallas_call(table_kernel, out_shape=[pltpu.VMEM((2 * N_TILE, WIN, 2 *...  2.7 us
  transfers between devices with their start and end apart: 12, of which 6 were waited for; matrix products, arithmetic and copies ran while one was open for 0% of the time, Pallas kernels for 10%

profile of v5, /device:TPU:2, one launch (start us, length us, event | category | flops | bytes accessed | tf_op | source)
XLA Modules:
  0.0 59.4 jit_solution(10667959922858325061)
XLA Ops:
  0.0 0.9 %first_rows.1 = bf16[520,128]{1,0:T(8,128)(2,1)S(1)} custom-call(bf16[1,512,128]{2,1,0:T(8,128)(2,1)} %traces_ref.1, s32[1,16]{1,0:T(1,128)} %routes_ref.1, s32[1,64]{1,0:T(1,128)} %codes_ref.1), custom_call_target="tpu_custom_call" | custom-call | tf_op jit(solution)/shard_map/first_rows/pallas_call | solution.py:60
  1.0 4.0 %collective-permute-start.2 = (bf16[520,128]{1,0:T(8,128)(2,1)S(1)}, bf16[520,128]{1,0:T(8,128)(2,1)S(1)}, u32[]{:S(2)}, u32[]{:S(2)}) collective-permute-start(bf16[520,128]{1,0:T(8,128)(2,1)S(1)} %first_rows.1), channel_id=1, source_target_pairs={{0,2},{1,3},{2,0},{3,1},{4,6},{5,7},{6,4},{7,5},{8,10},{9,11},{10,... | collective-permute-start | bytes 399368 | tf_op jit(solution)/shard_map/ppermute | solution.py:391
  4.9 0.7 %collective-permute-start.1 = (bf16[520,128]{1,0:T(8,128)(2,1)S(1)}, bf16[520,128]{1,0:T(8,128)(2,1)S(1)}, u32[]{:S(2)}, u32[]{:S(2)}) collective-permute-start(bf16[520,128]{1,0:T(8,128)(2,1)S(1)} %first_rows.1), channel_id=1, source_target_pairs={{0,3},{1,0},{2,1},{3,2},{4,7},{5,4},{6,5},{7,6},{8,11},{9,8},{10,9... | collective-permute-start | bytes 399368 | tf_op jit(solution)/shard_map/ppermute | solution.py:391
  5.6 1.3 %collective-permute-start = (bf16[520,128]{1,0:T(8,128)(2,1)S(1)}, bf16[520,128]{1,0:T(8,128)(2,1)S(1)}, u32[]{:S(2)}, u32[]{:S(2)}) collective-permute-start(bf16[520,128]{1,0:T(8,128)(2,1)S(1)} %first_rows.1), channel_id=1, source_target_pairs={{0,1},{1,2},{2,3},{3,0},{4,5},{5,6},{6,7},{7,4},{8,9},{9,10},{10,1... | collective-permute-start | bytes 399368 | tf_op jit(solution)/shard_map/ppermute | solution.py:391
  6.9 0.9 %collective-permute-done.2 = bf16[520,128]{1,0:T(8,128)(2,1)S(1)} collective-permute-done((bf16[520,128]{1,0:T(8,128)(2,1)S(1)}, bf16[520,128]{1,0:T(8,128)(2,1)S(1)}, u32[]{:S(2)}, u32[]{:S(2)}) %collective-permute-start.2) | collective-permute-done | bytes 133152 | tf_op jit(solution)/shard_map/ppermute | solution.py:391
  7.9 2.4 %collective-permute-done.1 = bf16[520,128]{1,0:T(8,128)(2,1)S(1)} collective-permute-done((bf16[520,128]{1,0:T(8,128)(2,1)S(1)}, bf16[520,128]{1,0:T(8,128)(2,1)S(1)}, u32[]{:S(2)}, u32[]{:S(2)}) %collective-permute-start.1) | collective-permute-done | bytes 133152 | tf_op jit(solution)/shard_map/ppermute | solution.py:391
  10.3 1.5 %collective-permute-done = bf16[520,128]{1,0:T(8,128)(2,1)S(1)} collective-permute-done((bf16[520,128]{1,0:T(8,128)(2,1)S(1)}, bf16[520,128]{1,0:T(8,128)(2,1)S(1)}, u32[]{:S(2)}, u32[]{:S(2)}) %collective-permute-start) | collective-permute-done | bytes 133152 | tf_op jit(solution)/shard_map/ppermute | solution.py:391
  11.9 2.2 %collective-permute-start.5 = (bf16[4,520,128]{2,1,0:T(8,128)(2,1)S(1)}, bf16[4,520,128]{2,1,0:T(8,128)(2,1)S(1)}, u32[]{:S(2)}, u32[]{:S(2)}) collective-permute-start(bf16[4,520,128]{2,1,0:T(8,128)(2,1)S(1)} %pad_maximum_fusion.refs_0_), channel_id=1, source_target_pairs={{0,8},{1,9},{2,10},{3,11},{4,12},{5,13},{6,14},{7,15},{8,0},{9,1},... | collective-permute-start | bytes 1597448 | tf_op jit(solution)/shard_map/ppermute | solution.py:391
  14.1 1.4 %collective-permute-start.4 = (bf16[4,520,128]{2,1,0:T(8,128)(2,1)S(1)}, bf16[4,520,128]{2,1,0:T(8,128)(2,1)S(1)}, u32[]{:S(2)}, u32[]{:S(2)}) collective-permute-start(bf16[4,520,128]{2,1,0:T(8,128)(2,1)S(1)} %pad_maximum_fusion.refs_0_), channel_id=1, source_target_pairs={{0,12},{1,13},{2,14},{3,15},{4,0},{5,1},{6,2},{7,3},{8,4},{9,5},{1... | collective-permute-start | bytes 1597448 | tf_op jit(solution)/shard_map/ppermute | solution.py:391
  16.1 1.3 %collective-permute-start.6 = (bf16[4,64,128]{2,1,0:T(8,128)(2,1)S(1)}, bf16[4,64,128]{2,1,0:T(8,128)(2,1)S(1)}, u32[]{:S(2)}, u32[]{:S(2)}) collective-permute-start(bf16[4,64,128]{2,1,0:T(8,128)(2,1)S(1)} %slice.4), channel_id=1, source_target_pairs={{16,0},{32,16},{48,32},{64,48},{80,64},{96,80},{112,96},{17,1},{33... | collective-permute-start | bytes 196616 | tf_op jit(solution)/shard_map/ppermute | solution.py:400
  17.4 1.8 %collective-permute-done.6 = bf16[4,64,128]{2,1,0:T(8,128)(2,1)S(1)} collective-permute-done((bf16[4,64,128]{2,1,0:T(8,128)(2,1)S(1)}, bf16[4,64,128]{2,1,0:T(8,128)(2,1)S(1)}, u32[]{:S(2)}, u32[]{:S(2)}) %collective-permute-start.6) | collective-permute-done | bytes 65568 | tf_op jit(solution)/shard_map/ppermute | solution.py:400
  19.3 1.2 %collective-permute-start.9 = (bf16[4,64,128]{2,1,0:T(8,128)(2,1)S(1)}, bf16[4,64,128]{2,1,0:T(8,128)(2,1)S(1)}, u32[]{:S(2)}, u32[]{:S(2)}) collective-permute-start(bf16[4,64,128]{2,1,0:T(8,128)(2,1)S(1)} %collective-permute-done.6), channel_id=1, source_target_pairs={{0,2},{1,3},{2,0},{3,1},{4,6},{5,7},{6,4},{7,5},{8,10},{9,11},{10,... | collective-permute-start | bytes 196616 | tf_op jit(solution)/shard_map/ppermute | solution.py:391
  20.4 1.6 %collective-permute-start.8 = (bf16[4,64,128]{2,1,0:T(8,128)(2,1)S(1)}, bf16[4,64,128]{2,1,0:T(8,128)(2,1)S(1)}, u32[]{:S(2)}, u32[]{:S(2)}) collective-permute-start(bf16[4,64,128]{2,1,0:T(8,128)(2,1)S(1)} %collective-permute-done.6), channel_id=1, source_target_pairs={{0,3},{1,0},{2,1},{3,2},{4,7},{5,4},{6,5},{7,6},{8,11},{9,8},{10,9... | collective-permute-start | bytes 196616 | tf_op jit(solution)/shard_map/ppermute | solution.py:391
  22.0 3.0 %collective-permute-done.9 = bf16[4,64,128]{2,1,0:T(8,128)(2,1)S(1)} collective-permute-done((bf16[4,64,128]{2,1,0:T(8,128)(2,1)S(1)}, bf16[4,64,128]{2,1,0:T(8,128)(2,1)S(1)}, u32[]{:S(2)}, u32[]{:S(2)}) %collective-permute-start.9) | collective-permute-done | bytes 65568 | tf_op jit(solution)/shard_map/ppermute | solution.py:391
  25.0 0.8 %collective-permute-start.7 = (bf16[4,64,128]{2,1,0:T(8,128)(2,1)S(1)}, bf16[4,64,128]{2,1,0:T(8,128)(2,1)S(1)}, u32[]{:S(2)}, u32[]{:S(2)}) collective-permute-start(bf16[4,64,128]{2,1,0:T(8,128)(2,1)S(1)} %collective-permute-done.6), channel_id=1, source_target_pairs={{0,1},{1,2},{2,3},{3,0},{4,5},{5,6},{6,7},{7,4},{8,9},{9,10},{10,1... | collective-permute-start | bytes 196616 | tf_op jit(solution)/shard_map/ppermute | solution.py:391
  25.8 2.7 %slant_tables.1 = (bf16[32,128,256]{2,1,0:T(8,128)(2,1)S(1)}, bf16[2,4096,1024]{2,1,0:T(8,128)(2,1)S(1)}) custom-call(bf16[1,1,2,4096,1024]{4,3,2,1,0:T(8,128)(2,1)} %refs_6_.1), custom_call_target="tpu_custom_call" | custom-call | tf_op jit(solution)/shard_map/slant_tables/pallas_call | solution.py:103
  28.5 2.2 %held_more.1.refs_7_ = bf16[2,4096,1024]{2,1,0:T(8,128)(2,1)S(1)} custom-call(bf16[1,1,2,4096,1024]{4,3,2,1,0:T(8,128)(2,1)} %refs_6_.1, bf16[2,4096,1024]{2,1,0:T(8,128)(2,1)S(1)} %get-tuple-element.14.before_ref), custom_call_target="tpu_custom_call", output_to_operand_aliasing={{}: (1, {})} | custom-call | tf_op jit(solution)/shard_map/held_more/pallas_call | solution.py:138
  30.9 5.3 %partial_image.1 = (bf16[8,8,16,128]{3,2,1,0:T(8,128)(2,1)S(1)}, bf16[2,4096,1024]{2,1,0:T(8,128)(2,1)S(1)}) custom-call(bf16[4,520,128]{2,1,0:T(8,128)(2,1)S(1)} %pad_maximum_fusion.refs_0_, bf16[4,520,128]{2,1,0:T(8,128)(2,1)S(1)} %collective-permute-done.3.refs_1_, ...), custom_call_target="tpu_custom_call", output_to_operand_aliasing={{1}: (7, {})} | custom-call | tf_op jit(solution)/shard_map/partial_image/pallas_call | solution.py:274
  36.2 11.8 %all_to_all.5.parts_ref = bf16[8,8,16,128]{3,2,1,0:T(8,128)(2,1)S(1)} all-to-all(bf16[8,8,16,128]{3,2,1,0:T(8,128)(2,1)S(1)} %get-tuple-element.15), channel_id=1, replica_groups=mesh['line'=8,'tile'=16] {'line'}, dimensions={0} | all-to-all | bytes 524288 | tf_op jit(solution)/shard_map/all_to_all | solution.py:404
  48.0 3.0 %collective-permute-start.10 = (f32[2,16,128]{2,1,0:T(8,128)S(1)}, f32[2,16,128]{2,1,0:T(8,128)S(1)}, u32[]{:S(2)}, u32[]{:S(2)}) collective-permute-start(f32[2,16,128]{2,1,0:T(8,128)S(1)} %get-tuple-element.18), channel_id=1, source_target_pairs={{0,1},{1,0},{2,3},{3,2},{4,5},{5,4},{6,7},{7,6},{8,9},{9,8},{10,11... | collective-permute-start | bytes 49160 | tf_op jit(solution)/shard_map/ppermute | solution.py:407
  51.0 3.6 %collective-permute-start.11 = (f32[2,16,128]{2,1,0:T(8,128)S(1)}, f32[2,16,128]{2,1,0:T(8,128)S(1)}, u32[]{:S(2)}, u32[]{:S(2)}) collective-permute-start(f32[2,16,128]{2,1,0:T(8,128)S(1)} %get-tuple-element.20), channel_id=1, source_target_pairs={{1,2},{2,1},{3,4},{4,3},{5,6},{6,5},{7,8},{8,7},{9,10},{10,9},{11,... | collective-permute-start | bytes 49160 | tf_op jit(solution)/shard_map/ppermute | solution.py:408
  54.6 0.8 %inner_filtered.1 = (f32[8,16,128]{2,1,0:T(8,128)S(1)}, f32[32,128]{1,0:T(8,128)S(1)}) custom-call(f32[5,5]{1,0:T(8,128)S(1)} %copy-done, f32[8,16,128]{2,1,0:T(8,128)S(1)} %get-tuple-element.16.image_ref), custom_call_target="tpu_custom_call" | custom-call | tf_op jit(solution)/shard_map/inner_filtered/pallas_call | solution.py:366
  55.4 3.3 %collective-permute-done.11.second_ref = f32[2,16,128]{2,1,0:T(8,128)S(1)} collective-permute-done((f32[2,16,128]{2,1,0:T(8,128)S(1)}, f32[2,16,128]{2,1,0:T(8,128)S(1)}, u32[]{:S(2)}, u32[]{:S(2)}) %collective-permute-start.11) | collective-permute-done | bytes 16416 | tf_op jit(solution)/shard_map/ppermute | solution.py:408
  58.7 0.7 %outer_filtered.1 = f32[128,128]{1,0:T(8,128)} custom-call(f32[32,128]{1,0:T(8,128)S(1)} %get-tuple-element.17.taps_ref, f32[2,16,128]{2,1,0:T(8,128)S(1)} %collective-permute-done.10.first_ref, f32[8,16,128]{2,1,0:T(8,128)S(1)} %get-tuple-element.19.inner_ref, f32[2,16,128]{2,1,0:T(8,128)S(1)} %collective-permute-done.11.second_ref), custom_call_target="tpu_custom_call" | custom-call | tf_op jit(solution)/shard_map/outer_filtered/pallas_call | solution.py:378
  (13 shorter events, 0.8 us)
Async XLA Ops:
  1.0 6.9 %collective-permute-start.2 = (bf16[520,128]{1,0:T(8,128)(2,1)S(1)}, bf16[520,128]{1,0:T(8,128)(2,1)S(1)}, u32[]{:S(2)}, u32[]{:S(2)}) collective-permute-start(bf16[520,128]{1,0:T(8,128)(2,1)S(1)} %first_rows.1), channel_id=1, source_target_pairs={{0,2},{1,3},{2,0},{3,1},{4,6},{5,7},{6,4},{7,5},{8,10},{9,11},{10,... | collective-permute-start | bytes 399368 | tf_op jit(solution)/shard_map/ppermute | solution.py:391
  4.9 5.4 %collective-permute-start.1 = (bf16[520,128]{1,0:T(8,128)(2,1)S(1)}, bf16[520,128]{1,0:T(8,128)(2,1)S(1)}, u32[]{:S(2)}, u32[]{:S(2)}) collective-permute-start(bf16[520,128]{1,0:T(8,128)(2,1)S(1)} %first_rows.1), channel_id=1, source_target_pairs={{0,3},{1,0},{2,1},{3,2},{4,7},{5,4},{6,5},{7,6},{8,11},{9,8},{10,9... | collective-permute-start | bytes 399368 | tf_op jit(solution)/shard_map/ppermute | solution.py:391
  5.6 6.2 %collective-permute-start = (bf16[520,128]{1,0:T(8,128)(2,1)S(1)}, bf16[520,128]{1,0:T(8,128)(2,1)S(1)}, u32[]{:S(2)}, u32[]{:S(2)}) collective-permute-start(bf16[520,128]{1,0:T(8,128)(2,1)S(1)} %first_rows.1), channel_id=1, source_target_pairs={{0,1},{1,2},{2,3},{3,0},{4,5},{5,6},{6,7},{7,4},{8,9},{9,10},{10,1... | collective-permute-start | bytes 399368 | tf_op jit(solution)/shard_map/ppermute | solution.py:391
  11.9 18.9 %collective-permute-start.5 = (bf16[4,520,128]{2,1,0:T(8,128)(2,1)S(1)}, bf16[4,520,128]{2,1,0:T(8,128)(2,1)S(1)}, u32[]{:S(2)}, u32[]{:S(2)}) collective-permute-start(bf16[4,520,128]{2,1,0:T(8,128)(2,1)S(1)} %pad_maximum_fusion.refs_0_), channel_id=1, source_target_pairs={{0,8},{1,9},{2,10},{3,11},{4,12},{5,13},{6,14},{7,15},{8,0},{9,1},... | collective-permute-start | bytes 1597448 | tf_op jit(solution)/shard_map/ppermute | solution.py:391
  14.1 16.8 %collective-permute-start.4 = (bf16[4,520,128]{2,1,0:T(8,128)(2,1)S(1)}, bf16[4,520,128]{2,1,0:T(8,128)(2,1)S(1)}, u32[]{:S(2)}, u32[]{:S(2)}) collective-permute-start(bf16[4,520,128]{2,1,0:T(8,128)(2,1)S(1)} %pad_maximum_fusion.refs_0_), channel_id=1, source_target_pairs={{0,12},{1,13},{2,14},{3,15},{4,0},{5,1},{6,2},{7,3},{8,4},{9,5},{1... | collective-permute-start | bytes 1597448 | tf_op jit(solution)/shard_map/ppermute | solution.py:391
  15.5 15.3 %collective-permute-start.3 = (bf16[4,520,128]{2,1,0:T(8,128)(2,1)S(1)}, bf16[4,520,128]{2,1,0:T(8,128)(2,1)S(1)}, u32[]{:S(2)}, u32[]{:S(2)}) collective-permute-start(bf16[4,520,128]{2,1,0:T(8,128)(2,1)S(1)} %pad_maximum_fusion.refs_0_), channel_id=1, source_target_pairs={{0,4},{1,5},{2,6},{3,7},{4,8},{5,9},{6,10},{7,11},{8,12},{9,13},{1... | collective-permute-start | bytes 1597448 | tf_op jit(solution)/shard_map/ppermute | solution.py:391
  16.1 3.1 %collective-permute-start.6 = (bf16[4,64,128]{2,1,0:T(8,128)(2,1)S(1)}, bf16[4,64,128]{2,1,0:T(8,128)(2,1)S(1)}, u32[]{:S(2)}, u32[]{:S(2)}) collective-permute-start(bf16[4,64,128]{2,1,0:T(8,128)(2,1)S(1)} %slice.4), channel_id=1, source_target_pairs={{16,0},{32,16},{48,32},{64,48},{80,64},{96,80},{112,96},{17,1},{33... | collective-permute-start | bytes 196616 | tf_op jit(solution)/shard_map/ppermute | solution.py:400
  19.3 5.8 %collective-permute-start.9 = (bf16[4,64,128]{2,1,0:T(8,128)(2,1)S(1)}, bf16[4,64,128]{2,1,0:T(8,128)(2,1)S(1)}, u32[]{:S(2)}, u32[]{:S(2)}) collective-permute-start(bf16[4,64,128]{2,1,0:T(8,128)(2,1)S(1)} %collective-permute-done.6), channel_id=1, source_target_pairs={{0,2},{1,3},{2,0},{3,1},{4,6},{5,7},{6,4},{7,5},{8,10},{9,11},{10,... | collective-permute-start | bytes 196616 | tf_op jit(solution)/shard_map/ppermute | solution.py:391
  20.4 10.3 %collective-permute-start.8 = (bf16[4,64,128]{2,1,0:T(8,128)(2,1)S(1)}, bf16[4,64,128]{2,1,0:T(8,128)(2,1)S(1)}, u32[]{:S(2)}, u32[]{:S(2)}) collective-permute-start(bf16[4,64,128]{2,1,0:T(8,128)(2,1)S(1)} %collective-permute-done.6), channel_id=1, source_target_pairs={{0,3},{1,0},{2,1},{3,2},{4,7},{5,4},{6,5},{7,6},{8,11},{9,8},{10,9... | collective-permute-start | bytes 196616 | tf_op jit(solution)/shard_map/ppermute | solution.py:391
  25.0 5.8 %collective-permute-start.7 = (bf16[4,64,128]{2,1,0:T(8,128)(2,1)S(1)}, bf16[4,64,128]{2,1,0:T(8,128)(2,1)S(1)}, u32[]{:S(2)}, u32[]{:S(2)}) collective-permute-start(bf16[4,64,128]{2,1,0:T(8,128)(2,1)S(1)} %collective-permute-done.6), channel_id=1, source_target_pairs={{0,1},{1,2},{2,3},{3,0},{4,5},{5,6},{6,7},{7,4},{8,9},{9,10},{10,1... | collective-permute-start | bytes 196616 | tf_op jit(solution)/shard_map/ppermute | solution.py:391
  30.9 23.7 %copy-start = (f32[5,5]{1,0:T(8,128)S(1)}, f32[5,5]{1,0:T(8,128)}, u32[]{:S(2)}) copy-start(f32[5,5]{1,0:T(8,128)} %filter_ref.1) | copy-start | bytes 304
  48.0 7.4 %collective-permute-start.10 = (f32[2,16,128]{2,1,0:T(8,128)S(1)}, f32[2,16,128]{2,1,0:T(8,128)S(1)}, u32[]{:S(2)}, u32[]{:S(2)}) collective-permute-start(f32[2,16,128]{2,1,0:T(8,128)S(1)} %get-tuple-element.18), channel_id=1, source_target_pairs={{0,1},{1,0},{2,3},{3,2},{4,5},{5,4},{6,7},{7,6},{8,9},{9,8},{10,11... | collective-permute-start | bytes 49160 | tf_op jit(solution)/shard_map/ppermute | solution.py:407
  51.0 7.7 %collective-permute-start.11 = (f32[2,16,128]{2,1,0:T(8,128)S(1)}, f32[2,16,128]{2,1,0:T(8,128)S(1)}, u32[]{:S(2)}, u32[]{:S(2)}) collective-permute-start(f32[2,16,128]{2,1,0:T(8,128)S(1)} %get-tuple-element.20), channel_id=1, source_target_pairs={{1,2},{2,1},{3,4},{4,3},{5,6},{6,5},{7,8},{8,7},{9,10},{10,9},{11,... | collective-permute-start | bytes 49160 | tf_op jit(solution)/shard_map/ppermute | solution.py:408

commit v6 on v5

--- a/solution.py
+++ b/solution.py
@@ -24,7 +24,7 @@
 N_TILE = 16
 QUAD = 4
 OCT = 8
-PIECES = (0, 1408, 2432, MAXB * BR)
+PIECES = (0, 1152, 2176, MAXB * BR)
 STREAMS = 4
 WIDE = TZ * TX
 
@@ -49,11 +49,12 @@
     for copy in copies:
         copy.start()
     rows[...] = jnp.zeros_like(rows)
-    for copy in copies:
+    for copy in copies[1:]:
         copy.wait()
     rows[0:1, :NB] = routes_v[...].astype(jnp.float32)
     rows[1:2, :S] = codes_v[...].astype(jnp.float32)
     main_ref[LOCAL:] = rows[...].astype(jnp.bfloat16)
+    copies[0].wait()
 
 
 def first_rows(traces, routes, codes):

time: 59.6 us -> 59.3 us (level)
  transfers between devices with their start and end apart: 12 -> 12, of which waited for: 6 -> 6; matrix products, arithmetic and copies ran while one was open for 0% -> 0% of each run, Pallas kernels for 10% -> 9%
where the time goes in v6:
time: 59.3 us; the launch traced here: 59.1 us
  starting transfers between devices  21.7 us (37%)
  waiting for transfers between devices  12.8 us (22%)
  Pallas kernels  12.6 us (21%)
  blocking collectives  11.8 us (20%)
    ppermute x9, starting transfers between devices, spread(): received.append(lax.ppermute(value, BOTH, hops(offset, x_first)))  13.8 us
    all_to_all x1, blocking collectives, per_device(): parts = lax.all_to_all(image, 'line', 0, 0, tiled=True)  11.8 us
    ppermute x9, waiting for transfers between devices, spread(): received.append(lax.ppermute(value, BOTH, hops(offset, x_first)))  7.94 us
    pallas_call x1, Pallas kernels, partial_image(): pl.pallas_call(image_kernel, out_shape=[pltpu.VMEM((N_LINE, TZ, 16, TX),...  5.58 us
    ppermute x1, starting transfers between devices, per_device(): lax.ppermute(second, 'tile', [(i, (i - 1 ^ 1) + 1) for i in range(1, N_TI...  3.94 us
    ppermute x1, waiting for transfers between devices, per_device(): lax.ppermute(second, 'tile', [(i, (i - 1 ^ 1) + 1) for i in range(1, N_TI...  2.99 us
    ppermute x1, starting transfers between devices, per_device(): first = lax.ppermute(first, 'tile', [(i, i ^ 1) for i in range(N_TILE)])  2.65 us
    pallas_call x1, Pallas kernels, slant_tables(): pl.pallas_call(table_kernel, out_shape=[pltpu.VMEM((2 * N_TILE, WIN, 2 *...  2.38 us
  transfers between devices with their start and end apart: 12, of which 6 were waited for; matrix products, arithmetic and copies ran while one was open for 0% of the time, Pallas kernels for 9%

profile of v6, /device:TPU:2, one launch (start us, length us, event | category | flops | bytes accessed | tf_op | source)
XLA Modules:
  0.0 59.1 jit_solution(12923484345295546055)
XLA Ops:
  0.0 0.9 %first_rows.1 = bf16[520,128]{1,0:T(8,128)(2,1)S(1)} custom-call(bf16[1,512,128]{2,1,0:T(8,128)(2,1)} %traces_ref.1, s32[1,16]{1,0:T(1,128)} %routes_ref.1, s32[1,64]{1,0:T(1,128)} %codes_ref.1), custom_call_target="tpu_custom_call" | custom-call | tf_op jit(solution)/shard_map/first_rows/pallas_call | solution.py:61
  0.9 4.0 %collective-permute-start.2 = (bf16[520,128]{1,0:T(8,128)(2,1)S(1)}, bf16[520,128]{1,0:T(8,128)(2,1)S(1)}, u32[]{:S(2)}, u32[]{:S(2)}) collective-permute-start(bf16[520,128]{1,0:T(8,128)(2,1)S(1)} %first_rows.1), channel_id=1, source_target_pairs={{0,2},{1,3},{2,0},{3,1},{4,6},{5,7},{6,4},{7,5},{8,10},{9,11},{10,... | collective-permute-start | bytes 399368 | tf_op jit(solution)/shard_map/ppermute | solution.py:392
  4.9 0.7 %collective-permute-start.1 = (bf16[520,128]{1,0:T(8,128)(2,1)S(1)}, bf16[520,128]{1,0:T(8,128)(2,1)S(1)}, u32[]{:S(2)}, u32[]{:S(2)}) collective-permute-start(bf16[520,128]{1,0:T(8,128)(2,1)S(1)} %first_rows.1), channel_id=1, source_target_pairs={{0,3},{1,0},{2,1},{3,2},{4,7},{5,4},{6,5},{7,6},{8,11},{9,8},{10,9... | collective-permute-start | bytes 399368 | tf_op jit(solution)/shard_map/ppermute | solution.py:392
  5.6 1.3 %collective-permute-start = (bf16[520,128]{1,0:T(8,128)(2,1)S(1)}, bf16[520,128]{1,0:T(8,128)(2,1)S(1)}, u32[]{:S(2)}, u32[]{:S(2)}) collective-permute-start(bf16[520,128]{1,0:T(8,128)(2,1)S(1)} %first_rows.1), channel_id=1, source_target_pairs={{0,1},{1,2},{2,3},{3,0},{4,5},{5,6},{6,7},{7,4},{8,9},{9,10},{10,1... | collective-permute-start | bytes 399368 | tf_op jit(solution)/shard_map/ppermute | solution.py:392
  6.9 0.9 %collective-permute-done.2 = bf16[520,128]{1,0:T(8,128)(2,1)S(1)} collective-permute-done((bf16[520,128]{1,0:T(8,128)(2,1)S(1)}, bf16[520,128]{1,0:T(8,128)(2,1)S(1)}, u32[]{:S(2)}, u32[]{:S(2)}) %collective-permute-start.2) | collective-permute-done | bytes 133152 | tf_op jit(solution)/shard_map/ppermute | solution.py:392
  7.9 2.4 %collective-permute-done.1 = bf16[520,128]{1,0:T(8,128)(2,1)S(1)} collective-permute-done((bf16[520,128]{1,0:T(8,128)(2,1)S(1)}, bf16[520,128]{1,0:T(8,128)(2,1)S(1)}, u32[]{:S(2)}, u32[]{:S(2)}) %collective-permute-start.1) | collective-permute-done | bytes 133152 | tf_op jit(solution)/shard_map/ppermute | solution.py:392
  10.3 1.5 %collective-permute-done = bf16[520,128]{1,0:T(8,128)(2,1)S(1)} collective-permute-done((bf16[520,128]{1,0:T(8,128)(2,1)S(1)}, bf16[520,128]{1,0:T(8,128)(2,1)S(1)}, u32[]{:S(2)}, u32[]{:S(2)}) %collective-permute-start) | collective-permute-done | bytes 133152 | tf_op jit(solution)/shard_map/ppermute | solution.py:392
  11.9 2.2 %collective-permute-start.5 = (bf16[4,520,128]{2,1,0:T(8,128)(2,1)S(1)}, bf16[4,520,128]{2,1,0:T(8,128)(2,1)S(1)}, u32[]{:S(2)}, u32[]{:S(2)}) collective-permute-start(bf16[4,520,128]{2,1,0:T(8,128)(2,1)S(1)} %pad_maximum_fusion.refs_0_), channel_id=1, source_target_pairs={{0,8},{1,9},{2,10},{3,11},{4,12},{5,13},{6,14},{7,15},{8,0},{9,1},... | collective-permute-start | bytes 1597448 | tf_op jit(solution)/shard_map/ppermute | solution.py:392
  14.1 1.4 %collective-permute-start.4 = (bf16[4,520,128]{2,1,0:T(8,128)(2,1)S(1)}, bf16[4,520,128]{2,1,0:T(8,128)(2,1)S(1)}, u32[]{:S(2)}, u32[]{:S(2)}) collective-permute-start(bf16[4,520,128]{2,1,0:T(8,128)(2,1)S(1)} %pad_maximum_fusion.refs_0_), channel_id=1, source_target_pairs={{0,12},{1,13},{2,14},{3,15},{4,0},{5,1},{6,2},{7,3},{8,4},{9,5},{1... | collective-permute-start | bytes 1597448 | tf_op jit(solution)/shard_map/ppermute | solution.py:392
  16.1 1.3 %collective-permute-start.6 = (bf16[4,64,128]{2,1,0:T(8,128)(2,1)S(1)}, bf16[4,64,128]{2,1,0:T(8,128)(2,1)S(1)}, u32[]{:S(2)}, u32[]{:S(2)}) collective-permute-start(bf16[4,64,128]{2,1,0:T(8,128)(2,1)S(1)} %slice.4), channel_id=1, source_target_pairs={{16,0},{32,16},{48,32},{64,48},{80,64},{96,80},{112,96},{17,1},{33... | collective-permute-start | bytes 196616 | tf_op jit(solution)/shard_map/ppermute | solution.py:401
  17.4 1.8 %collective-permute-done.6 = bf16[4,64,128]{2,1,0:T(8,128)(2,1)S(1)} collective-permute-done((bf16[4,64,128]{2,1,0:T(8,128)(2,1)S(1)}, bf16[4,64,128]{2,1,0:T(8,128)(2,1)S(1)}, u32[]{:S(2)}, u32[]{:S(2)}) %collective-permute-start.6) | collective-permute-done | bytes 65568 | tf_op jit(solution)/shard_map/ppermute | solution.py:401
  19.3 1.2 %collective-permute-start.9 = (bf16[4,64,128]{2,1,0:T(8,128)(2,1)S(1)}, bf16[4,64,128]{2,1,0:T(8,128)(2,1)S(1)}, u32[]{:S(2)}, u32[]{:S(2)}) collective-permute-start(bf16[4,64,128]{2,1,0:T(8,128)(2,1)S(1)} %collective-permute-done.6), channel_id=1, source_target_pairs={{0,2},{1,3},{2,0},{3,1},{4,6},{5,7},{6,4},{7,5},{8,10},{9,11},{10,... | collective-permute-start | bytes 196616 | tf_op jit(solution)/shard_map/ppermute | solution.py:392
  20.4 1.6 %collective-permute-start.8 = (bf16[4,64,128]{2,1,0:T(8,128)(2,1)S(1)}, bf16[4,64,128]{2,1,0:T(8,128)(2,1)S(1)}, u32[]{:S(2)}, u32[]{:S(2)}) collective-permute-start(bf16[4,64,128]{2,1,0:T(8,128)(2,1)S(1)} %collective-permute-done.6), channel_id=1, source_target_pairs={{0,3},{1,0},{2,1},{3,2},{4,7},{5,4},{6,5},{7,6},{8,11},{9,8},{10,9... | collective-permute-start | bytes 196616 | tf_op jit(solution)/shard_map/ppermute | solution.py:392
  22.0 3.0 %collective-permute-done.9 = bf16[4,64,128]{2,1,0:T(8,128)(2,1)S(1)} collective-permute-done((bf16[4,64,128]{2,1,0:T(8,128)(2,1)S(1)}, bf16[4,64,128]{2,1,0:T(8,128)(2,1)S(1)}, u32[]{:S(2)}, u32[]{:S(2)}) %collective-permute-start.9) | collective-permute-done | bytes 65568 | tf_op jit(solution)/shard_map/ppermute | solution.py:392
  25.0 0.8 %collective-permute-start.7 = (bf16[4,64,128]{2,1,0:T(8,128)(2,1)S(1)}, bf16[4,64,128]{2,1,0:T(8,128)(2,1)S(1)}, u32[]{:S(2)}, u32[]{:S(2)}) collective-permute-start(bf16[4,64,128]{2,1,0:T(8,128)(2,1)S(1)} %collective-permute-done.6), channel_id=1, source_target_pairs={{0,1},{1,2},{2,3},{3,0},{4,5},{5,6},{6,7},{7,4},{8,9},{9,10},{10,1... | collective-permute-start | bytes 196616 | tf_op jit(solution)/shard_map/ppermute | solution.py:392
  25.8 2.4 %slant_tables.1 = (bf16[32,128,256]{2,1,0:T(8,128)(2,1)S(1)}, bf16[2,4096,1024]{2,1,0:T(8,128)(2,1)S(1)}) custom-call(bf16[1,1,2,4096,1024]{4,3,2,1,0:T(8,128)(2,1)} %refs_6_.1), custom_call_target="tpu_custom_call" | custom-call | tf_op jit(solution)/shard_map/slant_tables/pallas_call | solution.py:104
  28.2 2.2 %held_more.1.refs_7_ = bf16[2,4096,1024]{2,1,0:T(8,128)(2,1)S(1)} custom-call(bf16[1,1,2,4096,1024]{4,3,2,1,0:T(8,128)(2,1)} %refs_6_.1, bf16[2,4096,1024]{2,1,0:T(8,128)(2,1)S(1)} %get-tuple-element.14.before_ref), custom_call_target="tpu_custom_call", output_to_operand_aliasing={{}: (1, {})} | custom-call | tf_op jit(solution)/shard_map/held_more/pallas_call | solution.py:139
  30.6 5.6 %partial_image.1 = (bf16[8,8,16,128]{3,2,1,0:T(8,128)(2,1)S(1)}, bf16[2,4096,1024]{2,1,0:T(8,128)(2,1)S(1)}) custom-call(bf16[4,520,128]{2,1,0:T(8,128)(2,1)S(1)} %pad_maximum_fusion.refs_0_, bf16[4,520,128]{2,1,0:T(8,128)(2,1)S(1)} %collective-permute-done.3.refs_1_, ...), custom_call_target="tpu_custom_call", output_to_operand_aliasing={{1}: (7, {})} | custom-call | tf_op jit(solution)/shard_map/partial_image/pallas_call | solution.py:275
  36.2 11.8 %all_to_all.5.parts_ref = bf16[8,8,16,128]{3,2,1,0:T(8,128)(2,1)S(1)} all-to-all(bf16[8,8,16,128]{3,2,1,0:T(8,128)(2,1)S(1)} %get-tuple-element.15), channel_id=1, replica_groups=mesh['line'=8,'tile'=16] {'line'}, dimensions={0} | all-to-all | bytes 524288 | tf_op jit(solution)/shard_map/all_to_all | solution.py:405
  48.0 2.6 %collective-permute-start.10 = (f32[2,16,128]{2,1,0:T(8,128)S(1)}, f32[2,16,128]{2,1,0:T(8,128)S(1)}, u32[]{:S(2)}, u32[]{:S(2)}) collective-permute-start(f32[2,16,128]{2,1,0:T(8,128)S(1)} %get-tuple-element.18), channel_id=1, source_target_pairs={{0,1},{1,0},{2,3},{3,2},{4,5},{5,4},{6,7},{7,6},{8,9},{9,8},{10,11... | collective-permute-start | bytes 49160 | tf_op jit(solution)/shard_map/ppermute | solution.py:408
  50.6 3.9 %collective-permute-start.11 = (f32[2,16,128]{2,1,0:T(8,128)S(1)}, f32[2,16,128]{2,1,0:T(8,128)S(1)}, u32[]{:S(2)}, u32[]{:S(2)}) collective-permute-start(f32[2,16,128]{2,1,0:T(8,128)S(1)} %get-tuple-element.20), channel_id=1, source_target_pairs={{1,2},{2,1},{3,4},{4,3},{5,6},{6,5},{7,8},{8,7},{9,10},{10,9},{11,... | collective-permute-start | bytes 49160 | tf_op jit(solution)/shard_map/ppermute | solution.py:409
  54.6 0.8 %inner_filtered.1 = (f32[8,16,128]{2,1,0:T(8,128)S(1)}, f32[32,128]{1,0:T(8,128)S(1)}) custom-call(f32[5,5]{1,0:T(8,128)S(1)} %copy-done, f32[8,16,128]{2,1,0:T(8,128)S(1)} %get-tuple-element.16.image_ref), custom_call_target="tpu_custom_call" | custom-call | tf_op jit(solution)/shard_map/inner_filtered/pallas_call | solution.py:367
  55.4 3.0 %collective-permute-done.11.second_ref = f32[2,16,128]{2,1,0:T(8,128)S(1)} collective-permute-done((f32[2,16,128]{2,1,0:T(8,128)S(1)}, f32[2,16,128]{2,1,0:T(8,128)S(1)}, u32[]{:S(2)}, u32[]{:S(2)}) %collective-permute-start.11) | collective-permute-done | bytes 16416 | tf_op jit(solution)/shard_map/ppermute | solution.py:409
  58.4 0.7 %outer_filtered.1 = f32[128,128]{1,0:T(8,128)} custom-call(f32[32,128]{1,0:T(8,128)S(1)} %get-tuple-element.17.taps_ref, f32[2,16,128]{2,1,0:T(8,128)S(1)} %collective-permute-done.10.first_ref, f32[8,16,128]{2,1,0:T(8,128)S(1)} %get-tuple-element.19.inner_ref, f32[2,16,128]{2,1,0:T(8,128)S(1)} %collective-permute-done.11.second_ref), custom_call_target="tpu_custom_call" | custom-call | tf_op jit(solution)/shard_map/outer_filtered/pallas_call | solution.py:379
  (13 shorter events, 0.8 us)
Async XLA Ops:
  0.9 6.9 %collective-permute-start.2 = (bf16[520,128]{1,0:T(8,128)(2,1)S(1)}, bf16[520,128]{1,0:T(8,128)(2,1)S(1)}, u32[]{:S(2)}, u32[]{:S(2)}) collective-permute-start(bf16[520,128]{1,0:T(8,128)(2,1)S(1)} %first_rows.1), channel_id=1, source_target_pairs={{0,2},{1,3},{2,0},{3,1},{4,6},{5,7},{6,4},{7,5},{8,10},{9,11},{10,... | collective-permute-start | bytes 399368 | tf_op jit(solution)/shard_map/ppermute | solution.py:392
  4.9 5.4 %collective-permute-start.1 = (bf16[520,128]{1,0:T(8,128)(2,1)S(1)}, bf16[520,128]{1,0:T(8,128)(2,1)S(1)}, u32[]{:S(2)}, u32[]{:S(2)}) collective-permute-start(bf16[520,128]{1,0:T(8,128)(2,1)S(1)} %first_rows.1), channel_id=1, source_target_pairs={{0,3},{1,0},{2,1},{3,2},{4,7},{5,4},{6,5},{7,6},{8,11},{9,8},{10,9... | collective-permute-start | bytes 399368 | tf_op jit(solution)/shard_map/ppermute | solution.py:392
  5.6 6.2 %collective-permute-start = (bf16[520,128]{1,0:T(8,128)(2,1)S(1)}, bf16[520,128]{1,0:T(8,128)(2,1)S(1)}, u32[]{:S(2)}, u32[]{:S(2)}) collective-permute-start(bf16[520,128]{1,0:T(8,128)(2,1)S(1)} %first_rows.1), channel_id=1, source_target_pairs={{0,1},{1,2},{2,3},{3,0},{4,5},{5,6},{6,7},{7,4},{8,9},{9,10},{10,1... | collective-permute-start | bytes 399368 | tf_op jit(solution)/shard_map/ppermute | solution.py:392
  11.9 18.7 %collective-permute-start.5 = (bf16[4,520,128]{2,1,0:T(8,128)(2,1)S(1)}, bf16[4,520,128]{2,1,0:T(8,128)(2,1)S(1)}, u32[]{:S(2)}, u32[]{:S(2)}) collective-permute-start(bf16[4,520,128]{2,1,0:T(8,128)(2,1)S(1)} %pad_maximum_fusion.refs_0_), channel_id=1, source_target_pairs={{0,8},{1,9},{2,10},{3,11},{4,12},{5,13},{6,14},{7,15},{8,0},{9,1},... | collective-permute-start | bytes 1597448 | tf_op jit(solution)/shard_map/ppermute | solution.py:392
  14.1 16.5 %collective-permute-start.4 = (bf16[4,520,128]{2,1,0:T(8,128)(2,1)S(1)}, bf16[4,520,128]{2,1,0:T(8,128)(2,1)S(1)}, u32[]{:S(2)}, u32[]{:S(2)}) collective-permute-start(bf16[4,520,128]{2,1,0:T(8,128)(2,1)S(1)} %pad_maximum_fusion.refs_0_), channel_id=1, source_target_pairs={{0,12},{1,13},{2,14},{3,15},{4,0},{5,1},{6,2},{7,3},{8,4},{9,5},{1... | collective-permute-start | bytes 1597448 | tf_op jit(solution)/shard_map/ppermute | solution.py:392
  15.5 15.0 %collective-permute-start.3 = (bf16[4,520,128]{2,1,0:T(8,128)(2,1)S(1)}, bf16[4,520,128]{2,1,0:T(8,128)(2,1)S(1)}, u32[]{:S(2)}, u32[]{:S(2)}) collective-permute-start(bf16[4,520,128]{2,1,0:T(8,128)(2,1)S(1)} %pad_maximum_fusion.refs_0_), channel_id=1, source_target_pairs={{0,4},{1,5},{2,6},{3,7},{4,8},{5,9},{6,10},{7,11},{8,12},{9,13},{1... | collective-permute-start | bytes 1597448 | tf_op jit(solution)/shard_map/ppermute | solution.py:392
  16.1 3.1 %collective-permute-start.6 = (bf16[4,64,128]{2,1,0:T(8,128)(2,1)S(1)}, bf16[4,64,128]{2,1,0:T(8,128)(2,1)S(1)}, u32[]{:S(2)}, u32[]{:S(2)}) collective-permute-start(bf16[4,64,128]{2,1,0:T(8,128)(2,1)S(1)} %slice.4), channel_id=1, source_target_pairs={{16,0},{32,16},{48,32},{64,48},{80,64},{96,80},{112,96},{17,1},{33... | collective-permute-start | bytes 196616 | tf_op jit(solution)/shard_map/ppermute | solution.py:401
  19.3 5.8 %collective-permute-start.9 = (bf16[4,64,128]{2,1,0:T(8,128)(2,1)S(1)}, bf16[4,64,128]{2,1,0:T(8,128)(2,1)S(1)}, u32[]{:S(2)}, u32[]{:S(2)}) collective-permute-start(bf16[4,64,128]{2,1,0:T(8,128)(2,1)S(1)} %collective-permute-done.6), channel_id=1, source_target_pairs={{0,2},{1,3},{2,0},{3,1},{4,6},{5,7},{6,4},{7,5},{8,10},{9,11},{10,... | collective-permute-start | bytes 196616 | tf_op jit(solution)/shard_map/ppermute | solution.py:392
  20.4 10.0 %collective-permute-start.8 = (bf16[4,64,128]{2,1,0:T(8,128)(2,1)S(1)}, bf16[4,64,128]{2,1,0:T(8,128)(2,1)S(1)}, u32[]{:S(2)}, u32[]{:S(2)}) collective-permute-start(bf16[4,64,128]{2,1,0:T(8,128)(2,1)S(1)} %collective-permute-done.6), channel_id=1, source_target_pairs={{0,3},{1,0},{2,1},{3,2},{4,7},{5,4},{6,5},{7,6},{8,11},{9,8},{10,9... | collective-permute-start | bytes 196616 | tf_op jit(solution)/shard_map/ppermute | solution.py:392
  25.0 5.5 %collective-permute-start.7 = (bf16[4,64,128]{2,1,0:T(8,128)(2,1)S(1)}, bf16[4,64,128]{2,1,0:T(8,128)(2,1)S(1)}, u32[]{:S(2)}, u32[]{:S(2)}) collective-permute-start(bf16[4,64,128]{2,1,0:T(8,128)(2,1)S(1)} %collective-permute-done.6), channel_id=1, source_target_pairs={{0,1},{1,2},{2,3},{3,0},{4,5},{5,6},{6,7},{7,4},{8,9},{9,10},{10,1... | collective-permute-start | bytes 196616 | tf_op jit(solution)/shard_map/ppermute | solution.py:392
  30.6 24.0 %copy-start = (f32[5,5]{1,0:T(8,128)S(1)}, f32[5,5]{1,0:T(8,128)}, u32[]{:S(2)}) copy-start(f32[5,5]{1,0:T(8,128)} %filter_ref.1) | copy-start | bytes 304
  48.0 7.4 %collective-permute-start.10 = (f32[2,16,128]{2,1,0:T(8,128)S(1)}, f32[2,16,128]{2,1,0:T(8,128)S(1)}, u32[]{:S(2)}, u32[]{:S(2)}) collective-permute-start(f32[2,16,128]{2,1,0:T(8,128)S(1)} %get-tuple-element.18), channel_id=1, source_target_pairs={{0,1},{1,0},{2,3},{3,2},{4,5},{5,4},{6,7},{7,6},{8,9},{9,8},{10,11... | collective-permute-start | bytes 49160 | tf_op jit(solution)/shard_map/ppermute | solution.py:408
  50.6 7.7 %collective-permute-start.11 = (f32[2,16,128]{2,1,0:T(8,128)S(1)}, f32[2,16,128]{2,1,0:T(8,128)S(1)}, u32[]{:S(2)}, u32[]{:S(2)}) collective-permute-start(f32[2,16,128]{2,1,0:T(8,128)S(1)} %get-tuple-element.20), channel_id=1, source_target_pairs={{1,2},{2,1},{3,4},{4,3},{5,6},{6,5},{7,8},{8,7},{9,10},{10,9},{11,... | collective-permute-start | bytes 49160 | tf_op jit(solution)/shard_map/ppermute | solution.py:409
